TPU v7x, 32 devices: a whole 2x2x4 slice. The times are simulated.
32 devices in a mesh: seq: 16 (over z, y, core), fsdp: 2 (over x).
Axes of the slice: x: 2, y: 2, z: 4, core: 2. Of those that a mesh axis runs over, the one named last changes fastest.
Arguments:
- inputs: bfloat16 [2, 2, 2048, 1536], P('fsdp', None, 'seq'), may hold values from -6 to 6
- lengths: int32 [2, 2, 4], P('fsdp'), may hold values from 1 to 1024, 2048 in all within a row
- attn_gain: bfloat16 [1536], P(('seq', 'fsdp')), may hold values from 0.25 to 1.75
- query_weight: bfloat16 [1536, 1536], P(('seq', 'fsdp')), may hold values from -0.3125 to 0.3125
- query_bias: bfloat16 [1536], P(('seq', 'fsdp')), may hold values from -3 to 3
- key_matrix: bfloat16 [1536, 256], P(('seq', 'fsdp')), may hold values from -0.15625 to 0.15625
- key_bias_vector: bfloat16 [256], P(('seq', 'fsdp')), may hold values from -3 to 3
- value_matrix: bfloat16 [1536, 256], P(('seq', 'fsdp')), may hold values from -0.15625 to 0.15625
- value_bias_vector: bfloat16 [256], P(('seq', 'fsdp')), may hold values from -3 to 3
- output_weight: bfloat16 [1536, 1536], P(('seq', 'fsdp')), may hold values from -0.625 to 0.625
- mlp_gain: bfloat16 [1536], P(('seq', 'fsdp')), may hold values from 0.25 to 1.75
- gate_weight: bfloat16 [1536, 8960], P(('seq', 'fsdp')), may hold values from -0.15625 to 0.15625
- up_weight: bfloat16 [1536, 8960], P(('seq', 'fsdp')), may hold values from -0.15625 to 0.15625
- down_weight: bfloat16 [8960, 1536], P(('seq', 'fsdp')), may hold values from -0.0625 to 0.0625
- cotangent: bfloat16 [2, 2, 2048, 1536], P('fsdp', None, 'seq'), may hold values from -6 to 6
Outputs:
- outputs: bfloat16 [2, 2, 2048, 1536], P('fsdp', None, 'seq')
- input_grad: float32 [2, 2, 2048, 1536], P('fsdp', None, 'seq')
- attn_gain_grad: float32 [1536], P(('seq', 'fsdp'))
- query_weight_grad: float32 [1536, 1536], P(('seq', 'fsdp'))
- query_bias_grad: float32 [1536], P(('seq', 'fsdp'))
- key_weight_grad: float32 [1536, 256], P(('seq', 'fsdp'))
- key_bias_grad: float32 [256], P(('seq', 'fsdp'))
- value_weight_grad: float32 [1536, 256], P(('seq', 'fsdp'))
- value_bias_grad: float32 [256], P(('seq', 'fsdp'))
- output_weight_grad: float32 [1536, 1536], P(('seq', 'fsdp'))
- mlp_gain_grad: float32 [1536], P(('seq', 'fsdp'))
- gate_weight_grad: float32 [1536, 8960], P(('seq', 'fsdp'))
- up_weight_grad: float32 [1536, 8960], P(('seq', 'fsdp'))
- down_weight_grad: float32 [8960, 1536], P(('seq', 'fsdp'))
Inputs may be any that keep to these rules, and one draw needn't show every extreme that they name: Each stream's 4 item lengths sum to 2048, and the longest is exactly half of 2048.
All inputs are finite; a program needn't handle non-finite values.
Results may differ from a plain program's by a relative error of at most 0.018.
Values may be sent and summed in bfloat16 or wider, within the bound.
A program may use at most 448 MiB of HBM per device.

v0:
```python
import jax
import jax.numpy as jnp
from jax import lax
from jax.sharding import PartitionSpec as P

QUERY_HEADS = 12
KEY_VALUE_HEADS = 2
HEAD_WIDTH = 128


EPSILON = 1e-06
THETA = 10000.0


def locate(item_lengths, positions_at):
    ends = jnp.cumsum(item_lengths)
    starts = ends - item_lengths
    segment_ids = jnp.sum((ends[None, :] <= positions_at[:, None]).astype(jnp.int32), axis=1)
    onehot = segment_ids[:, None] == jnp.arange(item_lengths.shape[0], dtype=jnp.int32)[None, :]
    first = jnp.sum(jnp.where(onehot, starts[None, :], 0), axis=1)
    return (segment_ids, positions_at - first, first)


def rotary_tables(offsets, head_size):
    freqs = 1.0 / THETA ** (jnp.arange(0, head_size, 2, dtype=jnp.float32) / head_size)
    angles = offsets.astype(jnp.float32)[:, None] * freqs[None, :]
    cosine_table = jnp.concatenate([jnp.cos(angles), jnp.cos(angles)], axis=1)
    sine_table = jnp.concatenate([jnp.sin(angles), jnp.sin(angles)], axis=1)
    return (cosine_table, sine_table)


def apply_rotary(values, cosine_table, sine_table):
    half = values.shape[-1] // 2
    turned = jnp.concatenate([-values[..., half:], values[..., :half]], axis=-1)
    return values * cosine_table[:, None, :] + turned * sine_table[:, None, :]


def inverse_rotary(grads, cosine_table, sine_table):
    half = grads.shape[-1] // 2
    scaled = grads * sine_table[:, None, :]
    turned = jnp.concatenate([scaled[..., half:], -scaled[..., :half]], axis=-1)
    return grads * cosine_table[:, None, :] + turned


def rms_forward(rows, gain):
    recip = lax.rsqrt(jnp.mean(rows * rows, axis=-1, keepdims=True) + EPSILON)
    return (rows * recip * gain, recip)


def rms_backward(rows, recip, gain, upstream):
    weighted = upstream * gain
    grad_rows = recip * weighted - rows * (recip * recip * recip) * jnp.mean(
        rows * weighted, axis=-1, keepdims=True
    )
    gain_grad = jnp.sum(upstream * rows * recip, axis=0)
    return (grad_rows, gain_grad)


def contract_rows(left, right):
    return lax.dot_general(
        left, right, (((0,), (0,)), ((), ())), preferred_element_type=jnp.float32
    )


def contract_cols(left, right):
    return lax.dot_general(
        left, right, (((1,), (1,)), ((), ())), preferred_element_type=jnp.float32
    )


def flatten_lanes(matrix):
    return matrix.reshape(-1, 128)


def block_scores(queries, keys, values, key_seg, query_seg, query_index, start, block_slice):
    key_block = lax.dynamic_slice_in_dim(keys, start, block_slice, 0)
    value_block = lax.dynamic_slice_in_dim(values, start, block_slice, 0)
    seg_block = lax.dynamic_slice_in_dim(key_seg, start, block_slice, 0)
    key_index = start + jnp.arange(block_slice, dtype=jnp.int32)
    allowed = (seg_block[None, :] == query_seg[:, None]) & (
        key_index[None, :] <= query_index[:, None]
    )
    scores = jnp.einsum(
        "tghd,kgd->ghtk", queries, key_block, preferred_element_type=jnp.float32
    ) * queries.shape[-1] ** (-0.5)
    return (scores, allowed[None, None], key_block, value_block)


def attend_forward(queries, keys, values, key_seg, query_seg, query_index, earliest):
    residual_stream = keys.shape[0]
    block_slice = min(512, residual_stream)
    item_count = residual_stream // block_slice
    latest = query_index[-1]
    row_shape = (queries.shape[1], queries.shape[2], queries.shape[0])

    def needed(start):
        return (start <= latest) & (start + block_slice > earliest)

    def first_pass(number, carry):
        start = (number * block_slice).astype(jnp.int32)

        def work(state):
            scores, allowed, key_block, value_block = block_scores(
                queries, keys, values, key_seg, query_seg, query_index, start, block_slice
            )
            masked = jnp.where(allowed, scores, -1e30)
            new_max = jnp.maximum(state[0], jnp.max(masked, axis=-1))
            total = state[1] * jnp.exp(state[0] - new_max) + jnp.sum(
                jnp.where(allowed, jnp.exp(masked - new_max[..., None]), 0.0), axis=-1
            )
            return (new_max, total)

        return lax.cond(needed(start), work, lambda state: state, carry)

    run_max, run_sum = lax.fori_loop(
        0,
        item_count,
        first_pass,
        (jnp.full(row_shape, -1e30, jnp.float32), jnp.zeros(row_shape, jnp.float32)),
    )
    log_total = run_max + jnp.log(run_sum)

    def second_pass(number, accum):
        start = (number * block_slice).astype(jnp.int32)

        def work(state):
            scores, allowed, key_block, value_block = block_scores(
                queries, keys, values, key_seg, query_seg, query_index, start, block_slice
            )
            probs = jnp.where(allowed, jnp.exp(scores - log_total[..., None]), 0.0).astype(
                jnp.bfloat16
            )
            return state + jnp.einsum(
                "ghtk,kgd->tghd", probs, value_block, preferred_element_type=jnp.float32
            )

        return lax.cond(needed(start), work, lambda state: state, accum)

    accum = lax.fori_loop(0, item_count, second_pass, jnp.zeros(queries.shape, jnp.float32))
    return (accum, log_total)


def attend_backward(
    queries, keys, values, key_seg, query_seg, query_index, earliest, log_total, grad_out
):
    residual_stream = keys.shape[0]
    block_slice = min(512, residual_stream)
    item_count = residual_stream // block_slice
    latest = query_index[-1]
    inv_root = queries.shape[-1] ** (-0.5)

    def needed(start):
        return (start <= latest) & (start + block_slice > earliest)

    def probs_and_grads(start):
        scores, allowed, key_block, value_block = block_scores(
            queries, keys, values, key_seg, query_seg, query_index, start, block_slice
        )
        probs = jnp.where(allowed, jnp.exp(scores - log_total[..., None]), 0.0)
        grad_probs = jnp.einsum(
            "tghd,kgd->ghtk", grad_out, value_block, preferred_element_type=jnp.float32
        )
        return (probs, grad_probs, key_block)

    def first_pass(number, delta):
        start = (number * block_slice).astype(jnp.int32)

        def work(state):
            probs, grad_probs, key_block = probs_and_grads(start)
            return state + jnp.sum(probs * grad_probs, axis=-1)

        return lax.cond(needed(start), work, lambda state: state, delta)

    delta = lax.fori_loop(0, item_count, first_pass, jnp.zeros(log_total.shape, jnp.float32))

    def second_pass(number, carry):
        start = (number * block_slice).astype(jnp.int32)

        def work(state):
            grad_query, grad_keys, grad_values = state
            probs, grad_probs, key_block = probs_and_grads(start)
            grad_scores = (probs * (grad_probs - delta[..., None])).astype(jnp.bfloat16)
            grad_query = grad_query + jnp.einsum(
                "ghtk,kgd->tghd", grad_scores, key_block, preferred_element_type=jnp.float32
            )
            key_part = jnp.einsum(
                "ghtk,tghd->kgd", grad_scores, queries, preferred_element_type=jnp.float32
            )
            value_part = jnp.einsum(
                "ghtk,tghd->kgd",
                probs.astype(jnp.bfloat16),
                grad_out,
                preferred_element_type=jnp.float32,
            )
            grad_keys = lax.dynamic_update_slice_in_dim(
                grad_keys,
                lax.dynamic_slice_in_dim(grad_keys, start, block_slice, 0) + key_part,
                start,
                0,
            )
            grad_values = lax.dynamic_update_slice_in_dim(
                grad_values,
                lax.dynamic_slice_in_dim(grad_values, start, block_slice, 0) + value_part,
                start,
                0,
            )
            return (grad_query, grad_keys, grad_values)

        return lax.cond(needed(start), work, lambda state: state, carry)

    start_state = (
        jnp.zeros(queries.shape, jnp.float32),
        jnp.zeros(keys.shape, jnp.float32),
        jnp.zeros(values.shape, jnp.float32),
    )
    grad_query, grad_keys, grad_values = lax.fori_loop(0, item_count, second_pass, start_state)
    return (grad_query * inv_root, grad_keys * inv_root, grad_values)


def body(
    inputs,
    lengths,
    attn_gain,
    query_weight,
    query_bias,
    key_matrix,
    key_bias_vector,
    value_matrix,
    value_bias_vector,
    output_weight,
    mlp_gain,
    gate_weight,
    up_weight,
    down_weight,
    cotangent,
):
    micro = inputs.shape[1]
    token_rows = inputs.shape[2]
    width = inputs.shape[3]
    kv_width = key_matrix.shape[1]
    hidden_width = gate_weight.shape[1]
    query_groups = QUERY_HEADS // KEY_VALUE_HEADS
    gain_attn_sum = jnp.zeros((width,), jnp.float32)
    gain_mlp_sum = jnp.zeros((width,), jnp.float32)
    bias_query_sum = jnp.zeros((width,), jnp.float32)
    bias_key_sum = jnp.zeros((kv_width,), jnp.float32)
    bias_value_sum = jnp.zeros((kv_width,), jnp.float32)
    kept_normed = []
    kept_query = []
    kept_key = []
    kept_value = []
    kept_attended = []
    kept_branch = []
    kept_normed_two = []
    kept_gate = []
    kept_up = []
    kept_hidden = []
    kept_upstream = []
    results = []
    input_grads = []
    for number in range(micro):
        attn_full = (
            lax.all_gather(attn_gain, ("seq", "fsdp"), axis=0, tiled=True),
            lax.all_gather(query_weight, ("seq", "fsdp"), axis=0, tiled=True),
            lax.all_gather(query_bias, ("seq", "fsdp"), axis=0, tiled=True),
            lax.all_gather(key_matrix, ("seq", "fsdp"), axis=0, tiled=True),
            lax.all_gather(key_bias_vector, ("seq", "fsdp"), axis=0, tiled=True),
            lax.all_gather(value_matrix, ("seq", "fsdp"), axis=0, tiled=True),
            lax.all_gather(value_bias_vector, ("seq", "fsdp"), axis=0, tiled=True),
            lax.all_gather(output_weight, ("seq", "fsdp"), axis=0, tiled=True),
        )
        mlp_full = (
            lax.all_gather(mlp_gain, ("seq", "fsdp"), axis=0, tiled=True),
            lax.all_gather(gate_weight, ("seq", "fsdp"), axis=0, tiled=True),
            lax.all_gather(up_weight, ("seq", "fsdp"), axis=0, tiled=True),
            lax.all_gather(down_weight, ("seq", "fsdp"), axis=0, tiled=True),
        )
        gain_attn, w_query, b_query, w_key, b_key, w_value, b_value, w_output = attn_full
        gain_mlp, w_gate, w_up, w_down = mlp_full
        gain_attn = gain_attn.astype(jnp.float32)
        gain_mlp = gain_mlp.astype(jnp.float32)
        rows = inputs[0, number].astype(jnp.float32)
        item_lengths = lengths[0, number]
        positions_at = lax.axis_index("seq") * token_rows + jnp.arange(token_rows, dtype=jnp.int32)
        segment_ids, offsets, first = locate(item_lengths, positions_at)
        cosine_table, sine_table = rotary_tables(offsets, HEAD_WIDTH)
        normed, recip_one = rms_forward(rows, gain_attn)
        normed_low = normed.astype(jnp.bfloat16)
        query_unrotated = jnp.dot(
            normed_low, w_query, preferred_element_type=jnp.float32
        ) + b_query.astype(jnp.float32)
        key_unrotated = jnp.dot(
            normed_low, w_key, preferred_element_type=jnp.float32
        ) + b_key.astype(jnp.float32)
        value_reduced = (
            jnp.dot(normed_low, w_value, preferred_element_type=jnp.float32)
            + b_value.astype(jnp.float32)
        ).astype(jnp.bfloat16)
        query_rotated = (
            apply_rotary(
                query_unrotated.reshape(token_rows, QUERY_HEADS, HEAD_WIDTH),
                cosine_table,
                sine_table,
            )
            .astype(jnp.bfloat16)
            .reshape(token_rows, KEY_VALUE_HEADS, query_groups, HEAD_WIDTH)
        )
        key_rotated = (
            apply_rotary(
                key_unrotated.reshape(token_rows, KEY_VALUE_HEADS, HEAD_WIDTH),
                cosine_table,
                sine_table,
            )
            .astype(jnp.bfloat16)
            .reshape(token_rows, kv_width)
        )
        gathered_keys, gathered_values = (
            lax.all_gather(key_rotated, "seq", axis=0, tiled=True),
            lax.all_gather(value_reduced, "seq", axis=0, tiled=True),
        )
        residual_stream = gathered_keys.shape[0]
        gathered_keys = gathered_keys.reshape(residual_stream, KEY_VALUE_HEADS, HEAD_WIDTH)
        gathered_values = gathered_values.reshape(residual_stream, KEY_VALUE_HEADS, HEAD_WIDTH)
        key_segment = locate(item_lengths, jnp.arange(residual_stream, dtype=jnp.int32))[0]
        earliest = first[0]
        attended_rows, log_total = attend_forward(
            query_rotated,
            gathered_keys,
            gathered_values,
            key_segment,
            segment_ids,
            positions_at,
            earliest,
        )
        attended_low = attended_rows.reshape(token_rows, width).astype(jnp.bfloat16)
        middle = rows + jnp.dot(attended_low, w_output, preferred_element_type=jnp.float32)
        normed_two, recip_two = rms_forward(middle, gain_mlp)
        normed_two_low = normed_two.astype(jnp.bfloat16)
        gate_pre = jnp.dot(normed_two_low, w_gate, preferred_element_type=jnp.float32)
        up_pre = jnp.dot(normed_two_low, w_up, preferred_element_type=jnp.float32)
        sigma = jax.nn.sigmoid(gate_pre)
        activated = gate_pre * sigma
        hidden_low = (activated * up_pre).astype(jnp.bfloat16)
        final_rows = middle + jnp.dot(hidden_low, w_down, preferred_element_type=jnp.float32)
        results.append(final_rows.astype(jnp.bfloat16))
        upstream = cotangent[0, number].astype(jnp.float32)
        upstream_low = cotangent[0, number]
        grad_hidden = contract_cols(upstream_low, w_down)
        grad_gate = (grad_hidden * up_pre * sigma * (1.0 + gate_pre * (1.0 - sigma))).astype(
            jnp.bfloat16
        )
        grad_up = (grad_hidden * activated).astype(jnp.bfloat16)
        grad_normed_two = contract_cols(grad_gate, w_gate) + contract_cols(grad_up, w_up)
        grad_middle_norm, grad_gain_mlp = rms_backward(middle, recip_two, gain_mlp, grad_normed_two)
        grad_middle = upstream + grad_middle_norm
        gain_mlp_sum = gain_mlp_sum + grad_gain_mlp
        grad_branch_low = grad_middle.astype(jnp.bfloat16)
        grad_attended = (
            contract_cols(grad_branch_low, w_output)
            .astype(jnp.bfloat16)
            .reshape(token_rows, KEY_VALUE_HEADS, query_groups, HEAD_WIDTH)
        )
        grad_qrot, grad_keys, grad_values = attend_backward(
            query_rotated,
            gathered_keys,
            gathered_values,
            key_segment,
            segment_ids,
            positions_at,
            earliest,
            log_total,
            grad_attended,
        )
        local_keys, own_values = (
            lax.psum_scatter(
                grad_keys.reshape(residual_stream, kv_width), "seq", scatter_dimension=0, tiled=True
            ),
            lax.psum_scatter(
                grad_values.reshape(residual_stream, kv_width),
                "seq",
                scatter_dimension=0,
                tiled=True,
            ),
        )
        grad_query = (
            inverse_rotary(
                grad_qrot.reshape(token_rows, QUERY_HEADS, HEAD_WIDTH), cosine_table, sine_table
            )
            .reshape(token_rows, width)
            .astype(jnp.bfloat16)
        )
        grad_key = (
            inverse_rotary(
                local_keys.reshape(token_rows, KEY_VALUE_HEADS, HEAD_WIDTH),
                cosine_table,
                sine_table,
            )
            .reshape(token_rows, kv_width)
            .astype(jnp.bfloat16)
        )
        grad_value = own_values.astype(jnp.bfloat16)
        bias_query_sum = bias_query_sum + jnp.sum(grad_query.astype(jnp.float32), axis=0)
        bias_key_sum = bias_key_sum + jnp.sum(grad_key.astype(jnp.float32), axis=0)
        bias_value_sum = bias_value_sum + jnp.sum(grad_value.astype(jnp.float32), axis=0)
        grad_normed = (
            contract_cols(grad_query, w_query)
            + contract_cols(grad_key, w_key)
            + contract_cols(grad_value, w_value)
        )
        grad_rows_norm, grad_gain_attn = rms_backward(rows, recip_one, gain_attn, grad_normed)
        gain_attn_sum = gain_attn_sum + grad_gain_attn
        input_grads.append(grad_middle + grad_rows_norm)
        kept_normed.append(normed_low)
        kept_query.append(grad_query)
        kept_key.append(grad_key)
        kept_value.append(grad_value)
        kept_attended.append(attended_low)
        kept_branch.append(grad_branch_low)
        kept_normed_two.append(normed_two_low)
        kept_gate.append(grad_gate)
        kept_up.append(grad_up)
        kept_hidden.append(hidden_low)
        kept_upstream.append(upstream_low)
    all_normed = jnp.concatenate(kept_normed, axis=0)
    all_normed_two = jnp.concatenate(kept_normed_two, axis=0)
    grad_down = contract_rows(
        jnp.concatenate(kept_hidden, axis=0), jnp.concatenate(kept_upstream, axis=0)
    )
    down_part = lax.psum_scatter(
        flatten_lanes(grad_down), ("seq", "fsdp"), scatter_dimension=0, tiled=True
    )
    grad_wgate = contract_rows(all_normed_two, jnp.concatenate(kept_gate, axis=0))
    grad_wup = contract_rows(all_normed_two, jnp.concatenate(kept_up, axis=0))
    mlp_parts = (
        lax.psum_scatter(gain_mlp_sum, ("seq", "fsdp"), scatter_dimension=0, tiled=True),
        lax.psum_scatter(
            flatten_lanes(grad_wgate), ("seq", "fsdp"), scatter_dimension=0, tiled=True
        ),
        lax.psum_scatter(flatten_lanes(grad_wup), ("seq", "fsdp"), scatter_dimension=0, tiled=True),
    )
    grad_wquery = contract_rows(all_normed, jnp.concatenate(kept_query, axis=0))
    grad_wkey = contract_rows(all_normed, jnp.concatenate(kept_key, axis=0))
    grad_wvalue = contract_rows(all_normed, jnp.concatenate(kept_value, axis=0))
    grad_woutput = contract_rows(
        jnp.concatenate(kept_attended, axis=0), jnp.concatenate(kept_branch, axis=0)
    )
    attn_parts = (
        lax.psum_scatter(gain_attn_sum, ("seq", "fsdp"), scatter_dimension=0, tiled=True),
        lax.psum_scatter(
            flatten_lanes(grad_wquery), ("seq", "fsdp"), scatter_dimension=0, tiled=True
        ),
        lax.psum_scatter(bias_query_sum, ("seq", "fsdp"), scatter_dimension=0, tiled=True),
        lax.psum_scatter(
            flatten_lanes(grad_wkey), ("seq", "fsdp"), scatter_dimension=0, tiled=True
        ),
        lax.psum_scatter(bias_key_sum, ("seq", "fsdp"), scatter_dimension=0, tiled=True),
        lax.psum_scatter(
            flatten_lanes(grad_wvalue), ("seq", "fsdp"), scatter_dimension=0, tiled=True
        ),
        lax.psum_scatter(bias_value_sum, ("seq", "fsdp"), scatter_dimension=0, tiled=True),
        lax.psum_scatter(
            flatten_lanes(grad_woutput), ("seq", "fsdp"), scatter_dimension=0, tiled=True
        ),
    )
    outputs = jnp.stack(results)[None]
    input_grad = jnp.stack(input_grads)[None]
    return (
        outputs,
        input_grad,
        attn_parts[0],
        attn_parts[1].reshape(-1, width),
        attn_parts[2],
        attn_parts[3].reshape(-1, kv_width),
        attn_parts[4],
        attn_parts[5].reshape(-1, kv_width),
        attn_parts[6],
        attn_parts[7].reshape(-1, width),
        mlp_parts[0],
        mlp_parts[1].reshape(-1, hidden_width),
        mlp_parts[2].reshape(-1, hidden_width),
        down_part.reshape(-1, width),
    )


def solution(mesh):
    in_specs = (
        P("fsdp", None, "seq", None),
        P("fsdp", None, None),
        P(("seq", "fsdp")),
        P(("seq", "fsdp"), None),
        P(("seq", "fsdp")),
        P(("seq", "fsdp"), None),
        P(("seq", "fsdp")),
        P(("seq", "fsdp"), None),
        P(("seq", "fsdp")),
        P(("seq", "fsdp"), None),
        P(("seq", "fsdp")),
        P(("seq", "fsdp"), None),
        P(("seq", "fsdp"), None),
        P(("seq", "fsdp"), None),
        P("fsdp", None, "seq", None),
    )
    out_specs = (
        P("fsdp", None, "seq", None),
        P("fsdp", None, "seq", None),
        P(("seq", "fsdp")),
        P(("seq", "fsdp"), None),
        P(("seq", "fsdp")),
        P(("seq", "fsdp"), None),
        P(("seq", "fsdp")),
        P(("seq", "fsdp"), None),
        P(("seq", "fsdp")),
        P(("seq", "fsdp"), None),
        P(("seq", "fsdp")),
        P(("seq", "fsdp"), None),
        P(("seq", "fsdp"), None),
        P(("seq", "fsdp"), None),
    )
    return jax.shard_map(body, mesh=mesh, in_specs=in_specs, out_specs=out_specs, check_vma=False)
```

profile of v0, /device:TPU:0, one launch (start us, length us, event | category | flops | bytes accessed | tf_op | source)
XLA Modules:
  0.0 3231.3 jit_solution(10275223559282558791)
XLA Ops:
  11.5 42.2 %all-reduce.11 = (bf16[1536]{0:T(1024)(128)(2,1)S(1)}, bf16[256]{0:T(256)(128)(2,1)S(1)}, bf16[256]{0:T(256)(128)(2,1)S(1)}, bf16[1536]{0:T(1024)(128)(2,1)S(1)}, bf16[1536]{0:T(1024)(128)(2,1)S(1)}) all-reduce(bf16[1536]{0:T(1024)(128)(2,1)S(1)} %dynamic-update-slice, ...), channel_id=1, replica_groups=mesh['seq'=16,'fsdp'=2] {'seq','fsdp'}, use_global_device_ids=true, to_apply=%add | all-reduce | flops 5120 | bytes 20480
  55.1 71.0 %all_gather.61 = bf16[1536,256]{1,0:T(8,128)(2,1)S(1)} all-gather(bf16[48,256]{1,0:T(8,128)(2,1)} %param.54), channel_id=1, replica_groups=mesh['seq'=16,'fsdp'=2] {'seq','fsdp'}, dimensions={0}, use_global_device_ids=true | all-gather | bytes 811008 | tf_op jit(solution)/shard_map/all_gather | solution.py:268
  130.2 69.0 %all_gather.64 = bf16[1536,256]{1,0:T(8,128)(2,1)S(1)} all-gather(bf16[48,256]{1,0:T(8,128)(2,1)S(1)} %copy-done.102), channel_id=1, replica_groups=mesh['seq'=16,'fsdp'=2] {'seq','fsdp'}, dimensions={0}, use_global_device_ids=true | all-gather | bytes 811008 | tf_op jit(solution)/shard_map/all_gather | solution.py:266
  217.3 26.1 all-gather.26.cloned.1.call-done
  244.8 38.1 %all-gather.12.cloned.1.call-done = bf16[2048,256]{1,0:T(8,128)(2,1)} async-done(((bf16[128,256]{1,0:T(8,128)(2,1)}), bf16[2048,256]{1,0:T(8,128)(2,1)}) %all-gather.12.cloned.1.call-update) | async-done | bytes 1048592 | tf_op jit(solution)/shard_map/all_gather | solution.py:318
  284.3 63.9 %all-gather.14.cloned.1.call-done = bf16[1536,1536]{1,0:T(8,128)(2,1)} async-done(((bf16[48,1536]{1,0:T(8,128)(2,1)}), bf16[1536,1536]{1,0:T(8,128)(2,1)}) %all-gather.14.cloned.1.call-update) | async-done | bytes 4718608 | tf_op jit(solution)/shard_map/all_gather | solution.py:264
  417.7 161.8 %all-gather.18.cloned.1.call-done = bf16[1536,8960]{1,0:T(8,128)(2,1)} async-done(((bf16[48,8960]{1,0:T(8,128)(2,1)}), bf16[1536,8960]{1,0:T(8,128)(2,1)}) %all-gather.18.cloned.1.call-update) | async-done | bytes 27525136 | tf_op jit(solution)/shard_map/all_gather | solution.py:274
  594.2 151.8 %all-gather.20.cloned.1.call-done = bf16[1536,8960]{1,0:T(8,128)(2,1)} async-done(((bf16[48,8960]{1,0:T(8,128)(2,1)}), bf16[1536,8960]{1,0:T(8,128)(2,1)}) %all-gather.20.cloned.1.call-update) | async-done | bytes 27525136 | tf_op jit(solution)/shard_map/all_gather | solution.py:275
  760.6 151.8 %all-gather.22.cloned.1.call-done = bf16[8960,1536]{1,0:T(8,128)(2,1)} async-done(((bf16[280,1536]{1,0:T(8,128)(2,1)}), bf16[8960,1536]{1,0:T(8,128)(2,1)}) %all-gather.22.cloned.1.call-update) | async-done | bytes 27525136 | tf_op jit(solution)/shard_map/all_gather | solution.py:276
  1110.2 34.8 %reduce-scatter.16.cloned.1.call-done = f32[128,256]{1,0:T(8,128)} async-done(((f32[2048,256]{1,0:T(8,128)}), f32[128,256]{1,0:T(8,128)}) %reduce-scatter.16.cloned.1.call-update) | async-done | bytes 131088 | tf_op jit(solution)/shard_map/reduce_scatter | solution.py:375
  1146.0 63.5 %reduce-scatter.12.cloned.1.call-done = f32[128,256]{1,0:T(8,128)} async-done(((f32[2048,256]{1,0:T(8,128)}), f32[128,256]{1,0:T(8,128)}) %reduce-scatter.12.cloned.1.call-update) | async-done | bytes 131088 | tf_op jit(solution)/shard_map/reduce_scatter | solution.py:375
  1219.4 54.5 %reduce-scatter.18.cloned.1.call-done = f32[128,256]{0,1:T(8,128)} async-done(((f32[2048,256]{0,1:T(8,128)}), f32[128,256]{0,1:T(8,128)}) %reduce-scatter.18.cloned.1.call-update) | async-done | bytes 131088 | tf_op jit(solution)/shard_map/reduce_scatter | solution.py:378
  1275.4 62.9 %reduce-scatter.14.cloned.1.call-done = f32[128,256]{0,1:T(8,128)} async-done(((f32[2048,256]{0,1:T(8,128)}), f32[128,256]{0,1:T(8,128)}) %reduce-scatter.14.cloned.1.call-update) | async-done | bytes 131088 | tf_op jit(solution)/shard_map/reduce_scatter | solution.py:378
  1380.8 21.8 fusion.142
  1402.6 54.0 %reshape.854 = f32[107520,128]{1,0:T(8,128)} reshape(f32[1536,8960]{1,0:T(8,128)} %fusion.142) | data formatting | bytes 110100480 | tf_op jit(solution)/shard_map/reshape | solution.py:72
  1458.3 22.0 fusion.146
  1480.3 54.1 %reshape.856 = f32[107520,128]{1,0:T(8,128)} reshape(f32[1536,8960]{1,0:T(8,128)} %fusion.146) | data formatting | bytes 110100480 | tf_op jit(solution)/shard_map/reshape | solution.py:72
  1536.2 22.3 fusion.150
  1558.6 57.2 %reshape.858 = f32[107520,128]{1,0:T(8,128)} reshape(f32[8960,1536]{1,0:T(8,128)} %fusion.150) | data formatting | bytes 110100480 | tf_op jit(solution)/shard_map/reshape | solution.py:72
  1652.4 40.5 %all-reduce.10 = (f32[1536]{0:T(1024)S(1)}, f32[1536]{0:T(1024)S(1)}, f32[256]{0:T(256)S(1)}, f32[256]{0:T(256)S(1)}, f32[1536]{0:T(1024)S(1)}) all-reduce(f32[1536]{0:T(1024)S(1)} %add.643, f32[1536]{0:T(1024)S(1)} %add.647, f32[256]{0:T(256)S(1)} %add.648, ...), channel_id=6, replica_groups=mesh['seq'=16,'fsdp'=2] {'seq','fsdp'}, use_global_device_ids=true, to_apply=%region_60.61.clone | all-reduce | flops 5120 | bytes 40960
  1703.2 122.4 %reduce-scatter.26.cloned.1.call-done = f32[576,128]{1,0:T(8,128)} async-done(((f32[18432,128]{1,0:T(8,128)}), f32[576,128]{1,0:T(8,128)}) %reduce-scatter.26.cloned.1.call-update) | async-done | bytes 294928 | tf_op jit(solution)/shard_map/reduce_scatter | solution.py:461
  1827.4 463.4 %reduce-scatter.28.cloned.1.call-done = f32[3360,128]{1,0:T(8,128)} async-done(((f32[107520,128]{1,0:T(8,128)}), f32[3360,128]{1,0:T(8,128)}) %reduce-scatter.28.cloned.1.call-update) | async-done | bytes 1720336 | tf_op jit(solution)/shard_map/reduce_scatter | solution.py:436
  2293.5 462.8 %reduce-scatter.30.cloned.1.call-done = f32[3360,128]{1,0:T(8,128)} async-done(((f32[107520,128]{1,0:T(8,128)}), f32[3360,128]{1,0:T(8,128)}) %reduce-scatter.30.cloned.1.call-update) | async-done | bytes 1720336 | tf_op jit(solution)/shard_map/reduce_scatter | solution.py:439
  2759.0 462.7 %reduce-scatter.32.cloned.1.call-done = f32[3360,128]{1,0:T(8,128)} async-done(((f32[107520,128]{1,0:T(8,128)}), f32[3360,128]{1,0:T(8,128)}) %reduce-scatter.32.cloned.1.call-update) | async-done | bytes 1720336 | tf_op jit(solution)/shard_map/reduce_scatter | solution.py:429
  (611 shorter events, 506.4 us)
Async XLA Ops:
  7.2 204.4 %all-gather.24.cloned.1.call-start = ((), (), s32[]{:S(2)}) async-start(), calls=%async_computation.18 | async-start | bytes 1114112 | tf_op jit(solution)/shard_map/all_gather | solution.py:319
  129.1 84.9 %all-gather.10.cloned.1.call-start = ((), (), s32[]{:S(2)}) async-start(), calls=%async_computation.11 | async-start | bytes 1114112 | tf_op jit(solution)/shard_map/all_gather | solution.py:319
  130.1 113.3 %all-gather.26.cloned.1.call-start = ((), (), s32[]{:S(2)}) async-start(), calls=%async_computation.19 | async-start | bytes 1114112 | tf_op jit(solution)/shard_map/all_gather | solution.py:318
  203.2 79.7 %all-gather.12.cloned.1.call-start = ((), (), s32[]{:S(2)}) async-start(), calls=%async_computation.12 | async-start | bytes 1114112 | tf_op jit(solution)/shard_map/all_gather | solution.py:318
  205.6 142.5 %all-gather.14.cloned.1.call-start = ((), (), s32[]{:S(2)}) async-start(), calls=%async_computation.13 | async-start | bytes 4866048 | tf_op jit(solution)/shard_map/all_gather | solution.py:264
  206.2 206.6 %all-gather.16.cloned.1.call-start = ((), (), s32[]{:S(2)}) async-start(), calls=%async_computation.14 | async-start | bytes 4866048 | tf_op jit(solution)/shard_map/all_gather | solution.py:270
  206.8 372.7 %all-gather.18.cloned.1.call-start = ((), (), s32[]{:S(2)}) async-start(), calls=%async_computation.15 | async-start | bytes 28385280 | tf_op jit(solution)/shard_map/all_gather | solution.py:274
  207.5 538.4 %all-gather.20.cloned.1.call-start = ((), (), s32[]{:S(2)}) async-start(), calls=%async_computation.16 | async-start | bytes 28385280 | tf_op jit(solution)/shard_map/all_gather | solution.py:275
  208.3 704.1 %all-gather.22.cloned.1.call-start = ((), (), s32[]{:S(2)}) async-start(), calls=%async_computation.17 | async-start | bytes 28385280 | tf_op jit(solution)/shard_map/all_gather | solution.py:276
  209.0 936.0 %reduce-scatter.16.cloned.1.call-start = ((), (), s32[]{:S(2)}) async-start(), calls=%async_computation.22 | async-start | bytes 2228224 | tf_op jit(solution)/shard_map/reduce_scatter | solution.py:375
  416.2 626.1 %copy-start.17 = (f32[128,1536]{1,0:T(8,128)}, f32[128,1536]{1,0:T(8,128)S(1)}, u32[]{:S(2)}) copy-start(f32[128,1536]{1,0:T(8,128)S(1)} %get-tuple-element.2868) | copy-start | bytes 2359300
  417.5 624.8 %copy-start.19 = (f32[128,1536]{1,0:T(8,128)}, f32[128,1536]{1,0:T(8,128)S(1)}, u32[]{:S(2)}) copy-start(f32[128,1536]{1,0:T(8,128)S(1)} %get-tuple-element.2870) | copy-start | bytes 2359300
  417.7 328.2 %copy-start.33 = (bf16[128,1536]{1,0:T(8,128)(2,1)}, bf16[128,1536]{1,0:T(8,128)(2,1)S(1)}, u32[]{:S(2)}) copy-start(bf16[128,1536]{1,0:T(8,128)(2,1)S(1)} %multiply_convert_fusion.7) | copy-start | bytes 1179652
  594.2 318.2 %copy-start.54 = (bf16[1,2,128,1536]{3,2,1,0:T(8,128)(2,1)S(1)}, bf16[1,2,128,1536]{3,2,1,0:T(8,128)(2,1)}, u32[]{:S(2)}) copy-start(bf16[1,2,128,1536]{3,2,1,0:T(8,128)(2,1)} %param.61) | copy-start | bytes 2359300
  1073.8 135.7 %reduce-scatter.12.cloned.1.call-start = ((), (), s32[]{:S(2)}) async-start(), calls=%async_computation.20 | async-start | bytes 2228224 | tf_op jit(solution)/shard_map/reduce_scatter | solution.py:375
  1104.0 169.9 %reduce-scatter.18.cloned.1.call-start = ((), (), s32[]{:S(2)}) async-start(), calls=%async_computation.23 | async-start | bytes 2228224 | tf_op jit(solution)/shard_map/reduce_scatter | solution.py:378
  1106.9 231.4 %reduce-scatter.14.cloned.1.call-start = ((), (), s32[]{:S(2)}) async-start(), calls=%async_computation.21 | async-start | bytes 2228224 | tf_op jit(solution)/shard_map/reduce_scatter | solution.py:378
  1110.0 588.7 %reduce-scatter.22.cloned.1.call-start = ((), (), s32[]{:S(2)}) async-start(), calls=%async_computation.25 | async-start | bytes 1622016 | tf_op jit(solution)/shard_map/reduce_scatter | solution.py:453
  1219.4 480.7 %reduce-scatter.24.cloned.1.call-start = ((), (), s32[]{:S(2)}) async-start(), calls=%async_computation.26 | async-start | bytes 1622016 | tf_op jit(solution)/shard_map/reduce_scatter | solution.py:457
  1344.0 357.5 %reduce-scatter.20.cloned.1.call-start = ((), (), s32[]{:S(2)}) async-start(), calls=%async_computation.24 | async-start | bytes 9732096 | tf_op jit(solution)/shard_map/reduce_scatter | solution.py:449
  1362.1 463.6 %reduce-scatter.26.cloned.1.call-start = ((), (), s32[]{:S(2)}) async-start(), calls=%async_computation.27 | async-start | bytes 9732096 | tf_op jit(solution)/shard_map/reduce_scatter | solution.py:461
  1379.0 911.7 %reduce-scatter.28.cloned.1.call-start = ((), (), s32[]{:S(2)}) async-start(), calls=%async_computation.28 | async-start | bytes 56770560 | tf_op jit(solution)/shard_map/reduce_scatter | solution.py:436
  1456.6 1299.6 %reduce-scatter.30.cloned.1.call-start = ((), (), s32[]{:S(2)}) async-start(), calls=%async_computation.29 | async-start | bytes 56770560 | tf_op jit(solution)/shard_map/reduce_scatter | solution.py:439
  1534.3 1687.3 %reduce-scatter.32.cloned.1.call-start = ((), (), s32[]{:S(2)}) async-start(), calls=%async_computation.30 | async-start | bytes 56770560 | tf_op jit(solution)/shard_map/reduce_scatter | solution.py:429
  (122 other events, 3649.4 us)
Sparse Core Ops, SparseCore 0:
  129.2 34.0 all-gather.23
  166.1 37.1 all-gather.9
  206.0 37.3 all-gather.25
  246.0 36.8 all-gather.11
  285.7 62.4 all-gather.13
  351.0 61.7 all-gather.15
  415.7 163.7 all-gather.17
  582.4 163.4 all-gather.19
  748.9 163.4 all-gather.21
  1073.9 71.0 reduce-scatter.15
  1148.8 60.7 reduce-scatter.11
  1213.1 60.6 reduce-scatter.17
  1277.6 60.6 reduce-scatter.13
  1344.0 96.8 reduce-scatter.21
  1446.6 97.0 reduce-scatter.23
  1549.4 135.2 reduce-scatter.19
  1690.5 135.0 reduce-scatter.25
  1831.9 458.7 reduce-scatter.27
  2297.2 459.0 reduce-scatter.29
  2762.5 459.0 reduce-scatter.31
where the time goes:
time: 3250 us; the launch traced here: 3230 us
  waiting for transfers between devices  2340 us (72%)
  matrix products  320 us (10%)
  local copies, waits for them, and re-layouts  258 us (8%)
  blocking collectives  223 us (7%)
  other arithmetic  43.5 us (1%)
    reduce_scatter x1, waiting for transfers between devices, body(): lax.psum_scatter(flatten_lanes(grad_wgate), ('seq', 'fsdp'), scatter_dime...  463 us
    reduce_scatter x1, waiting for transfers between devices, body(): lax.psum_scatter(flatten_lanes(grad_wup), ('seq', 'fsdp'), scatter_dimens...  463 us
    reduce_scatter x1, waiting for transfers between devices, body(): lax.psum_scatter(flatten_lanes(grad_down), ('seq', 'fsdp'), scatter_dimen...  463 us
    reshape x7, local copies, waits for them, and re-layouts, flatten_lanes(): return matrix.reshape(-1, 128)  191 us
    all_gather x1, waiting for transfers between devices, body(): lax.all_gather(gate_weight, ('seq', 'fsdp'), axis=0, tiled=True)  162 us
    all_gather x1, waiting for transfers between devices, body(): lax.all_gather(down_weight, ('seq', 'fsdp'), axis=0, tiled=True)  152 us
    all_gather x1, waiting for transfers between devices, body(): lax.all_gather(up_weight, ('seq', 'fsdp'), axis=0, tiled=True)  152 us
    reduce_scatter x1, waiting for transfers between devices, body(): lax.psum_scatter(flatten_lanes(grad_woutput), ('seq', 'fsdp'), scatter_di...  122 us
  transfers between devices with their start and end apart: 20, of which 15 were waited for; matrix products, arithmetic and copies ran while one was open for 14% of the time, Pallas kernels for 0%

commit v1 on v0

v1 whole, which is shorter than its diff:
```python
import functools

import jax
import jax.numpy as jnp
from jax import lax
from jax.experimental import pallas as pl
from jax.experimental.pallas import tpu as pltpu
from jax.sharding import Mesh, PartitionSpec as P

QUERY_HEADS = 12
KEY_VALUE_HEADS = 2
HEAD_WIDTH = 128
EPSILON = 1e-06
THETA = 10000.0
GROUP = QUERY_HEADS // KEY_VALUE_HEADS
SCALE = HEAD_WIDTH ** (-0.5)
F32 = jnp.float32
BF16 = jnp.bfloat16
SWAP = [(0, 1), (1, 0)]


def locate(item_lengths, positions_at):
    ends = jnp.cumsum(item_lengths)
    starts = ends - item_lengths
    segment_ids = jnp.sum((ends[None, :] <= positions_at[:, None]).astype(jnp.int32), axis=1)
    onehot = segment_ids[:, None] == jnp.arange(item_lengths.shape[0], dtype=jnp.int32)[None, :]
    first = jnp.sum(jnp.where(onehot, starts[None, :], 0), axis=1)
    return (positions_at - first, first)


def rotary_tables(offsets, head_size):
    freqs = 1.0 / THETA ** (jnp.arange(0, head_size, 2, dtype=F32) / head_size)
    angles = offsets.astype(F32)[:, None] * freqs[None, :]
    cosine, sine = jnp.cos(angles), jnp.sin(angles)
    return (jnp.concatenate([cosine, cosine], axis=1), jnp.concatenate([sine, sine], axis=1))


def apply_rotary(values, cosine_table, sine_table):
    half = values.shape[-1] // 2
    turned = jnp.concatenate([-values[..., half:], values[..., :half]], axis=-1)
    return values * cosine_table[:, None, :] + turned * sine_table[:, None, :]


def inverse_rotary(grads, cosine_table, sine_table):
    half = grads.shape[-1] // 2
    scaled = grads * sine_table[:, None, :]
    turned = jnp.concatenate([scaled[..., half:], -scaled[..., :half]], axis=-1)
    return grads * cosine_table[:, None, :] + turned


def rms_forward(rows, gain):
    recip = lax.rsqrt(jnp.mean(rows * rows, axis=-1, keepdims=True) + EPSILON)
    return (rows * recip * gain, recip)


def rms_backward(rows, recip, gain, upstream):
    weighted = upstream * gain
    grad_rows = recip * weighted - rows * (recip * recip * recip) * jnp.mean(
        rows * weighted, axis=-1, keepdims=True
    )
    gain_grad = jnp.sum(upstream * rows * recip, axis=0)
    return (grad_rows, gain_grad)


def dot(left, right, dims, out=F32):
    return lax.dot_general(left, right, ((dims[0], dims[1]), ((), ())), preferred_element_type=out)


def rows_dot(left, right):
    return dot(left, right, ((0,), (0,)))


def cols_dot(left, right):
    return dot(left, right, ((1,), (1,)))


def mat_dot(left, right):
    return dot(left, right, ((1,), (0,)))


def attend_forward_kernel(meta, q_ref, k_ref, v_ref, span_ref, o_ref, lse_ref):
    rows = q_ref.shape[0]
    queries = jnp.concatenate(
        [q_ref[:, h * HEAD_WIDTH : (h + 1) * HEAD_WIDTH] for h in range(GROUP)], axis=0
    )
    first, last = span_ref[0:1, :], span_ref[1:2, :]
    wide = GROUP * rows
    local = lax.broadcasted_iota(jnp.int32, (rows, 1), 0)

    def step(block, carry):
        top, total, accum = carry
        slot = meta[2 + block]
        keys, values = k_ref[slot], v_ref[slot]
        scores = dot(keys, queries, ((1,), (1,))) * SCALE
        index = block * rows + local
        scores = jnp.where((index >= first) & (index <= last), scores, -1e30)
        new_top = jnp.maximum(top, jnp.max(scores, axis=0, keepdims=True))
        fade = jnp.exp(top - new_top)
        probs = jnp.exp(scores - new_top)
        total = total * fade + jnp.sum(probs, axis=0, keepdims=True)
        accum = accum * fade + dot(values, probs.astype(BF16), ((0,), (0,)))
        return (new_top, total, accum)

    top, total, accum = lax.fori_loop(
        meta[0],
        meta[1] + 1,
        step,
        (
            jnp.full((1, wide), -1e30, F32),
            jnp.zeros((1, wide), F32),
            jnp.zeros((HEAD_WIDTH, wide), F32),
        ),
    )
    attended = (accum / total).T.astype(BF16)
    for h in range(GROUP):
        o_ref[:, h * HEAD_WIDTH : (h + 1) * HEAD_WIDTH] = attended[h * rows : (h + 1) * rows]
    lse_ref[0] = top + jnp.log(total)


def attend_forward(meta, queries, stack, span):
    pieces, rows, _ = stack.shape
    width = queries.shape[1]
    part = width // KEY_VALUE_HEADS
    spec = pltpu.PrefetchScalarGridSpec(
        num_scalar_prefetch=1,
        grid=(KEY_VALUE_HEADS,),
        in_specs=[
            pl.BlockSpec((rows, part), lambda g, m: (0, g)),
            pl.BlockSpec((pieces, rows, HEAD_WIDTH), lambda g, m: (0, 0, g)),
            pl.BlockSpec((pieces, rows, HEAD_WIDTH), lambda g, m: (0, 0, KEY_VALUE_HEADS + g)),
            pl.BlockSpec((8, GROUP * rows), lambda g, m: (0, 0)),
        ],
        out_specs=[
            pl.BlockSpec((rows, part), lambda g, m: (0, g)),
            pl.BlockSpec((1, 1, GROUP * rows), lambda g, m: (g, 0, 0)),
        ],
    )
    return pl.pallas_call(
        attend_forward_kernel,
        grid_spec=spec,
        out_shape=(
            jax.ShapeDtypeStruct((rows, width), BF16),
            jax.ShapeDtypeStruct((KEY_VALUE_HEADS, 1, GROUP * rows), F32),
        ),
        cost_estimate=pl.CostEstimate(
            flops=4 * rows * rows * 6 * width, bytes_accessed=stack.size * 2, transcendentals=0
        ),
        name="attend_forward",
    )(meta, queries, stack, stack, span)


def attend_backward_kernel(
    meta, q_ref, do_ref, k_ref, v_ref, span_ref, lse_ref, dq_ref, dk_ref, dv_ref, p_ref, dp_ref
):
    rows = q_ref.shape[0]
    wide = GROUP * rows
    cols = [slice(h * HEAD_WIDTH, (h + 1) * HEAD_WIDTH) for h in range(GROUP)]
    queries = jnp.concatenate([q_ref[:, c] for c in cols], axis=0)
    grads = jnp.concatenate([do_ref[:, c] for c in cols], axis=0)
    first, last = span_ref[0:1, :], span_ref[1:2, :]
    lse = lse_ref[0]
    local = lax.broadcasted_iota(jnp.int32, (rows, 1), 0)
    low = meta[0]
    dk_ref[...] = jnp.zeros_like(dk_ref)
    dv_ref[...] = jnp.zeros_like(dv_ref)

    def collect(block, delta):
        slot = meta[2 + block]
        scores = dot(k_ref[slot], queries, ((1,), (1,))) * SCALE
        index = block * rows + local
        probs = jnp.where((index >= first) & (index <= last), jnp.exp(scores - lse), 0.0)
        grad_probs = dot(v_ref[slot], grads, ((1,), (1,)))
        p_ref[block - low] = probs
        dp_ref[block - low] = grad_probs
        return delta + jnp.sum(probs * grad_probs, axis=0, keepdims=True)

    delta = lax.fori_loop(low, meta[1] + 1, collect, jnp.zeros((1, wide), F32))

    def spread(block, accum):
        slot = meta[2 + block]
        probs = p_ref[block - low]
        grad_scores = (probs * (dp_ref[block - low] - delta)).astype(BF16)
        dk_ref[slot] = (mat_dot(grad_scores, queries) * SCALE).astype(BF16)
        dv_ref[slot] = mat_dot(probs.astype(BF16), grads).astype(BF16)
        return accum + dot(k_ref[slot], grad_scores, ((0,), (0,)))

    accum = lax.fori_loop(low, meta[1] + 1, spread, jnp.zeros((HEAD_WIDTH, wide), F32))
    grad_queries = (accum * SCALE).T
    for h in range(GROUP):
        dq_ref[:, cols[h]] = grad_queries[h * rows : (h + 1) * rows]


def attend_backward(meta, queries, grads, stack, span, lse):
    pieces, rows, _ = stack.shape
    width = queries.shape[1]
    part = width // KEY_VALUE_HEADS
    most = pieces // 2 + 1
    head = (pieces, rows, HEAD_WIDTH)
    spec = pltpu.PrefetchScalarGridSpec(
        num_scalar_prefetch=1,
        grid=(KEY_VALUE_HEADS,),
        in_specs=[
            pl.BlockSpec((rows, part), lambda g, m: (0, g)),
            pl.BlockSpec((rows, part), lambda g, m: (0, g)),
            pl.BlockSpec(head, lambda g, m: (0, 0, g)),
            pl.BlockSpec(head, lambda g, m: (0, 0, KEY_VALUE_HEADS + g)),
            pl.BlockSpec((8, GROUP * rows), lambda g, m: (0, 0)),
            pl.BlockSpec((1, 1, GROUP * rows), lambda g, m: (g, 0, 0)),
        ],
        out_specs=[
            pl.BlockSpec((rows, part), lambda g, m: (0, g)),
            pl.BlockSpec(head, lambda g, m: (0, 0, g)),
            pl.BlockSpec(head, lambda g, m: (0, 0, g)),
        ],
        scratch_shapes=[
            pltpu.VMEM((most, rows, GROUP * rows), F32),
            pltpu.VMEM((most, rows, GROUP * rows), F32),
        ],
    )
    kv_shape = jax.ShapeDtypeStruct((pieces, rows, KEY_VALUE_HEADS * HEAD_WIDTH), BF16)
    return pl.pallas_call(
        attend_backward_kernel,
        grid_spec=spec,
        out_shape=(jax.ShapeDtypeStruct((rows, width), F32), kv_shape, kv_shape),
        cost_estimate=pl.CostEstimate(
            flops=10 * rows * rows * 6 * width, bytes_accessed=stack.size * 4, transcendentals=0
        ),
        name="attend_backward",
    )(meta, queries, grads, stack, stack, span, lse)


def body(
    sizes,
    inputs,
    lengths,
    attn_gain,
    query_weight,
    query_bias,
    key_matrix,
    key_bias_vector,
    value_matrix,
    value_bias_vector,
    output_weight,
    mlp_gain,
    gate_weight,
    up_weight,
    down_weight,
    cotangent,
):
    far, fsdp = sizes
    micro, token_rows, width = inputs.shape[1:]
    shard = query_weight.shape[0]
    kv_width = key_matrix.shape[1]
    hidden_width = gate_weight.shape[1]
    devices = far * 8 * fsdp
    seq = far * 8
    ih, ip, iy, ic, ix = (lax.axis_index(name) for name in ("h", "p", "y", "c", "x"))
    me8 = (ip * 2 + iy) * 2 + ic
    me_seq = ih * 8 + me8

    def hop(array, axis, shift=1):
        if axis == "h":
            return lax.ppermute(array, "h", [(i, (i + shift) % far) for i in range(far)])
        return lax.ppermute(array, axis, SWAP)

    def gather_far(array):
        pair = jnp.concatenate([array, hop(array, "p")], axis=0)
        return jnp.concatenate([pair] + [hop(pair, "h", k) for k in range(1, far)], axis=0)

    def gather_seq(array):
        for axis in ("y", "c"):
            array = array if axis == "c" else gather_far(array)
            array = jnp.concatenate([array, hop(array, axis)], axis=0)
        return array

    def gather_all(array):
        array = gather_far(array)
        for axis in ("y", "x", "c"):
            array = jnp.concatenate([array, hop(array, axis)], axis=0)
        return array

    def halve(array, axis):
        half = array.shape[0] // 2
        received = hop(array[half:].astype(BF16), axis)
        return array[:half].astype(F32) + received.astype(F32)

    def reduce_seq(array):
        array = halve(array, "c").astype(BF16)
        array = halve(array, "y").astype(BF16)
        count = array.shape[0] // far
        total = array[:count].astype(F32)
        for k in range(1, far):
            total = total + hop(array[k * count : (k + 1) * count], "h", -k).astype(F32)
        return halve(total, "p")

    def pick(array, index, axis):
        return lax.dynamic_index_in_dim(array, index, axis, keepdims=False)

    def reduce_all(array):
        def fold(block, axis, name, index):
            sent = pick(block, 1 - index, axis)
            kept = pick(block, index, axis)
            return kept.astype(F32) + hop(sent, name).astype(F32)

        array = fold(array, 3, "c", ic).astype(BF16)
        array = fold(array, 3, "x", ix).astype(BF16)
        array = fold(array, 2, "y", iy).astype(BF16)
        array = fold(array, 1, "p", ip).astype(BF16)
        total = pick(array, ih, 0).astype(F32)
        for k in range(1, far):
            total = total + hop(pick(array, (ih + k) % far, 0), "h", k).astype(F32)
        return total

    def gather8(array):
        half = array.shape[0] // 2
        a, b = array[:half], array[half:]
        ay, bp = hop(a, "y"), hop(b, "p")
        a_far = hop(jnp.concatenate([a, ay], axis=0), "p")
        b_far = hop(jnp.concatenate([b, bp], axis=0), "y")
        quad = jnp.concatenate(
            [a, b, ay, b_far[:half], a_far[:half], bp, a_far[half:], b_far[half:]], axis=0
        )
        return jnp.concatenate([quad, hop(quad, "c")], axis=0)

    def reduce8(array):
        count = array.shape[0] // 16
        quad = halve(array, "c").reshape(2, 2, 2, count, width)
        a, b = quad[:, :, 0], quad[:, :, 1]
        a = a[0] + hop(a[1].astype(BF16), "p").astype(F32)
        b = b[:, 0] + hop(b[:, 1].astype(BF16), "y").astype(F32)
        a = a[0] + hop(a[1].astype(BF16), "y").astype(F32)
        b = b[0] + hop(b[1].astype(BF16), "p").astype(F32)
        return jnp.concatenate([a, b], axis=0)

    def exchange8(array):
        c = jnp.stack([array[:, :, 0], hop(array[:, :, 1], "c")], axis=2)
        y = jnp.stack([c[:, 0], hop(c[:, 1], "y")], axis=1)
        return jnp.stack([y[0], hop(y[1], "p")], axis=0)

    group_index = jnp.arange(8, dtype=jnp.int32) ^ me8
    seq_index = jnp.arange(seq, dtype=jnp.int32)
    seq_slot = (
        (((seq_index % 2) ^ ic) * 2 + ((seq_index // 2 % 2) ^ iy)) * far
        + (ih - seq_index // 8) % far
    ) * 2 + ((seq_index // 4 % 2) ^ ip)
    all_index = jnp.arange(devices, dtype=jnp.int32)
    dx, ds = all_index % fsdp, all_index // fsdp
    all_slot = (
        ((((ds % 2) ^ ic) * 2 + (dx ^ ix)) * 2 + ((ds // 2 % 2) ^ iy)) * far
        + (ih - ds // 8) % far
    ) * 2 + ((ds // 4 % 2) ^ ip)
    weight_slot = ((ds // 8) * fsdp + dx) * 8 + ((ds % 8) ^ me8)
    far_index = jnp.arange(devices, dtype=jnp.int32)
    back_slot = ((far_index // (8 * fsdp)) * 8 + ((far_index % 8) ^ me8)) * fsdp + (
        far_index // 8 % fsdp
    )

    def ordered(array, columns):
        return jnp.take(array.reshape(devices, -1, columns), all_slot, axis=0).reshape(-1, columns)

    vectors = jnp.concatenate(
        [attn_gain, query_bias, key_bias_vector, value_bias_vector, mlp_gain]
    ).astype(F32)[None]
    vectors = jnp.take(gather_all(vectors), all_slot, axis=0)
    cuts = [0]
    for part in (attn_gain, query_bias, key_bias_vector, value_bias_vector, mlp_gain):
        cuts.append(cuts[-1] + part.shape[0])
    gain_attn, b_query, b_key, b_value, gain_mlp = (
        vectors[:, cuts[i] : cuts[i + 1]].reshape(-1) for i in range(5)
    )
    w_kv = ordered(
        gather_all(jnp.concatenate([key_matrix, value_matrix], axis=1)), 2 * kv_width
    )
    w_query = ordered(gather_all(query_weight), width)

    rows = inputs[0].astype(F32).reshape(micro * token_rows, width)
    positions_at = me_seq * token_rows + jnp.arange(token_rows, dtype=jnp.int32)
    tables, spans, metas = [], [], []
    for number in range(micro):
        offsets, first = locate(lengths[0, number], positions_at)
        tables.append(rotary_tables(offsets, HEAD_WIDTH))
        spans.append(
            jnp.concatenate(
                [
                    jnp.tile(first, GROUP)[None],
                    jnp.tile(positions_at, GROUP)[None],
                    jnp.zeros((6, GROUP * token_rows), jnp.int32),
                ],
                axis=0,
            )
        )
        low = jnp.maximum(first[0] // token_rows, me_seq - seq // 2)
        metas.append(jnp.concatenate([jnp.stack([low, me_seq]), seq_slot]).astype(jnp.int32))
    cosine_table = jnp.concatenate([t[0] for t in tables], axis=0)
    sine_table = jnp.concatenate([t[1] for t in tables], axis=0)

    normed, recip_one = rms_forward(rows, gain_attn)
    normed_low = normed.astype(BF16)
    kv_pre = mat_dot(normed_low, w_kv)
    key_rotated = apply_rotary(
        (kv_pre[:, :kv_width] + b_key).reshape(-1, KEY_VALUE_HEADS, HEAD_WIDTH),
        cosine_table,
        sine_table,
    ).reshape(-1, kv_width)
    own_kv = jnp.concatenate([key_rotated, kv_pre[:, kv_width:] + b_value], axis=1).astype(BF16)
    stacks = [
        gather_seq(own_kv[m * token_rows : (m + 1) * token_rows]).reshape(
            seq, token_rows, 2 * kv_width
        )
        for m in range(micro)
    ]
    w_output = ordered(gather_all(output_weight), width)
    query_rotated = (
        apply_rotary(
            (mat_dot(normed_low, w_query) + b_query).reshape(-1, QUERY_HEADS, HEAD_WIDTH),
            cosine_table,
            sine_table,
        )
        .astype(BF16)
        .reshape(-1, width)
    )

    def slices(matrix):
        parts = matrix.reshape(shard, far, 8, hidden_width // (8 * far))
        return parts.transpose(2, 0, 1, 3).reshape(8, shard, hidden_width // 8)

    both = jnp.concatenate([slices(gate_weight), slices(up_weight)], axis=2)
    both = jnp.take(both, group_index, axis=0).reshape(2, 2, 2, shard, -1)
    both = exchange8(both).reshape(8 * shard, -1)
    slice_width = hidden_width // 8

    def whole(part):
        part = lax.all_gather(part, ("h", "x"), axis=0, tiled=True)
        part = jnp.take(part.reshape(devices, shard, slice_width), weight_slot, axis=0)
        return part.reshape(-1, slice_width)

    w_gate, w_up = whole(both[:, :slice_width]), whole(both[:, slice_width:])
    w_down = lax.all_gather(down_weight, ("h", "x"), axis=0, tiled=True)
    upstream_low = [cotangent[0, m] for m in range(micro)]
    upstream_all = [gather8(upstream_low[m]) for m in range(micro)]

    kept = []
    for m in range(micro):
        part = slice(m * token_rows, (m + 1) * token_rows)
        attended, lse = attend_forward(metas[m], query_rotated[part], stacks[m], spans[m])
        middle = rows[part] + mat_dot(attended, w_output)
        normed_two, recip_two = rms_forward(middle, gain_mlp)
        kept.append((attended, lse, middle, recip_two, gather8(normed_two.astype(BF16))))

    results, grads_two = [], []
    g_gate = g_up = g_down = 0.0
    for m in range(micro):
        middle, recip_two, tokens = kept[m][2:]
        gate_pre = mat_dot(tokens, w_gate)
        up_pre = mat_dot(tokens, w_up)
        sigma = jax.nn.sigmoid(gate_pre)
        activated = gate_pre * sigma
        hidden = (activated * up_pre).astype(BF16)
        grad_hidden = cols_dot(upstream_all[m], w_down)
        grad_gate = (grad_hidden * up_pre * sigma * (1.0 + gate_pre * (1.0 - sigma))).astype(BF16)
        grad_up = (grad_hidden * activated).astype(BF16)
        grads_two.append(reduce8(cols_dot(grad_gate, w_gate) + cols_dot(grad_up, w_up)))
        results.append((middle + reduce8(mat_dot(hidden, w_down))).astype(BF16))
        g_gate = g_gate + rows_dot(tokens, grad_gate)
        g_up = g_up + rows_dot(tokens, grad_up)
        g_down = g_down + rows_dot(hidden, upstream_all[m])

    gain_mlp_sum = 0.0
    grad_middles, grad_branches, grad_queries, grad_kvs = [], [], [], []
    for m in range(micro):
        attended, lse, middle, recip_two, _ = kept[m]
        part = slice(m * token_rows, (m + 1) * token_rows)
        grad_norm, gain_part = rms_backward(middle, recip_two, gain_mlp, grads_two[m])
        gain_mlp_sum = gain_mlp_sum + gain_part
        grad_middle = upstream_low[m].astype(F32) + grad_norm
        grad_branch = grad_middle.astype(BF16)
        grad_attended = cols_dot(grad_branch, w_output).astype(BF16)
        grad_query, grad_keys, grad_values = attend_backward(
            metas[m], query_rotated[part], grad_attended, stacks[m], spans[m], lse
        )
        stacked = jnp.concatenate([grad_keys, grad_values], axis=2)
        grad_kvs.append(reduce_seq(stacked.reshape(seq * token_rows, 2 * kv_width)))
        grad_middles.append(grad_middle)
        grad_branches.append(grad_branch)
        grad_queries.append(grad_query)

    blocks = (far, 2, 2, 2, fsdp, shard)
    g_output = rows_dot(
        jnp.concatenate([kept[m][0] for m in range(micro)], axis=0),
        jnp.concatenate(grad_branches, axis=0),
    ).astype(BF16)
    output_part = reduce_all(g_output.reshape(blocks + (width,)))

    grad_middle = jnp.concatenate(grad_middles, axis=0)
    grad_query = (
        inverse_rotary(
            jnp.concatenate(grad_queries, axis=0).reshape(-1, QUERY_HEADS, HEAD_WIDTH),
            cosine_table,
            sine_table,
        )
        .reshape(-1, width)
        .astype(BF16)
    )
    grad_kv = jnp.concatenate(grad_kvs, axis=0)
    grad_key = inverse_rotary(
        grad_kv[:, :kv_width].reshape(-1, KEY_VALUE_HEADS, HEAD_WIDTH), cosine_table, sine_table
    ).reshape(-1, kv_width)
    grad_kv = jnp.concatenate([grad_key, grad_kv[:, kv_width:]], axis=1).astype(BF16)
    grad_normed = cols_dot(grad_query, w_query) + cols_dot(grad_kv, w_kv)
    grad_rows, gain_attn_sum = rms_backward(rows, recip_one, gain_attn, grad_normed)
    input_grad = grad_middle + grad_rows
    query_part = reduce_all(
        rows_dot(normed_low, grad_query).astype(BF16).reshape(blocks + (width,))
    )
    kv_part = reduce_all(
        rows_dot(normed_low, grad_kv).astype(BF16).reshape(blocks + (2 * kv_width,))
    )
    bias_query = jnp.sum(grad_query.astype(F32), axis=0)
    bias_kv = jnp.sum(grad_kv.astype(F32), axis=0)
    vector_sums = jnp.concatenate(
        [
            v.reshape(devices, -1)
            for v in (
                gain_attn_sum,
                bias_query,
                bias_kv[:kv_width],
                bias_kv[kv_width:],
                gain_mlp_sum,
            )
        ],
        axis=1,
    )
    vector_part = lax.psum_scatter(
        vector_sums, ("h", "p", "y", "c", "x"), scatter_dimension=0, tiled=True
    )[0]

    def scattered(grad):
        grad = jnp.take(
            grad.astype(BF16).reshape(devices, shard, slice_width), back_slot, axis=0
        )
        return lax.psum_scatter(
            grad.reshape(devices * shard, slice_width), ("h", "x"), scatter_dimension=0, tiled=True
        )

    down_part = lax.psum_scatter(
        g_down.astype(BF16), ("h", "x"), scatter_dimension=0, tiled=True
    ).astype(F32)
    both = jnp.concatenate([scattered(g_gate), scattered(g_up)], axis=1)
    both = exchange8(both.reshape(2, 2, 2, shard, -1)).reshape(8, shard, -1)
    both = jnp.take(both, group_index, axis=0)

    def joined(part):
        part = part.reshape(8, shard, far, -1).transpose(1, 2, 0, 3)
        return part.reshape(shard, hidden_width).astype(F32)

    return (
        jnp.stack(results)[None],
        input_grad.reshape(1, micro, token_rows, width),
        vector_part[cuts[0] : cuts[1]],
        query_part,
        vector_part[cuts[1] : cuts[2]],
        kv_part[:, :kv_width],
        vector_part[cuts[2] : cuts[3]],
        kv_part[:, kv_width:],
        vector_part[cuts[3] : cuts[4]],
        output_part,
        vector_part[cuts[4] : cuts[5]],
        joined(both[:, :, :slice_width]),
        joined(both[:, :, slice_width:]),
        down_part,
    )


def solution(mesh):
    fsdp = mesh.shape["fsdp"]
    far = mesh.shape["seq"] // 8
    inner = Mesh(mesh.devices.reshape(far, 2, 2, 2, fsdp), ("h", "p", "y", "c", "x"))
    seq = ("h", "p", "y", "c")
    every = seq + ("x",)
    tokens = P("x", None, seq, None)
    matrix, vector = P(every, None), P(every)
    in_specs = (
        tokens,
        P("x", None, None),
        vector,
        matrix,
        vector,
        matrix,
        vector,
        matrix,
        vector,
        matrix,
        vector,
        matrix,
        matrix,
        matrix,
        tokens,
    )
    out_specs = (
        tokens,
        tokens,
        vector,
        matrix,
        vector,
        matrix,
        vector,
        matrix,
        vector,
        matrix,
        vector,
        matrix,
        matrix,
        matrix,
    )
    return jax.shard_map(
        functools.partial(body, (far, fsdp)),
        mesh=inner,
        in_specs=in_specs,
        out_specs=out_specs,
        check_vma=False,
    )
```

time: 3250 us -> 966 us (0.30)
  waiting for transfers between devices: 2340 us -> 379 us
  matrix products: 320 us -> 129 us
  blocking collectives: 223 us -> 40 us
  starting transfers between devices: 1.96 us -> 116 us
  local copies, waits for them, and re-layouts: 258 us -> 177 us
  other arithmetic: 43.5 us -> 78.9 us
    reduce_scatter x11 -> x3, waiting for transfers between devices: 1730 us -> 0.01 us  [the longest x2 0.01 us: scattered(): lax.psum_scatter(grad.reshape(devices * shard, slice_width), ('h', 'x'),...]
    all_gather x9 -> x3, waiting for transfers between devices: 609 us -> 0.02 us  [the longest x2 0.02 us: whole(): part = lax.all_gather(part, ('h', 'x'), axis=0, tiled=True)]
    ppermute x0 -> x97, waiting for transfers between devices: none -> 378 us  [the longest x86 269 us: hop(): return lax.ppermute(array, axis, SWAP)]
    reshape x18 -> x12, local copies, waits for them, and re-layouts: 209 us -> 11 us  [the longest x4 6.6 us: slices(): parts = matrix.reshape(shard, far, 8, hidden_width // (8 * far))]
    dot_general x53 -> x29, matrix products: 320 us -> 129 us  [dot(): lax.dot_general(left, right, ((dims[0], dims[1]), ((), ())), preferred_el...]
    all_gather x2 -> x0, blocking collectives: 140 us -> none  [the longest x1 71 us: body(): lax.all_gather(value_matrix, ('seq', 'fsdp'), axis=0, tiled=True)]
    ppermute x0 -> x97, starting transfers between devices: none -> 115 us  [the longest x86 103 us: hop(): return lax.ppermute(array, axis, SWAP)]
    unnamed x2 -> x1, blocking collectives: 82.7 us -> 40 us
  transfers between devices with their start and end apart: 20 -> 103, of which waited for: 15 -> 51; matrix products, arithmetic and copies ran while one was open for 14% -> 28% of each run, Pallas kernels for 0% -> 2%
where the time goes in v1:
time: 966 us; the launch traced here: 957 us
  waiting for transfers between devices  379 us (39%)
  local copies, waits for them, and re-layouts  177 us (18%)
  matrix products  129 us (13%)
  starting transfers between devices  116 us (12%)
  other arithmetic  78.9 us (8%)
  blocking collectives  40 us (4%)
  Pallas kernels  19.7 us (2%)
  between operations  17.9 us (2%)
    ppermute x86, waiting for transfers between devices, hop(): return lax.ppermute(array, axis, SWAP)  269 us
    dot_general x29, matrix products, dot(): lax.dot_general(left, right, ((dims[0], dims[1]), ((), ())), preferred_el...  129 us
    ppermute x11, waiting for transfers between devices, hop(): lax.ppermute(array, 'h', [(i, (i + shift) % far) for i in range(far)])  109 us
    ppermute x86, starting transfers between devices, hop(): return lax.ppermute(array, axis, SWAP)  103 us
    unnamed x330, local copies, waits for them, and re-layouts  58.7 us
    unnamed x1, blocking collectives  40 us
  transfers between devices with their start and end apart: 103, of which 51 were waited for; matrix products, arithmetic and copies ran while one was open for 28% of the time, Pallas kernels for 2%

profile of v1, /device:TPU:0, one launch (start us, length us, event | category | flops | bytes accessed | tf_op | source)
XLA Modules:
  0.0 957.5 jit_solution(2008525567368622184)
XLA Ops:
  24.5 19.9 %collective-permute-done.30 = bf16[2,2,48,2240]{3,2,0,1:T(8,128)(2,1)S(1)} collective-permute-done((bf16[2,2,48,2240]{3,2,0,1:T(8,128)(2,1)S(1)}, bf16[2,2,48,2240]{3,2,0,1:T(8,128)(2,1)S(1)}, u32[]{:S(2)}, u32[]{:S(2)}) %collective-permute-start.30) | collective-permute-done | bytes 860192 | tf_op jit(solution)/shard_map/ppermute | solution.py:264
  46.5 19.3 %collective-permute-done.31 = bf16[2,2,48,2240]{3,2,1,0:T(8,128)(2,1)S(1)} collective-permute-done((bf16[2,2,48,2240]{3,2,1,0:T(8,128)(2,1)S(1)}, bf16[2,2,48,2240]{3,2,1,0:T(8,128)(2,1)S(1)}, u32[]{:S(2)}, u32[]{:S(2)}) %collective-permute-start.31) | collective-permute-done | bytes 860192 | tf_op jit(solution)/shard_map/ppermute | solution.py:264
  112.0 23.9 %collective-permute-done.11 = bf16[96,512]{1,0:T(8,128)(2,1)S(1)} collective-permute-done((bf16[96,512]{1,0:T(8,128)(2,1)S(1)}, bf16[96,512]{1,0:T(8,128)(2,1)S(1)}, u32[]{:S(2)}, u32[]{:S(2)}) %collective-permute-start.11) | collective-permute-done | bytes 98336 | tf_op jit(solution)/shard_map/ppermute | solution.py:263
  142.8 10.3 %collective-permute-start.12 = (bf16[192,512]{1,0:T(8,128)(2,1)S(1)}, bf16[192,512]{1,0:T(8,128)(2,1)S(1)}, u32[]{:S(2)}, u32[]{:S(2)}) collective-permute-start(bf16[192,512]{1,0:T(8,128)(2,1)S(1)} %pad_maximum_fusion.35), channel_id=1, source_target_pairs={{0,4},{4,0},{1,5},{5,1},{2,6},{6,2},{3,7},{7,3},{8,12},{12,8},{9,1... | collective-permute-start | bytes 589832 | tf_op jit(solution)/shard_map/ppermute | solution.py:264
  164.0 10.8 %collective-permute-done.6 = bf16[96,1536]{1,0:T(8,128)(2,1)S(1)} collective-permute-done((bf16[96,1536]{1,0:T(8,128)(2,1)S(1)}, bf16[96,1536]{1,0:T(8,128)(2,1)S(1)}, u32[]{:S(2)}, u32[]{:S(2)}) %collective-permute-start.6) | collective-permute-done | bytes 294944 | tf_op jit(solution)/shard_map/ppermute | solution.py:263
  232.4 28.8 %collective-permute-done.16 = bf16[256,512]{1,0:T(8,128)(2,1)S(1)} collective-permute-done((bf16[256,512]{1,0:T(8,128)(2,1)S(1)}, bf16[256,512]{1,0:T(8,128)(2,1)S(1)}, u32[]{:S(2)}, u32[]{:S(2)}) %collective-permute-start.16) | collective-permute-done | bytes 262176 | tf_op jit(solution)/shard_map/ppermute | solution.py:263
  261.2 10.5 %collective-permute-done.38 = bf16[256,512]{1,0:T(8,128)(2,1)S(1)} collective-permute-done((bf16[256,512]{1,0:T(8,128)(2,1)S(1)}, bf16[256,512]{1,0:T(8,128)(2,1)S(1)}, u32[]{:S(2)}, u32[]{:S(2)}) %collective-permute-start.38) | collective-permute-done | bytes 262176 | tf_op jit(solution)/shard_map/ppermute | solution.py:263
  417.2 7.8 fusion.163
  425.0 8.0 fusion.164
  433.1 10.6 %multiply_convert_fusion = (bf16[1024,1120]{0,1:T(8,128)(2,1)}, bf16[1024,1120]{0,1:T(8,128)(2,1)S(1)}, bf16[1024,1120]{0,1:T(8,128)(2,1)}) fusion(f32[1024,1120]{0,1:T(8,128)} %fusion.163, f32[1024,1120]{0,1:T(8,128)} %fusion.164, bf16[1024,1536]{1,0:T(8,128)(2,1)S(1)} %copy-done.77, bf16[1120,1536]{1,0:T(8,128)(2,1)} %all-gather.8.cloned.1.call-done), kind=kOutput, calls=%fused_computation.24 | convolution fusion | flops 3540418560 | bytes 22642688 | tf_op jit(solution)/shard_map/dot_general | solution.py:66
  450.8 9.6 multiply_convert_fusion.2
  588.0 8.0 collective-permute-done.67
  597.7 15.1 %collective-permute-done.47 = bf16[2,64,1536]{2,1,0:T(8,128)(2,1)S(1)} collective-permute-done((bf16[2,64,1536]{2,1,0:T(8,128)(2,1)S(1)}, bf16[2,64,1536]{2,1,0:T(8,128)(2,1)S(1)}, u32[]{:S(2)}, u32[]{:S(2)}) %collective-permute-start.47) | collective-permute-done | bytes 393248 | tf_op jit(solution)/shard_map/ppermute | solution.py:264
  614.6 12.2 %collective-permute-done.33 = bf16[2,64,1536]{2,1,0:T(8,128)(2,1)S(1)} collective-permute-done((bf16[2,64,1536]{2,1,0:T(8,128)(2,1)S(1)}, bf16[2,64,1536]{2,1,0:T(8,128)(2,1)S(1)}, u32[]{:S(2)}, u32[]{:S(2)}) %collective-permute-start.33) | collective-permute-done | bytes 393248 | tf_op jit(solution)/shard_map/ppermute | solution.py:264
  694.6 11.1 %collective-permute-done.76 = bf16[512,512]{1,0:T(8,128)(2,1)S(1)} collective-permute-done((bf16[512,512]{1,0:T(8,128)(2,1)S(1)}, bf16[512,512]{1,0:T(8,128)(2,1)S(1)}, u32[]{:S(2)}, u32[]{:S(2)}) %collective-permute-start.76) | collective-permute-done | bytes 524320 | tf_op jit(solution)/shard_map/ppermute | solution.py:264
  706.1 10.8 %collective-permute-done.72 = bf16[512,512]{1,0:T(8,128)(2,1)S(1)} collective-permute-done((bf16[512,512]{1,0:T(8,128)(2,1)S(1)}, bf16[512,512]{1,0:T(8,128)(2,1)S(1)}, u32[]{:S(2)}, u32[]{:S(2)}) %collective-permute-start.72) | collective-permute-done | bytes 524320 | tf_op jit(solution)/shard_map/ppermute | solution.py:264
  723.4 16.8 %collective-permute-done.77 = bf16[256,512]{1,0:T(8,128)(2,1)S(1)} collective-permute-done((bf16[256,512]{1,0:T(8,128)(2,1)S(1)}, bf16[256,512]{1,0:T(8,128)(2,1)S(1)}, u32[]{:S(2)}, u32[]{:S(2)}) %collective-permute-start.77) | collective-permute-done | bytes 262176 | tf_op jit(solution)/shard_map/ppermute | solution.py:263
  740.7 10.1 %collective-permute-done.73 = bf16[256,512]{1,0:T(8,128)(2,1)S(1)} collective-permute-done((bf16[256,512]{1,0:T(8,128)(2,1)S(1)}, bf16[256,512]{1,0:T(8,128)(2,1)S(1)}, u32[]{:S(2)}, u32[]{:S(2)}) %collective-permute-start.73) | collective-permute-done | bytes 262176 | tf_op jit(solution)/shard_map/ppermute | solution.py:263
  774.9 40.0 %all-reduce = f32[32,160]{1,0:T(8,128)S(1)} all-reduce(f32[32,160]{1,0:T(8,128)S(1)} %concatenate.378), channel_id=2, replica_groups=mesh['h'=2,'p'=2,'y'=2,'c'=2,'x'=2] {'h','p','y','c','x'}, use_global_device_ids=true, to_apply=%region_17.21.clone | all-reduce | flops 5120 | bytes 40960
  844.6 13.6 %collective-permute-done.80 = bf16[2,2,2,48,1536]{4,3,0,1,2:T(8,128)(2,1)S(1)} collective-permute-done((bf16[2,2,2,48,1536]{4,3,0,1,2:T(8,128)(2,1)S(1)}, bf16[2,2,2,48,1536]{4,3,0,1,2:T(8,128)(2,1)S(1)}, u32[]{:S(2)}, u32[]{:S(2)}) %collective-permute-start.80) | collective-permute-done | bytes 1179680 | tf_op jit(solution)/shard_map/ppermute | solution.py:264
  859.3 20.9 %collective-permute-done.90 = bf16[2,2,2,48,1536]{4,3,0,1,2:T(8,128)(2,1)S(1)} collective-permute-done((bf16[2,2,2,48,1536]{4,3,0,1,2:T(8,128)(2,1)S(1)}, bf16[2,2,2,48,1536]{4,3,0,1,2:T(8,128)(2,1)S(1)}, u32[]{:S(2)}, u32[]{:S(2)}) %collective-permute-start.90) | collective-permute-done | bytes 1179680 | tf_op jit(solution)/shard_map/ppermute | solution.py:264
  885.5 7.2 collective-permute-done.91
  904.1 8.2 collective-permute-done.95
  917.7 12.3 %collective-permute-done.96 = bf16[2,2,48,2240]{3,2,1,0:T(8,128)(2,1)S(1)} collective-permute-done((bf16[2,2,48,2240]{3,2,1,0:T(8,128)(2,1)S(1)}, bf16[2,2,48,2240]{3,2,1,0:T(8,128)(2,1)S(1)}, u32[]{:S(2)}, u32[]{:S(2)}) %collective-permute-start.96) | collective-permute-done | bytes 860192 | tf_op jit(solution)/shard_map/ppermute | solution.py:264
  (841 shorter events, 593.7 us)
Async XLA Ops:
  7.2 388.1 %all-gather.4.cloned.1.call-start = ((), (), s32[]{:S(2)}) async-start(), calls=%async_computation.3 | async-start | bytes 4423680 | tf_op jit(solution)/shard_map/all_gather | solution.py:433
  67.7 330.7 %all-gather.6.cloned.1.call-start = ((), (), s32[]{:S(2)}) async-start(), calls=%async_computation.4 | async-start | bytes 4423680 | tf_op jit(solution)/shard_map/all_gather | solution.py:433
  68.5 364.6 %all-gather.8.cloned.1.call-start = ((), (), s32[]{:S(2)}) async-start(), calls=%async_computation.5 | async-start | bytes 4300800 | tf_op jit(solution)/shard_map/all_gather | solution.py:438
  70.3 39.5 %collective-permute-start.19 = (bf16[48,1536]{1,0:T(8,128)(2,1)S(1)}, bf16[48,1536]{1,0:T(8,128)(2,1)S(1)}, u32[]{:S(2)}, u32[]{:S(2)}) collective-permute-start(bf16[48,1536]{1,0:T(8,128)(2,1)S(1)} %copy-done.30), channel_id=1, source_target_pairs={{0,8},{8,0},{1,9},{9,1},{2,10},{10,2},{3,11},{11,3},{4,12},{12,4},... | collective-permute-start | bytes 442376 | tf_op jit(solution)/shard_map/ppermute | solution.py:264
  70.8 41.1 %collective-permute-start.5 = (bf16[48,1536]{1,0:T(8,128)(2,1)S(1)}, bf16[48,1536]{1,0:T(8,128)(2,1)S(1)}, u32[]{:S(2)}, u32[]{:S(2)}) collective-permute-start(bf16[48,1536]{1,0:T(8,128)(2,1)S(1)} %copy-done.31), channel_id=1, source_target_pairs={{0,8},{8,0},{1,9},{9,1},{2,10},{10,2},{3,11},{11,3},{4,12},{12,4},... | collective-permute-start | bytes 442376 | tf_op jit(solution)/shard_map/ppermute | solution.py:264
  74.8 68.0 %collective-permute-start.51 = (bf16[64,1536]{1,0:T(8,128)(2,1)S(1)}, bf16[64,1536]{1,0:T(8,128)(2,1)}, u32[]{:S(2)}, u32[]{:S(2)}) collective-permute-start(bf16[64,1536]{1,0:T(8,128)(2,1)S(1)} %get-tuple-element.116), channel_id=1, source_target_pairs={{0,4},{4,0},{1,5},{5,1},{2,6},{6,2},{3,7},{7,3},{8,12},{12,8},{9,1... | collective-permute-start | bytes 589832 | tf_op jit(solution)/shard_map/ppermute | solution.py:264
  76.3 807.1 %reduce-scatter.6.cloned.1.call-start = ((), (), s32[]{:S(2)}) async-start(), calls=%async_computation.7 | async-start | bytes 4423680 | tf_op jit(solution)/shard_map/reduce_scatter | solution.py:541
  102.4 36.5 %collective-permute-start.52 = (bf16[64,1536]{1,0:T(8,128)(2,1)}, bf16[64,1536]{1,0:T(8,128)(2,1)S(1)}, u32[]{:S(2)}, u32[]{:S(2)}) collective-permute-start(bf16[64,1536]{1,0:T(8,128)(2,1)} %get-tuple-element.115), channel_id=1, source_target_pairs={{0,8},{8,0},{1,9},{9,1},{2,10},{10,2},{3,11},{11,3},{4,12},{12,4},... | collective-permute-start | bytes 589832 | tf_op jit(solution)/shard_map/ppermute | solution.py:264
  105.9 48.3 %collective-permute-start.61 = (bf16[64,1536]{1,0:T(8,128)(2,1)S(1)}, bf16[64,1536]{1,0:T(8,128)(2,1)S(1)}, u32[]{:S(2)}, u32[]{:S(2)}) collective-permute-start(bf16[64,1536]{1,0:T(8,128)(2,1)S(1)} %get-tuple-element.118), channel_id=1, source_target_pairs={{0,4},{4,0},{1,5},{5,1},{2,6},{6,2},{3,7},{7,3},{8,12},{12,8},{9,1... | collective-permute-start | bytes 589832 | tf_op jit(solution)/shard_map/ppermute | solution.py:264
  109.7 44.3 %collective-permute-start.62 = (bf16[64,1536]{1,0:T(8,128)(2,1)S(1)}, bf16[64,1536]{1,0:T(8,128)(2,1)S(1)}, u32[]{:S(2)}, u32[]{:S(2)}) collective-permute-start(bf16[64,1536]{1,0:T(8,128)(2,1)S(1)} %get-tuple-element.117), channel_id=1, source_target_pairs={{0,8},{8,0},{1,9},{9,1},{2,10},{10,2},{3,11},{11,3},{4,12},{12,4},... | collective-permute-start | bytes 589832 | tf_op jit(solution)/shard_map/ppermute | solution.py:264
  189.7 105.3 %collective-permute-start.55 = (bf16[512,1536]{1,0:T(8,128)(2,1)}, bf16[512,1536]{1,0:T(8,128)(2,1)}, u32[]{:S(2)}, u32[]{:S(2)}) collective-permute-start(bf16[512,1536]{1,0:T(8,128)(2,1)} %get-tuple-element.127), channel_id=1, source_target_pairs={{0,2},{2,0},{1,3},{3,1},{4,6},{6,4},{5,7},{7,5},{8,10},{10,8},{9,1... | collective-permute-start | bytes 4718600 | tf_op jit(solution)/shard_map/ppermute | solution.py:264
  200.5 72.8 %collective-permute-start.22 = (bf16[384,1536]{1,0:T(8,128)(2,1)}, bf16[384,1536]{1,0:T(8,128)(2,1)}, u32[]{:S(2)}, u32[]{:S(2)}) collective-permute-start(bf16[384,1536]{1,0:T(8,128)(2,1)} %pad_maximum_fusion.6), channel_id=1, source_target_pairs={{0,1},{1,0},{2,3},{3,2},{4,5},{5,4},{6,7},{7,6},{8,9},{9,8},{10,11... | collective-permute-start | bytes 3538952 | tf_op jit(solution)/shard_map/ppermute | solution.py:264
  206.9 69.4 %collective-permute-start.8 = (bf16[384,1536]{1,0:T(8,128)(2,1)}, bf16[384,1536]{1,0:T(8,128)(2,1)}, u32[]{:S(2)}, u32[]{:S(2)}) collective-permute-start(bf16[384,1536]{1,0:T(8,128)(2,1)} %pad_maximum_fusion.5), channel_id=1, source_target_pairs={{0,1},{1,0},{2,3},{3,2},{4,5},{5,4},{6,7},{7,6},{8,9},{9,8},{10,11... | collective-permute-start | bytes 3538952 | tf_op jit(solution)/shard_map/ppermute | solution.py:264
  228.5 43.2 %collective-permute-start.38 = (bf16[256,512]{1,0:T(8,128)(2,1)S(1)}, bf16[256,512]{1,0:T(8,128)(2,1)S(1)}, u32[]{:S(2)}, u32[]{:S(2)}) collective-permute-start(bf16[256,512]{1,0:T(8,128)(2,1)S(1)} %pad_maximum_fusion.32), channel_id=1, source_target_pairs={{0,16},{16,0},{1,17},{17,1},{2,18},{18,2},{3,19},{19,3},{4,20},{20... | collective-permute-start | bytes 786440 | tf_op jit(solution)/shard_map/ppermute | solution.py:263
  261.2 36.7 %collective-permute-start.65 = (bf16[512,1536]{1,0:T(8,128)(2,1)S(1)}, bf16[512,1536]{1,0:T(8,128)(2,1)S(1)}, u32[]{:S(2)}, u32[]{:S(2)}) collective-permute-start(bf16[512,1536]{1,0:T(8,128)(2,1)S(1)} %copy-done.72), channel_id=1, source_target_pairs={{0,2},{2,0},{1,3},{3,1},{4,6},{6,4},{5,7},{7,5},{8,10},{10,8},{9,1... | collective-permute-start | bytes 4718600 | tf_op jit(solution)/shard_map/ppermute | solution.py:264
  497.5 385.9 %reduce-scatter.4.cloned.1.call-start = ((), (), s32[]{:S(2)}) async-start(), calls=%async_computation.6 | async-start | bytes 4423680 | tf_op jit(solution)/shard_map/reduce_scatter | solution.py:541
  500.4 414.8 %reduce-scatter.8.cloned.1.call-start = ((), (), s32[]{:S(2)}) async-start(), calls=%async_computation.8 | async-start | bytes 4300800 | tf_op jit(solution)/shard_map/reduce_scatter | solution.py:545
  513.8 40.0 %collective-permute-start.56 = (bf16[512,1536]{1,0:T(8,128)(2,1)}, bf16[512,1536]{1,0:T(8,128)(2,1)}, u32[]{:S(2)}, u32[]{:S(2)}) collective-permute-start(bf16[512,1536]{1,0:T(8,128)(2,1)} %slice.1032), channel_id=1, source_target_pairs={{0,2},{2,0},{1,3},{3,1},{4,6},{6,4},{5,7},{7,5},{8,10},{10,8},{9,1... | collective-permute-start | bytes 4718600 | tf_op jit(solution)/shard_map/ppermute | solution.py:264
  585.7 41.1 %collective-permute-start.33 = (bf16[2,64,1536]{2,1,0:T(8,128)(2,1)S(1)}, bf16[2,64,1536]{2,1,0:T(8,128)(2,1)S(1)}, u32[]{:S(2)}, u32[]{:S(2)}) collective-permute-start(bf16[2,64,1536]{2,1,0:T(8,128)(2,1)S(1)} %fusion.63), channel_id=1, source_target_pairs={{0,8},{8,0},{1,9},{9,1},{2,10},{10,2},{3,11},{11,3},{4,12},{12,4},... | collective-permute-start | bytes 1179656 | tf_op jit(solution)/shard_map/ppermute | solution.py:264
  596.1 36.5 %collective-permute-start.58 = (bf16[64,1536]{1,0:T(8,128)(2,1)S(1)}, bf16[64,1536]{1,0:T(8,128)(2,1)S(1)}, u32[]{:S(2)}, u32[]{:S(2)}) collective-permute-start(bf16[64,1536]{1,0:T(8,128)(2,1)S(1)} %fusion.85), channel_id=1, source_target_pairs={{0,4},{4,0},{1,5},{5,1},{2,6},{6,2},{3,7},{7,3},{8,12},{12,8},{9,1... | collective-permute-start | bytes 589832 | tf_op jit(solution)/shard_map/ppermute | solution.py:264
  722.4 97.3 %collective-permute-start.79 = (bf16[2,2,2,2,48,1536]{5,4,0,1,2,3:T(8,128)(2,1)}, bf16[2,2,2,2,48,1536]{5,4,0,1,2,3:T(8,128)(2,1)}, u32[]{:S(2)}, u32[]{:S(2)}) collective-permute-start(bf16[2,2,2,2,48,1536]{5,4,0,1,2,3:T(8,128)(2,1)} %bitcast.457), channel_id=1, source_target_pairs={{0,2},{2,0},{1,3},{3,1},{4,6},{6,4},{5,7},{7,5},{8,10},{10,8},{9,1... | collective-permute-start | bytes 7077896 | tf_op jit(solution)/shard_map/ppermute | solution.py:264
  766.5 49.5 %collective-permute-start.84 = (bf16[2,2,2,2,48,512]{5,4,0,1,2,3:T(8,128)(2,1)}, bf16[2,2,2,2,48,512]{5,4,0,1,2,3:T(8,128)(2,1)}, u32[]{:S(2)}, u32[]{:S(2)}) collective-permute-start(bf16[2,2,2,2,48,512]{5,4,0,1,2,3:T(8,128)(2,1)} %bitcast.460), channel_id=1, source_target_pairs={{0,2},{2,0},{1,3},{3,1},{4,6},{6,4},{5,7},{7,5},{8,10},{10,8},{9,1... | collective-permute-start | bytes 2359304 | tf_op jit(solution)/shard_map/ppermute | solution.py:264
  773.0 62.4 %collective-permute-start.89 = (bf16[2,2,2,2,48,1536]{5,4,0,1,2,3:T(8,128)(2,1)}, bf16[2,2,2,2,48,1536]{5,4,0,1,2,3:T(8,128)(2,1)}, u32[]{:S(2)}, u32[]{:S(2)}) collective-permute-start(bf16[2,2,2,2,48,1536]{5,4,0,1,2,3:T(8,128)(2,1)} %bitcast.456), channel_id=1, source_target_pairs={{0,2},{2,0},{1,3},{3,1},{4,6},{6,4},{5,7},{7,5},{8,10},{10,8},{9,1... | collective-permute-start | bytes 7077896 | tf_op jit(solution)/shard_map/ppermute | solution.py:264
  840.8 39.4 %collective-permute-start.90 = (bf16[2,2,2,48,1536]{4,3,0,1,2:T(8,128)(2,1)S(1)}, bf16[2,2,2,48,1536]{4,3,0,1,2:T(8,128)(2,1)S(1)}, u32[]{:S(2)}, u32[]{:S(2)}) collective-permute-start(bf16[2,2,2,48,1536]{4,3,0,1,2:T(8,128)(2,1)S(1)} %dynamic-slice_bitcast_fusion), channel_id=1, source_target_pairs={{0,1},{1,0},{2,3},{3,2},{4,5},{5,4},{6,7},{7,6},{8,9},{9,8},{10,11... | collective-permute-start | bytes 3538952 | tf_op jit(solution)/shard_map/ppermute | solution.py:264
  (210 other events, 2716.1 us)
Sparse Core Ops, SparseCore 0:
  67.8 105.8 all-gather.3
  175.6 98.4 all-gather.5
  275.9 73.7 all-gather.7
  497.6 77.9 reduce-scatter.5
  578.6 75.7 reduce-scatter.3
  657.2 94.4 reduce-scatter.7

commit v2 on v1

v2 whole, which is shorter than its diff:
```python
import functools

import jax
import jax.numpy as jnp
from jax import lax
from jax.experimental import pallas as pl
from jax.experimental.pallas import tpu as pltpu
from jax.sharding import Mesh, PartitionSpec as P

QUERY_HEADS = 12
KEY_VALUE_HEADS = 2
HEAD_WIDTH = 128
EPSILON = 1e-06
THETA = 10000.0
GROUP = QUERY_HEADS // KEY_VALUE_HEADS
SCALE = HEAD_WIDTH ** (-0.5)
F32 = jnp.float32
BF16 = jnp.bfloat16
SWAP = [(0, 1), (1, 0)]


def locate(item_lengths, positions_at):
    ends = jnp.cumsum(item_lengths)
    starts = ends - item_lengths
    segment_ids = jnp.sum((ends[None, :] <= positions_at[:, None]).astype(jnp.int32), axis=1)
    onehot = segment_ids[:, None] == jnp.arange(item_lengths.shape[0], dtype=jnp.int32)[None, :]
    first = jnp.sum(jnp.where(onehot, starts[None, :], 0), axis=1)
    return (positions_at - first, first)


def rotary_tables(offsets, head_size):
    freqs = 1.0 / THETA ** (jnp.arange(0, head_size, 2, dtype=F32) / head_size)
    angles = offsets.astype(F32)[:, None] * freqs[None, :]
    cosine, sine = jnp.cos(angles), jnp.sin(angles)
    return (jnp.concatenate([cosine, cosine], axis=1), jnp.concatenate([sine, sine], axis=1))


def apply_rotary(values, cosine_table, sine_table):
    half = values.shape[-1] // 2
    turned = jnp.concatenate([-values[..., half:], values[..., :half]], axis=-1)
    return values * cosine_table[:, None, :] + turned * sine_table[:, None, :]


def inverse_rotary(grads, cosine_table, sine_table):
    half = grads.shape[-1] // 2
    scaled = grads * sine_table[:, None, :]
    turned = jnp.concatenate([scaled[..., half:], -scaled[..., :half]], axis=-1)
    return grads * cosine_table[:, None, :] + turned


def rms_forward(rows, gain):
    recip = lax.rsqrt(jnp.mean(rows * rows, axis=-1, keepdims=True) + EPSILON)
    return (rows * recip * gain, recip)


def rms_backward(rows, recip, gain, upstream):
    weighted = upstream * gain
    grad_rows = recip * weighted - rows * (recip * recip * recip) * jnp.mean(
        rows * weighted, axis=-1, keepdims=True
    )
    gain_grad = jnp.sum(upstream * rows * recip, axis=0)
    return (grad_rows, gain_grad)


def dot(left, right, dims, out=F32):
    return lax.dot_general(left, right, ((dims[0], dims[1]), ((), ())), preferred_element_type=out)


def rows_dot(left, right):
    return dot(left, right, ((0,), (0,)))


def cols_dot(left, right):
    return dot(left, right, ((1,), (1,)))


def mat_dot(left, right):
    return dot(left, right, ((1,), (0,)))


def attend_forward_kernel(meta, q_ref, k_ref, v_ref, span_ref, o_ref, lse_ref):
    rows = q_ref.shape[0]
    queries = jnp.concatenate(
        [q_ref[:, h * HEAD_WIDTH : (h + 1) * HEAD_WIDTH] for h in range(GROUP)], axis=0
    )
    first, last = span_ref[0:1, :], span_ref[1:2, :]
    wide = GROUP * rows
    local = lax.broadcasted_iota(jnp.int32, (rows, 1), 0)

    def step(block, carry):
        top, total, accum = carry
        keys, values = k_ref[block], v_ref[block]
        scores = dot(keys, queries, ((1,), (1,))) * SCALE
        index = block * rows + local
        scores = jnp.where((index >= first) & (index <= last), scores, -1e30)
        new_top = jnp.maximum(top, jnp.max(scores, axis=0, keepdims=True))
        fade = jnp.exp(top - new_top)
        probs = jnp.exp(scores - new_top)
        total = total * fade + jnp.sum(probs, axis=0, keepdims=True)
        accum = accum * fade + dot(values, probs.astype(BF16), ((0,), (0,)))
        return (new_top, total, accum)

    top, total, accum = lax.fori_loop(
        meta[0],
        meta[1] + 1,
        step,
        (
            jnp.full((1, wide), -1e30, F32),
            jnp.zeros((1, wide), F32),
            jnp.zeros((HEAD_WIDTH, wide), F32),
        ),
    )
    attended = (accum / total).T.astype(BF16)
    for h in range(GROUP):
        o_ref[:, h * HEAD_WIDTH : (h + 1) * HEAD_WIDTH] = attended[h * rows : (h + 1) * rows]
    lse_ref[0] = top + jnp.log(total)


def attend_forward(meta, queries, stack, span):
    pieces, rows, _ = stack.shape
    width = queries.shape[1]
    part = width // KEY_VALUE_HEADS
    spec = pltpu.PrefetchScalarGridSpec(
        num_scalar_prefetch=1,
        grid=(KEY_VALUE_HEADS,),
        in_specs=[
            pl.BlockSpec((rows, part), lambda g, m: (0, g)),
            pl.BlockSpec((pieces, rows, HEAD_WIDTH), lambda g, m: (0, 0, g)),
            pl.BlockSpec((pieces, rows, HEAD_WIDTH), lambda g, m: (0, 0, KEY_VALUE_HEADS + g)),
            pl.BlockSpec((8, GROUP * rows), lambda g, m: (0, 0)),
        ],
        out_specs=[
            pl.BlockSpec((rows, part), lambda g, m: (0, g)),
            pl.BlockSpec((1, 1, GROUP * rows), lambda g, m: (g, 0, 0)),
        ],
    )
    return pl.pallas_call(
        attend_forward_kernel,
        grid_spec=spec,
        out_shape=(
            jax.ShapeDtypeStruct((rows, width), BF16),
            jax.ShapeDtypeStruct((KEY_VALUE_HEADS, 1, GROUP * rows), F32),
        ),
        cost_estimate=pl.CostEstimate(
            flops=4 * rows * rows * 6 * width, bytes_accessed=stack.size * 2, transcendentals=0
        ),
        name="attend_forward",
    )(meta, queries, stack, stack, span)


def attend_backward_kernel(
    meta, q_ref, do_ref, k_ref, v_ref, span_ref, lse_ref, dq_ref, dk_ref, dv_ref, p_ref, dp_ref
):
    rows = q_ref.shape[0]
    wide = GROUP * rows
    cols = [slice(h * HEAD_WIDTH, (h + 1) * HEAD_WIDTH) for h in range(GROUP)]
    queries = jnp.concatenate([q_ref[:, c] for c in cols], axis=0)
    grads = jnp.concatenate([do_ref[:, c] for c in cols], axis=0)
    first, last = span_ref[0:1, :], span_ref[1:2, :]
    lse = lse_ref[0]
    local = lax.broadcasted_iota(jnp.int32, (rows, 1), 0)
    low = meta[0]
    dk_ref[...] = jnp.zeros_like(dk_ref)
    dv_ref[...] = jnp.zeros_like(dv_ref)

    def collect(block, delta):
        scores = dot(k_ref[block], queries, ((1,), (1,))) * SCALE
        index = block * rows + local
        probs = jnp.where((index >= first) & (index <= last), jnp.exp(scores - lse), 0.0)
        grad_probs = dot(v_ref[block], grads, ((1,), (1,)))
        p_ref[block - low] = probs
        dp_ref[block - low] = grad_probs
        return delta + jnp.sum(probs * grad_probs, axis=0, keepdims=True)

    delta = lax.fori_loop(low, meta[1] + 1, collect, jnp.zeros((1, wide), F32))

    def spread(block, accum):
        probs = p_ref[block - low]
        grad_scores = (probs * (dp_ref[block - low] - delta)).astype(BF16)
        dk_ref[block] = (mat_dot(grad_scores, queries) * SCALE).astype(BF16)
        dv_ref[block] = mat_dot(probs.astype(BF16), grads).astype(BF16)
        return accum + dot(k_ref[block], grad_scores, ((0,), (0,)))

    accum = lax.fori_loop(low, meta[1] + 1, spread, jnp.zeros((HEAD_WIDTH, wide), F32))
    grad_queries = (accum * SCALE).T
    for h in range(GROUP):
        dq_ref[:, cols[h]] = grad_queries[h * rows : (h + 1) * rows]


def attend_backward(meta, queries, grads, stack, span, lse):
    pieces, rows, _ = stack.shape
    width = queries.shape[1]
    part = width // KEY_VALUE_HEADS
    most = pieces // 2 + 1
    head = (pieces, rows, HEAD_WIDTH)
    spec = pltpu.PrefetchScalarGridSpec(
        num_scalar_prefetch=1,
        grid=(KEY_VALUE_HEADS,),
        in_specs=[
            pl.BlockSpec((rows, part), lambda g, m: (0, g)),
            pl.BlockSpec((rows, part), lambda g, m: (0, g)),
            pl.BlockSpec(head, lambda g, m: (0, 0, g)),
            pl.BlockSpec(head, lambda g, m: (0, 0, KEY_VALUE_HEADS + g)),
            pl.BlockSpec((8, GROUP * rows), lambda g, m: (0, 0)),
            pl.BlockSpec((1, 1, GROUP * rows), lambda g, m: (g, 0, 0)),
        ],
        out_specs=[
            pl.BlockSpec((rows, part), lambda g, m: (0, g)),
            pl.BlockSpec(head, lambda g, m: (0, 0, g)),
            pl.BlockSpec(head, lambda g, m: (0, 0, g)),
        ],
        scratch_shapes=[
            pltpu.VMEM((most, rows, GROUP * rows), F32),
            pltpu.VMEM((most, rows, GROUP * rows), F32),
        ],
    )
    kv_shape = jax.ShapeDtypeStruct((pieces, rows, KEY_VALUE_HEADS * HEAD_WIDTH), BF16)
    return pl.pallas_call(
        attend_backward_kernel,
        grid_spec=spec,
        out_shape=(jax.ShapeDtypeStruct((rows, width), F32), kv_shape, kv_shape),
        cost_estimate=pl.CostEstimate(
            flops=10 * rows * rows * 6 * width, bytes_accessed=stack.size * 4, transcendentals=0
        ),
        name="attend_backward",
    )(meta, queries, grads, stack, stack, span, lse)


MESH = pl.DeviceIdType.MESH
ANY = pl.BlockSpec(memory_space=pl.ANY)


class Copies:
    def __init__(self, send_sems, recv_sems):
        self.send_sems, self.recv_sems, self.started = send_sems, recv_sems, []

    def start(self, source, target, device):
        number = len(self.started)
        copy = pltpu.make_async_remote_copy(
            src_ref=source,
            dst_ref=target,
            send_sem=self.send_sems.at[number],
            recv_sem=self.recv_sems.at[number],
            device_id=device,
            device_id_type=MESH,
        )
        copy.start()
        self.started.append(copy)
        return copy


def greet(devices):
    barrier = pltpu.get_barrier_semaphore()
    for device in devices:
        pl.semaphore_signal(barrier, inc=1, device_id=device, device_id_type=MESH)
    pl.semaphore_wait(barrier, len(devices))


def other_h(far, k):
    return {"h": lax.rem(lax.axis_index("h") + k, far)}


def flip(*axes):
    return {axis: 1 - lax.axis_index(axis) for axis in axes}


def gather_steps(kind, far, copies, source, out, local):
    ih, ip, iy, ic, ix = (lax.axis_index(name) for name in ("h", "p", "y", "c", "x"))
    every = kind == "all"

    def block(h, p, y=iy, x=ix):
        return out.at[h, p, y, ic, x] if every else out.at[h, p, y, ic]

    local.start()
    pieces = [(lax.rem(ih - k + far, far), p) for p in (ip, 1 - ip) for k in range(far)]
    count = len(pieces)
    arrivals, plane, cross, core = [None] * count, [None] * count, [None] * count, [None] * count
    columns = source.shape[-1]
    half = columns // 2 if columns % 256 == 0 else columns

    def cut(ref, first):
        if half == columns:
            return ref
        return ref.at[:, pl.ds(0 if first else half, half)]

    for k in range(1, far):
        arrivals[k] = copies.start(source, block(ih, ip), other_h(far, k))
    for step in range(count + 3):
        if step < count:
            if arrivals[step] is not None:
                arrivals[step].wait_recv()
            h, p = pieces[step]
            held = source if step == 0 else block(h, p)
            if step < far:
                arrivals[far + step] = copies.start(held, block(h, p), flip("p"))
            plane[step] = [copies.start(held, block(h, p), flip("y"))]
            if every:
                plane[step].append(copies.start(held, block(h, p), flip("x")))
        if 0 <= step - 1 < count:
            h, p = pieces[step - 1]
            for copy in plane[step - 1]:
                copy.wait_recv()
            cross[step - 1] = []
            if every:
                ref = cut(block(h, p, x=1 - ix), True)
                cross[step - 1].append(copies.start(ref, ref, flip("y")))
                if half < columns:
                    ref = cut(block(h, p, y=1 - iy), False)
                    cross[step - 1].append(copies.start(ref, ref, flip("x")))
        if 0 <= step - 2 < count:
            h, p = pieces[step - 2]
            for copy in cross[step - 2]:
                copy.wait_recv()
            if step == 2:
                local.wait()
            ref = out.at[h, p, :, ic]
            core[step - 2] = copies.start(ref, ref, flip("c"))
        if 0 <= step - 3 < count:
            core[step - 3].wait_recv()
        yield


def group_steps(far, copies, source, out, local):
    ip, iy, ic = (lax.axis_index(name) for name in ("p", "y", "c"))
    half = source.shape[0] // 2
    top, low = pl.ds(0, half), pl.ds(half, half)

    def rows(p, y, part):
        return out.at[p, y, ic, part]

    def forward(ref, axis):
        return copies.start(ref, ref, flip(axis))

    local.start()
    first = [
        copies.start(source.at[top], rows(ip, iy, top), flip("y")),
        copies.start(source.at[low], rows(ip, iy, low), flip("p")),
    ]
    second = [
        copies.start(source.at[top], rows(ip, iy, top), flip("p")),
        copies.start(source.at[low], rows(ip, iy, low), flip("y")),
    ]
    core = [copies.start(source, out.at[ip, iy, ic], flip("c"))]
    yield
    first[0].wait_recv()
    second.append(forward(rows(ip, 1 - iy, top), "p"))
    core.append(forward(rows(ip, 1 - iy, top), "c"))
    first[1].wait_recv()
    second.append(forward(rows(1 - ip, iy, low), "y"))
    core.append(forward(rows(1 - ip, iy, low), "c"))
    yield
    for copy, p, y, part in (
        (second[0], 1 - ip, iy, top),
        (second[1], ip, 1 - iy, low),
        (second[2], 1 - ip, 1 - iy, top),
        (second[3], 1 - ip, 1 - iy, low),
    ):
        copy.wait_recv()
        core.append(forward(rows(p, y, part), "c"))
    yield
    for copy in core:
        copy.wait_recv()
    local.wait()


def pair_steps(far, copies, source, out, local, place):
    ih, ix = lax.axis_index("h"), lax.axis_index("x")
    local.start()
    arrived = [copies.start(source, place(ih, ix), other_h(far, k)) for k in range(1, far)]
    sent = [copies.start(source, place(ih, ix), flip("x"))]
    yield
    for k in range(1, far):
        arrived[k - 1].wait_recv()
        ref = place(lax.rem(ih - k + far, far), ix)
        sent.append(copies.start(ref, ref, flip("x")))
        yield
    for _ in range(far + 1):
        yield
    for copy in sent:
        copy.wait_recv()
    local.wait()


def spread_steps(far, copies, source, out, local):
    ip, iy, ic = (lax.axis_index(name) for name in ("p", "y", "c"))
    me = (ip * 2 + iy) * 2 + ic
    local.start()
    started = []
    for j in (1, 2, 4, 3, 5, 6, 7):
        p = 1 - ip if j & 4 else ip
        y = 1 - iy if j & 2 else iy
        c = 1 - ic if j & 1 else ic
        started.append(
            copies.start(source.at[(p * 2 + y) * 2 + c], out.at[me], {"p": p, "y": y, "c": c})
        )
    for _ in range(2 * far + 2):
        yield
    for copy in started:
        copy.wait_recv()
    local.wait()
    yield


def move_kernel(kinds, far, *refs):
    count = len(kinds)
    sources, outs = refs[:count], refs[count : 2 * count]
    send_sems, recv_sems, local_sems = refs[2 * count :]
    ih, ip, iy, ic, ix = (lax.axis_index(name) for name in ("h", "p", "y", "c", "x"))
    partners = [flip("p"), flip("y"), flip("c")]
    if set(kinds) - {"spread", "group"}:
        partners += [other_h(far, k) for k in range(1, far)]
    if "all" in kinds or "pair" in kinds or "pair8" in kinds:
        partners.append(flip("x"))
    if "spread" in kinds:
        partners += [flip("p", "y"), flip("p", "c"), flip("y", "c"), flip("p", "y", "c")]
    greet(partners)
    copies = Copies(send_sems, recv_sems)
    running = []
    for i, kind in enumerate(kinds):
        if kind == "spread":
            me = (ip * 2 + iy) * 2 + ic
            local = pltpu.make_async_copy(sources[i].at[me], outs[i].at[me], local_sems.at[i])
            running.append(spread_steps(far, copies, sources[i], outs[i], local))
        elif kind == "group":
            place = outs[i].at[ip, iy, ic]
            local = pltpu.make_async_copy(sources[i], place, local_sems.at[i])
            running.append(group_steps(far, copies, sources[i], outs[i], local))
        elif kind in ("pair", "pair8"):

            def place(h, x, out=outs[i], wide=kind == "pair8"):
                return out.at[h, :, x] if wide else out.at[h, x]

            local = pltpu.make_async_copy(sources[i], place(ih, ix), local_sems.at[i])
            running.append(pair_steps(far, copies, sources[i], outs[i], local, place))
        else:
            place = (ih, ip, iy, ic, ix) if kind == "all" else (ih, ip, iy, ic)
            local = pltpu.make_async_copy(sources[i], outs[i].at[place], local_sems.at[i])
            running.append(gather_steps(kind, far, copies, sources[i], outs[i], local))
    while running:
        running = [job for job in running if next(job, "end") != "end"]
    for copy in copies.started:
        copy.wait_send()


def move(name, number, far, fsdp, kinds, arrays):
    shapes, total = [], 0
    pieces = 2 * far
    for kind, array in zip(kinds, arrays):
        if kind == "all":
            lead, total = (far, 2, 2, 2, fsdp), total + (far - 1) + far + 5 * pieces
        elif kind == "seq":
            lead, total = (far, 2, 2, 2), total + (far - 1) + far + 2 * pieces
        elif kind == "group":
            lead, total = (2, 2, 2), total + 13
        elif kind == "pair":
            lead, total = (far, fsdp), total + 2 * far - 1
        elif kind == "pair8":
            lead, total = (far, 8, fsdp), total + 2 * far - 1
        else:
            lead, total = (), total + 7
        tail = array.shape[1:] if kind == "pair8" else array.shape
        shapes.append(jax.ShapeDtypeStruct(lead + tail, array.dtype))
    size = sum(s.size * s.dtype.itemsize for s in shapes)
    return pl.pallas_call(
        functools.partial(move_kernel, kinds, far),
        out_shape=tuple(shapes),
        in_specs=[ANY] * len(arrays),
        out_specs=tuple([ANY] * len(arrays)),
        scratch_shapes=[
            pltpu.SemaphoreType.DMA((total,)),
            pltpu.SemaphoreType.DMA((total,)),
            pltpu.SemaphoreType.DMA((len(arrays),)),
        ],
        compiler_params=pltpu.CompilerParams(collective_id=number, has_side_effects=True),
        cost_estimate=pl.CostEstimate(flops=0, bytes_accessed=8 * size, transcendentals=0),
        name=name,
    )(*arrays)


def reduce_plan(kind, far, fsdp, tail):
    rows, columns = tail
    if kind == "group":
        half = rows // 2
        return ("p", "y"), [
            ((pl.ds(0, half), slice(None)), (half, columns), ("p", "y")),
            ((pl.ds(half, half), slice(None)), (half, columns), ("y", "p")),
        ]
    if kind == "seq":
        return ("h", "p", "y"), [((slice(None), slice(None)), tail, ("y", "p", "h"))]
    names = ("h", "p", "y", "x")
    if columns % 256:
        return names, [((slice(None), slice(None)), tail, ("x", "y", "p", "h"))]
    half = columns // 2
    return names, [
        ((slice(None), pl.ds(0, half)), (rows, half), ("x", "y", "p", "h")),
        ((slice(None), pl.ds(half, half)), (rows, half), ("y", "x", "p", "h")),
    ]


def reduce_shapes(kind, far, fsdp, tail, dtype):
    length = {"h": far, "p": 2, "y": 2, "x": fsdp}
    names, parts = reduce_plan(kind, far, fsdp, tail)
    shapes = []
    for _, small, order in parts:
        left = list(names)
        full = tuple(length[n] for n in left) + small
        shapes += [full, full]
        for axis in order:
            left.remove(axis)
            lead = tuple(length[n] for n in left) + small
            shapes.append((far - 1,) + lead if axis == "h" else lead)
    return shapes


def reduce_steps(kind, far, fsdp, copies, source, out, scratch, local_sem):
    place = {name: lax.axis_index(name) for name in ("h", "p", "y", "x")}
    ic = lax.axis_index("c")
    length = {"h": far, "p": 2, "y": 2, "x": fsdp}
    core_dim = {"group": 2, "seq": 3, "all": 3}[kind]
    names, parts = reduce_plan(kind, far, fsdp, out.shape)
    jobs, position = [], 0
    for cut, small, order in parts:
        count = 2 + len(order)
        jobs.append((cut, small, order, scratch[position : position + count]))
        position += count

    def view(c, cut):
        lead = [slice(None)] * core_dim + [c] + [slice(None)] * (len(names) - core_dim)
        return source.at[tuple(lead) + cut]

    def add(sums, brought, fixed, left, target=None, also=()):
        sizes = [1 if n in fixed_now else length[n] for n in left for fixed_now in (also,)]
        total = 1
        for size in sizes:
            total *= size

        def one(number, _):
            index, rest = {}, number
            for n, size in reversed(list(zip(left, sizes))):
                index[n] = also[n] if n in also else rest % size
                rest = rest // size
            whole = tuple(fixed[n] if n in fixed else index[n] for n in names)
            value = sums[whole].astype(F32) + brought[tuple(index[n] for n in left)].astype(F32)
            if target is None:
                sums[whole] = value.astype(sums.dtype)
            else:
                target(value)
            return 0

        if total == 1:
            one(0, 0)
        else:
            lax.fori_loop(0, total, one, 0)

    loads, sent = [], []
    for i, (cut, small, order, refs) in enumerate(jobs):
        loads.append(pltpu.make_async_copy(view(ic, cut), refs[0], local_sem.at[i]))
        loads[i].start()
        sent.append(copies.start(view(1 - ic, cut), refs[1], flip("c")))
    yield
    for stage in range(len(jobs[0][2]) + 1):
        for i, (cut, small, order, refs) in enumerate(jobs):
            sums, brought = refs[0], refs[1 + stage]
            done = order[:stage]
            left = tuple(n for n in names if n not in done)
            fixed = {n: place[n] for n in done}
            if stage == 0:
                loads[i].wait()
            if stage > 0 and order[stage - 1] == "h":
                for copy in sent[i]:
                    copy.wait_recv()
            else:
                sent[i].wait_recv()
            if stage == len(order):
                if order[-1] == "h":
                    whole = tuple(place[n] for n in names)
                    value = sums[whole].astype(F32)
                    for k in range(far - 1):
                        value = value + brought[k].astype(F32)
                    out[cut] = value
                else:

                    def put(value, cut=cut):
                        out[cut] = value

                    add(sums, brought, fixed, left, put)
                continue
            axis = order[stage]
            if axis == "h":
                add(sums, brought, fixed, left)
                sent[i] = []
                for k in range(1, far):
                    goal = lax.rem(place["h"] + k, far)
                    whole = tuple(goal if n == "h" else place[n] for n in names)
                    sent[i].append(
                        copies.start(sums.at[whole], refs[2 + stage].at[k - 1], other_h(far, k))
                    )
            else:
                add(sums, brought, fixed, left, also={axis: 1 - place[axis]})
                index = tuple(
                    1 - place[n] if n == axis else fixed.get(n, slice(None)) for n in names
                )
                sent[i] = copies.start(sums.at[index], refs[2 + stage], flip(axis))
                add(sums, brought, fixed, left, also={axis: place[axis]})
        yield


def reduce_kernel(kinds, far, fsdp, counts, *refs):
    n = len(kinds)
    sources, outs = refs[:n], refs[n : 2 * n]
    scratch = refs[2 * n : -3]
    send_sems, recv_sems, local_sems = refs[-3:]
    partners = [flip("p"), flip("y"), flip("c")]
    if set(kinds) - {"group"}:
        partners += [other_h(far, k) for k in range(1, far)]
    if "all" in kinds:
        partners.append(flip("x"))
    greet(partners)
    copies = Copies(send_sems, recv_sems)
    running, position = [], 0
    for i, kind in enumerate(kinds):
        part = scratch[position : position + counts[i]]
        position += counts[i]
        running.append(
            reduce_steps(
                kind, far, fsdp, copies, sources[i], outs[i], part, local_sems.at[i]
            )
        )
    while running:
        running = [job for job in running if next(job, "end") != "end"]
    for copy in copies.started:
        copy.wait_send()


def reduce(name, number, far, fsdp, kinds, arrays):
    shapes, scratch, counts, total = [], [], [], 0
    for kind, array in zip(kinds, arrays):
        tail = array.shape[-2:]
        parts = reduce_plan(kind, far, fsdp, tail)[1]
        own = reduce_shapes(kind, far, fsdp, tail, array.dtype)
        counts.append(len(own))
        scratch += [pltpu.VMEM(shape, array.dtype) for shape in own]
        shapes.append(jax.ShapeDtypeStruct(tail, F32))
        total += sum(1 + len(order) + (far - 2 if "h" in order else 0) for _, _, order in parts)
    size = sum(a.size * a.dtype.itemsize for a in arrays)
    return pl.pallas_call(
        functools.partial(reduce_kernel, kinds, far, fsdp, tuple(counts)),
        out_shape=tuple(shapes),
        in_specs=[ANY] * len(arrays),
        out_specs=tuple([pl.BlockSpec(memory_space=pltpu.VMEM)] * len(arrays)),
        scratch_shapes=scratch
        + [
            pltpu.SemaphoreType.DMA((total,)),
            pltpu.SemaphoreType.DMA((total,)),
            pltpu.SemaphoreType.DMA((len(arrays), 2)),
        ],
        compiler_params=pltpu.CompilerParams(collective_id=number, has_side_effects=True),
        cost_estimate=pl.CostEstimate(flops=0, bytes_accessed=8 * size, transcendentals=0),
        name=name,
    )(*arrays)


def body(
    sizes,
    inputs,
    lengths,
    attn_gain,
    query_weight,
    query_bias,
    key_matrix,
    key_bias_vector,
    value_matrix,
    value_bias_vector,
    output_weight,
    mlp_gain,
    gate_weight,
    up_weight,
    down_weight,
    cotangent,
):
    far, fsdp = sizes
    micro, token_rows, width = inputs.shape[1:]
    shard = query_weight.shape[0]
    kv_width = key_matrix.shape[1]
    hidden_width = gate_weight.shape[1]
    devices = far * 8 * fsdp
    seq = far * 8
    ih, ip, iy, ic, ix = (lax.axis_index(name) for name in ("h", "p", "y", "c", "x"))
    me8 = (ip * 2 + iy) * 2 + ic
    me_seq = ih * 8 + me8

    def hop(array, axis, shift=1):
        if axis == "h":
            return lax.ppermute(array, "h", [(i, (i + shift) % far) for i in range(far)])
        return lax.ppermute(array, axis, SWAP)

    def pick(array, index, axis):
        return lax.dynamic_index_in_dim(array, index, axis, keepdims=False)

    slice_width = hidden_width // 8

    def slices(matrix):
        parts = matrix.reshape(shard, far, 8, hidden_width // (8 * far))
        return parts.transpose(2, 0, 1, 3).reshape(8, shard, slice_width)

    vectors = jnp.concatenate(
        [attn_gain, query_bias, key_bias_vector, value_bias_vector, mlp_gain]
    ).astype(F32)
    vectors = jnp.pad(vectors, (0, 1024 - vectors.shape[0])).reshape(8, 128)
    w_qkv, vectors, gate_parts, up_parts, w_down = move(
        "gather_first",
        0,
        far,
        fsdp,
        ("all", "all", "spread", "spread", "pair"),
        (
            jnp.concatenate([key_matrix, value_matrix, query_weight], axis=1),
            vectors,
            slices(gate_weight),
            slices(up_weight),
            down_weight,
        ),
    )
    w_down = w_down.reshape(slice_width, width)
    w_qkv = w_qkv.reshape(width, -1)
    vectors = vectors.reshape(devices, 1024)
    cuts = [0]
    for part in (attn_gain, query_bias, key_bias_vector, value_bias_vector, mlp_gain):
        cuts.append(cuts[-1] + part.shape[0])
    gain_attn, b_query, b_key, b_value, gain_mlp = (
        vectors[:, cuts[i] : cuts[i + 1]].reshape(-1) for i in range(5)
    )
    rows = inputs[0].astype(F32).reshape(micro * token_rows, width)
    upstream_low = cotangent[0].reshape(micro * token_rows, width)
    positions_at = me_seq * token_rows + jnp.arange(token_rows, dtype=jnp.int32)
    tables, spans, metas = [], [], []
    for number in range(micro):
        offsets, first = locate(lengths[0, number], positions_at)
        tables.append(rotary_tables(offsets, HEAD_WIDTH))
        spans.append(
            jnp.concatenate(
                [
                    jnp.tile(first, GROUP)[None],
                    jnp.tile(positions_at, GROUP)[None],
                    jnp.zeros((6, GROUP * token_rows), jnp.int32),
                ],
                axis=0,
            )
        )
        low = jnp.maximum(first[0] // token_rows, me_seq - seq // 2)
        metas.append(jnp.stack([low, me_seq]).astype(jnp.int32))
    cosine_table = jnp.concatenate([t[0] for t in tables], axis=0)
    sine_table = jnp.concatenate([t[1] for t in tables], axis=0)

    normed, recip_one = rms_forward(rows, gain_attn)
    normed_low = normed.astype(BF16)
    pre = mat_dot(normed_low, w_qkv)
    kv_pre = pre[:, : 2 * kv_width]
    key_rotated = apply_rotary(
        (kv_pre[:, :kv_width] + b_key).reshape(-1, KEY_VALUE_HEADS, HEAD_WIDTH),
        cosine_table,
        sine_table,
    ).reshape(-1, kv_width)
    own_kv = jnp.concatenate([key_rotated, kv_pre[:, kv_width:] + b_value], axis=1).astype(BF16)
    moved = move(
        "gather_second",
        1,
        far,
        fsdp,
        ("seq",) * micro + ("all", "pair8", "pair8", "group"),
        tuple(own_kv[m * token_rows : (m + 1) * token_rows] for m in range(micro))
        + (output_weight, gate_parts, up_parts, upstream_low),
    )
    stacks = [part.reshape(seq, token_rows, 2 * kv_width) for part in moved[:micro]]
    w_output = moved[micro].reshape(width, width)
    w_gate, w_up = (part.reshape(width, slice_width) for part in moved[micro + 1 : micro + 3])
    upstream_all = moved[micro + 3].reshape(-1, width)
    query_rotated = (
        apply_rotary(
            (pre[:, 2 * kv_width :] + b_query).reshape(-1, QUERY_HEADS, HEAD_WIDTH),
            cosine_table,
            sine_table,
        )
        .astype(BF16)
        .reshape(-1, width)
    )

    attended, lses = [], []
    for m in range(micro):
        part = slice(m * token_rows, (m + 1) * token_rows)
        result, lse = attend_forward(metas[m], query_rotated[part], stacks[m], spans[m])
        attended.append(result)
        lses.append(lse)
    attended = jnp.concatenate(attended, axis=0)
    middle = rows + mat_dot(attended, w_output)
    normed_two, recip_two = rms_forward(middle, gain_mlp)
    (tokens,) = move("gather_tokens", 2, far, fsdp, ("group",), (normed_two.astype(BF16),))
    tokens = tokens.reshape(-1, width)

    gate_pre = mat_dot(tokens, w_gate)
    up_pre = mat_dot(tokens, w_up)
    sigma = jax.nn.sigmoid(gate_pre)
    activated = gate_pre * sigma
    hidden = (activated * up_pre).astype(BF16)
    grad_hidden = cols_dot(upstream_all, w_down)
    grad_gate = (grad_hidden * up_pre * sigma * (1.0 + gate_pre * (1.0 - sigma))).astype(BF16)
    grad_up = (grad_hidden * activated).astype(BF16)
    group = (2, 2, 2, micro * token_rows, width)
    grad_two = (cols_dot(grad_gate, w_gate) + cols_dot(grad_up, w_up)).astype(BF16)
    final = mat_dot(hidden, w_down).astype(BF16)

    def paired(grad, axis):
        grad = grad.astype(BF16)
        kept = pick(grad, ix, axis).astype(F32) + hop(pick(grad, 1 - ix, axis), "x").astype(F32)
        kept = kept.astype(BF16)
        total = pick(kept, ih, 0).astype(F32)
        for k in range(1, far):
            total = total + hop(pick(kept, (ih + k) % far, 0), "h", k).astype(F32)
        return total

    eight = (far, 8, fsdp, shard, slice_width)
    gate_sum = paired(rows_dot(tokens, grad_gate).reshape(eight), 2).astype(BF16)
    up_sum = paired(rows_dot(tokens, grad_up).reshape(eight), 2).astype(BF16)
    down_part = paired(rows_dot(hidden, upstream_all).reshape(far, fsdp, -1, width), 1)

    (grad_two,) = reduce("reduce_tokens", 3, far, fsdp, ("group",), (grad_two.reshape(group),))
    grad_norm, gain_mlp_sum = rms_backward(middle, recip_two, gain_mlp, grad_two)
    grad_middle = upstream_low.astype(F32) + grad_norm
    grad_branch = grad_middle.astype(BF16)
    grad_attended = cols_dot(grad_branch, w_output).astype(BF16)
    grad_kvs, grad_query = [], []
    for m in range(micro):
        part = slice(m * token_rows, (m + 1) * token_rows)
        query_part, grad_keys, grad_values = attend_backward(
            metas[m], query_rotated[part], grad_attended[part], stacks[m], spans[m], lses[m]
        )
        stacked = jnp.concatenate([grad_keys, grad_values], axis=2)
        grad_kvs.append(stacked.reshape(far, 2, 2, 2, token_rows, 2 * kv_width))
        grad_query.append(query_part)

    blocks = (far, 2, 2, 2, fsdp, shard)
    g_output = rows_dot(attended, grad_branch).astype(BF16)
    reduced = reduce(
        "reduce_second",
        4,
        far,
        fsdp,
        ("seq",) * micro + ("all", "group"),
        tuple(grad_kvs) + (g_output.reshape(blocks + (width,)), final.reshape(group)),
    )
    grad_kvs, output_part = reduced[:micro], reduced[micro]
    results = (middle + reduced[micro + 1]).astype(BF16)
    grad_query = (
        inverse_rotary(
            jnp.concatenate(grad_query, axis=0).reshape(-1, QUERY_HEADS, HEAD_WIDTH),
            cosine_table,
            sine_table,
        )
        .reshape(-1, width)
        .astype(BF16)
    )
    grad_kv = jnp.concatenate(grad_kvs, axis=0)
    grad_key = inverse_rotary(
        grad_kv[:, :kv_width].reshape(-1, KEY_VALUE_HEADS, HEAD_WIDTH), cosine_table, sine_table
    ).reshape(-1, kv_width)
    grad_kv = jnp.concatenate([grad_key, grad_kv[:, kv_width:]], axis=1).astype(BF16)
    grad_normed = cols_dot(jnp.concatenate([grad_kv, grad_query], axis=1), w_qkv)
    grad_rows, gain_attn_sum = rms_backward(rows, recip_one, gain_attn, grad_normed)
    input_grad = grad_middle + grad_rows
    g_qkv = rows_dot(normed_low, jnp.concatenate([grad_kv, grad_query], axis=1)).astype(BF16)
    bias_query = jnp.sum(grad_query.astype(F32), axis=0)
    bias_kv = jnp.sum(grad_kv.astype(F32), axis=0)
    vector_sums = jnp.concatenate(
        [
            v.reshape(devices, -1)
            for v in (
                gain_attn_sum,
                bias_query,
                bias_kv[:kv_width],
                bias_kv[kv_width:],
                gain_mlp_sum,
            )
        ],
        axis=1,
    )
    vector_sums = jnp.pad(vector_sums, ((0, 0), (0, 1024 - vector_sums.shape[1])))
    qkv_part, vector_part = reduce(
        "reduce_last",
        5,
        far,
        fsdp,
        ("all", "all"),
        (g_qkv.reshape(blocks + (-1,)), vector_sums.reshape(far, 2, 2, 2, fsdp, 8, 128)),
    )
    kv_part, query_part = qkv_part[:, : 2 * kv_width], qkv_part[:, 2 * kv_width :]
    vector_part = vector_part.reshape(-1)
    gate_sum, up_sum = move("spread_last", 6, far, fsdp, ("spread", "spread"), (gate_sum, up_sum))

    def joined(part):
        part = part.reshape(8, shard, far, -1).transpose(1, 2, 0, 3)
        return part.reshape(shard, hidden_width).astype(F32)

    return (
        results.reshape(1, micro, token_rows, width),
        input_grad.reshape(1, micro, token_rows, width),
        vector_part[cuts[0] : cuts[1]],
        query_part,
        vector_part[cuts[1] : cuts[2]],
        kv_part[:, :kv_width],
        vector_part[cuts[2] : cuts[3]],
        kv_part[:, kv_width:],
        vector_part[cuts[3] : cuts[4]],
        output_part,
        vector_part[cuts[4] : cuts[5]],
        joined(gate_sum),
        joined(up_sum),
        down_part,
    )


def solution(mesh):
    fsdp = mesh.shape["fsdp"]
    far = mesh.shape["seq"] // 8
    inner = Mesh(mesh.devices.reshape(far, 2, 2, 2, fsdp), ("h", "p", "y", "c", "x"))
    seq = ("h", "p", "y", "c")
    every = seq + ("x",)
    tokens = P("x", None, seq, None)
    matrix, vector = P(every, None), P(every)
    in_specs = (
        tokens,
        P("x", None, None),
        vector,
        matrix,
        vector,
        matrix,
        vector,
        matrix,
        vector,
        matrix,
        vector,
        matrix,
        matrix,
        matrix,
        tokens,
    )
    out_specs = (
        tokens,
        tokens,
        vector,
        matrix,
        vector,
        matrix,
        vector,
        matrix,
        vector,
        matrix,
        vector,
        matrix,
        matrix,
        matrix,
    )
    return jax.shard_map(
        functools.partial(body, (far, fsdp)),
        mesh=inner,
        in_specs=in_specs,
        out_specs=out_specs,
        check_vma=False,
    )
```

time: 966 us -> 903 us (0.935)
  Pallas kernels: 19.7 us -> 519 us
  waiting for transfers between devices: 379 us -> 85.4 us
  starting transfers between devices: 116 us -> 10.3 us
  local copies, waits for them, and re-layouts: 177 us -> 89.5 us
  blocking collectives: 40 us -> 0 us
  other arithmetic: 78.9 us -> 44 us
  between operations: 17.9 us -> 2.12 us
  matrix products: 129 us -> 144 us
    pallas_call x0 -> x7, Pallas kernels: none -> 500 us  [the longest x4 297 us: move(): pl.pallas_call(functools.partial(move_kernel, kinds, far), out_shape=tupl...]
    ppermute x86 -> x3, waiting for transfers between devices: 269 us -> 0.01 us  [hop(): return lax.ppermute(array, axis, SWAP)]
    ppermute x86 -> x3, starting transfers between devices: 103 us -> 3.8 us  [hop(): return lax.ppermute(array, axis, SWAP)]
    unnamed x330 -> x157, local copies, waits for them, and re-layouts: 58.7 us -> 14.7 us
    unnamed x1 -> x0, blocking collectives: 40 us -> none
    gather x10 -> x0, local copies, waits for them, and re-layouts: 31.1 us -> none  [the longest x3 13.3 us: ordered(): jnp.take(array.reshape(devices, -1, columns), all_slot, axis=0)]
    ppermute x11 -> x3, waiting for transfers between devices: 109 us -> 85.4 us  [hop(): lax.ppermute(array, 'h', [(i, (i + shift) % far) for i in range(far)])]
    select_n x12 -> x0, other arithmetic: 17.7 us -> none  [the longest x3 8.58 us: ordered(): jnp.take(array.reshape(devices, -1, columns), all_slot, axis=0)]
  transfers between devices with their start and end apart: 103 -> 6, of which waited for: 51 -> 2; matrix products, arithmetic and copies ran while one was open for 28% -> 21% of each run, Pallas kernels for 2% -> 28%
where the time goes in v2:
time: 903 us; the launch traced here: 895 us
  Pallas kernels  519 us (57%)
  matrix products  144 us (16%)
  local copies, waits for them, and re-layouts  89.5 us (10%)
  waiting for transfers between devices  85.4 us (9%)
  other arithmetic  44 us (5%)
  starting transfers between devices  10.3 us (1%)
    pallas_call x4, Pallas kernels, move(): pl.pallas_call(functools.partial(move_kernel, kinds, far), out_shape=tupl...  297 us
    pallas_call x3, Pallas kernels, reduce(): pl.pallas_call(functools.partial(reduce_kernel, kinds, far, fsdp, tuple(c...  203 us
    dot_general x15, matrix products, dot(): lax.dot_general(left, right, ((dims[0], dims[1]), ((), ())), preferred_el...  144 us
    ppermute x3, waiting for transfers between devices, hop(): lax.ppermute(array, 'h', [(i, (i + shift) % far) for i in range(far)])  85.4 us
  transfers between devices with their start and end apart: 6, of which 2 were waited for; matrix products, arithmetic and copies ran while one was open for 21% of the time, Pallas kernels for 28%

profile of v2, /device:TPU:0, one launch (start us, length us, event | category | flops | bytes accessed | tf_op | source)
XLA Modules:
  0.0 895.0 jit_solution(11324374208821669143)
XLA Ops:
  10.7 74.5 %gather_first.1 = (bf16[2,2,2,2,2,48,2048]{6,5,4,3,2,1,0:T(8,128)(2,1)}, f32[2,2,2,2,2,8,128]{6,5,4,3,2,1,0:T(8,128)}, bf16[8,48,1120]{2,1,0:T(8,128)(2,1)}, bf1...) custom-call(bf16[48,2048]{1,0:T(8,128)(2,1)} %pad_maximum_fusion.7.refs_0_, f32[8,128]{1,0:T(8,128)} %bitcast_convert_fusion.refs_1_, ...), custom_call_target="tpu_custom_call" | custom-call | bytes 92667904 | tf_op jit(solution)/shard_map/gather_first/pallas_call | solution.py:464
  109.3 153.2 %gather_second.1 = (bf16[2,2,2,2,128,512]{5,4,3,2,1,0:T(8,128)(2,1)}, bf16[2,2,2,2,128,512]{5,4,3,2,1,0:T(8,128)(2,1)}, bf16[2,2,2,2,2,48,1536]{6,5,4,3,2,1,0:T(...) custom-call(bf16[128,512]{1,0:T(8,128)(2,1)} %get-tuple-element.98.r, ...), custom_call_target="tpu_custom_call" | custom-call | bytes 176685056 | tf_op jit(solution)/shard_map/gather_second/pallas_call | solution.py:464
  262.5 4.6 attend_forward.2
  279.3 35.0 %gather_tokens.1 = bf16[2,2,2,256,1536]{4,3,2,1,0:T(8,128)(2,1)} custom-call(bf16[256,1536]{1,0:T(8,128)(2,1)} %multiply_convert_fusion.4.refs_0_), custom_call_target="tpu_custom_call" | custom-call | bytes 50331648 | tf_op jit(solution)/shard_map/gather_tokens/pallas_call | solution.py:464
  314.3 12.8 %fusion.66 = f32[2048,1120]{0,1:T(8,128)} fusion(bf16[2048,1536]{1,0:T(8,128)(2,1)} %bitcast.225, bf16[1536,1120]{1,0:T(8,128)(2,1)} %bitcast.293), kind=kOutput, calls=%fused_computation.171 | convolution fusion | flops 7046430720 | bytes 18907136 | tf_op jit(solution)/shard_map/dot_general | solution.py:66
  327.1 14.1 %fusion = (bf16[1120,2048]{1,0:T(8,128)(2,1)}, f32[2048,1120]{0,1:T(8,128)}) fusion(f32[2048,1120]{0,1:T(8,128)} %fusion.66, bf16[2048,1536]{1,0:T(8,128)(2,1)S(1)} %bitcast.227, bf16[1536,1120]{1,0:T(8,128)(2,1)S(1)} %bitcast.291), kind=kOutput, calls=%fused_computation.2 | convolution fusion | flops 7060193280 | bytes 32669696 | tf_op jit(solution)/shard_map/dot_general | solution.py:66
  341.2 11.2 %convolution_convert_fusion.3 = bf16[2,2,280,1536]{3,2,1,0:T(8,128)(2,1)S(1)} fusion(bf16[2,2,280,2048]{3,2,1,0:T(8,128)(2,1)} %bitcast.297, bf16[2048,1536,1,1]{1,0,3,2:T(8,128)(2,1)} %bitcast.285), kind=kOutput, calls=%fused_computation.24 | convolution fusion | flops 7048151040 | bytes 14319616 | tf_op jit(solution)/shard_map/dot_general | solution.py:66
  356.1 8.8 copy.69
  364.9 18.6 %multiply_convert_fusion.1 = (bf16[2048,1120]{0,1:T(8,128)(2,1)S(1)}, bf16[2048,1120]{0,1:T(8,128)(2,1)}) fusion(f32[2048,1120]{0,1:T(8,128)} %fusion.66, f32[2048,1120]{0,1:T(8,128)} %get-tuple-element.133, bf16[2048,1536]{1,0:T(8,128)(2,1)} %bitcast.286, bf16[1120,1536]{1,0:T(8,128)(2,1)} %bitcast.295), kind=kOutput, calls=%fused_computation.9 | convolution fusion | flops 7076249600 | bytes 37257216 | tf_op jit(solution)/shard_map/dot_general | solution.py:66
  383.5 8.5 fusion.16
  394.3 8.7 fusion.11
  407.5 18.1 %convolution_convert_fusion = bf16[2048,1536]{1,0:T(8,128)(2,1)} fusion(bf16[1120,1536]{1,0:T(8,128)(2,1)S(1)} %bitcast.296, f32[2048,1120]{0,1:T(8,128)} %get-tuple-element.133, f32[2048,1120]{0,1:T(8,128)} %fusion.66), kind=kOutput, calls=%fused_computation.13 | convolution fusion | flops 7063339008 | bytes 28082176 | tf_op jit(solution)/shard_map/dot_general | solution.py:66
  425.5 13.3 %fusion.67 = f32[2048,1536]{1,0:T(8,128)} fusion(bf16[2048,1120]{0,1:T(8,128)(2,1)} %get-tuple-element.79, bf16[1536,1120]{1,0:T(8,128)(2,1)S(1)} %bitcast.294), kind=kOutput, calls=%fused_computation.172 | convolution fusion | flops 7046430720 | bytes 20611072 | tf_op jit(solution)/shard_map/dot_general | solution.py:66
  438.9 12.5 %add_convert_fusion = bf16[2048,1536]{1,0:T(8,128)(2,1)} fusion(f32[2048,1536]{1,0:T(8,128)} %fusion.67, bf16[2048,1120]{0,1:T(8,128)(2,1)S(1)} %get-tuple-element.78, bf16[1536,1120]{1,0:T(8,128)(2,1)S(1)} %bitcast.292), kind=kOutput, calls=%fused_computation | convolution fusion | flops 7052722176 | bytes 26902528 | tf_op jit(solution)/shard_map/dot_general | solution.py:66
  451.4 36.7 %reduce_tokens.1 = f32[256,1536]{1,0:T(8,128)} custom-call(bf16[2,2,2,256,1536]{4,3,2,1,0:T(8,128)(2,1)} %bitcast.249), custom_call_target="tpu_custom_call" | custom-call | bytes 50331648 | tf_op jit(solution)/shard_map/reduce_tokens/pallas_call | solution.py:646
  497.2 5.7 attend_backward.3
  506.0 5.3 attend_backward.2
  514.4 111.4 %reduce_second.1 = (f32[128,512]{1,0:T(8,128)}, f32[128,512]{1,0:T(8,128)}, f32[48,1536]{1,0:T(8,128)}, f32[256,1536]{1,0:T(8,128)}) custom-call(bf16[2,2,2,2,128,512]{5,4,3,2,1,0:T(8,128)(2,1)} %bitcast.239, bf16[2,2,2,2,128,512]{5,4,3,2,1,0:T(8,128)(2,1)} %bitcast.238, bf16[2,2,2,2,2,48,1536]{6,5,4,3,2,1,0:T(8,128)(2,1)} %bitcast.223, ...), custom_call_target="tpu_custom_call" | custom-call | bytes 121634816 | tf_op jit(solution)/shard_map/reduce_second/pallas_call | solution.py:646
  658.6 7.1 fusion.40
  668.0 5.8 convolution_convert_fusion.1
  673.9 54.7 %reduce_last.1 = (f32[48,2048]{1,0:T(8,128)}, f32[8,128]{1,0:T(8,128)}) custom-call(bf16[2,2,2,2,2,48,2048]{6,5,4,3,2,1,0:T(8,128)(2,1)} %bitcast.224, f32[2,2,2,2,2,8,128]{6,5,4,3,2,1,0:T(8,128)} %bitcast.264), custom_call_target="tpu_custom_call" | custom-call | bytes 51380224 | tf_op jit(solution)/shard_map/reduce_last/pallas_call | solution.py:646
  753.5 67.6 %collective-permute-done.3 = bf16[8,48,1120]{2,1,0:T(8,128)(2,1)S(1)} collective-permute-done((bf16[8,48,1120]{2,1,0:T(8,128)(2,1)S(1)}, bf16[8,48,1120]{2,1,0:T(8,128)(2,1)S(1)}, u32[]{:S(2)}, u32[]{:S(2)}) %collective-permute-start.3) | collective-permute-done | bytes 860192 | tf_op jit(solution)/shard_map/ppermute | solution.py:694
  822.2 17.8 %collective-permute-done.1 = bf16[8,48,1120]{2,1,0:T(8,128)(2,1)S(1)} collective-permute-done((bf16[8,48,1120]{2,1,0:T(8,128)(2,1)S(1)}, bf16[8,48,1120]{2,1,0:T(8,128)(2,1)S(1)}, u32[]{:S(2)}, u32[]{:S(2)}) %collective-permute-start.1) | collective-permute-done | bytes 860192 | tf_op jit(solution)/shard_map/ppermute | solution.py:694
  841.2 34.2 %spread_last.1 = (bf16[8,48,1120]{2,1,0:T(8,128)(2,1)}, bf16[8,48,1120]{2,1,0:T(8,128)(2,1)}) custom-call(bf16[8,48,1120]{2,1,0:T(8,128)(2,1)} %fusion.25.refs_0_, bf16[8,48,1120]{2,1,0:T(8,128)(2,1)} %fusion.24.refs_1_), custom_call_target="tpu_custom_call" | custom-call | bytes 13762560 | tf_op jit(solution)/shard_map/spread_last/pallas_call | solution.py:464
  (288 shorter events, 152.9 us)
Async XLA Ops:
  9.3 77.0 %copy-start.55 = (s32[1,2,4]{2,1,0:T(2,128)S(1)}, s32[1,2,4]{2,1,0:T(2,128)}, u32[]{:S(2)}) copy-start(s32[1,2,4]{2,1,0:T(2,128)} %param.16) | copy-start | bytes 100
  10.7 78.8 %copy-start.4 = (bf16[1,2,128,1536]{3,2,1,0:T(8,128)(2,1)S(1)}, bf16[1,2,128,1536]{3,2,1,0:T(8,128)(2,1)}, u32[]{:S(2)}) copy-start(bf16[1,2,128,1536]{3,2,1,0:T(8,128)(2,1)} %param.15) | copy-start | bytes 2359300
  89.2 13.6 %copy-start.27 = (f32[256,128]{0,1:T(8,128)}, f32[256,128]{0,1:T(8,128)S(1)}, u32[]{:S(2)}) copy-start(f32[256,128]{0,1:T(8,128)S(1)} %maximum_maximum_fusion.1) | copy-start | bytes 393220
  89.3 17.3 %copy-start.34 = (f32[256,128]{1,0:T(8,128)}, f32[256,128]{1,0:T(8,128)S(1)}, u32[]{:S(2)}) copy-start(f32[256,128]{1,0:T(8,128)S(1)} %copy.59) | copy-start | bytes 393220
  277.5 36.7 %copy-start.1 = (f32[256,1536]{1,0:T(8,128)}, f32[256,1536]{1,0:T(8,128)S(1)}, u32[]{:S(2)}) copy-start(f32[256,1536]{1,0:T(8,128)S(1)} %get-tuple-element.130) | copy-start | bytes 4718596
  278.2 36.1 %copy-start.51 = (f32[256]{0:T(256)}, f32[256]{0:T(256)S(1)}, u32[]{:S(2)}) copy-start(f32[256]{0:T(256)S(1)} %get-tuple-element.118) | copy-start | bytes 3076
  278.2 36.1 %copy-start.42 = (f32[1536]{0:T(1024)}, f32[1536]{0:T(1024)S(1)}, u32[]{:S(2)}) copy-start(f32[1536]{0:T(1024)S(1)} %mul.331) | copy-start | bytes 18436
  314.3 12.8 %copy-start = (bf16[2,2,2,256,1536]{4,3,2,1,0:T(8,128)(2,1)S(1)}, bf16[2,2,2,256,1536]{4,3,2,1,0:T(8,128)(2,1)}, u32[]{:S(2)}) copy-start(bf16[2,2,2,256,1536]{4,3,2,1,0:T(8,128)(2,1)} %gather_tokens.1) | copy-start | bytes 18874372
  314.3 12.8 %copy-start.65 = (bf16[2,8,2,48,1120]{4,3,2,1,0:T(8,128)(2,1)S(1)}, bf16[2,8,2,48,1120]{4,3,2,1,0:T(8,128)(2,1)}, u32[]{:S(2)}) copy-start(bf16[2,8,2,48,1120]{4,3,2,1,0:T(8,128)(2,1)} %get-tuple-element.54) | copy-start | bytes 10321924
  352.4 12.4 %copy-start.15 = (bf16[2,2,280,1536]{3,2,1,0:T(8,128)(2,1)}, bf16[2,2,280,1536]{3,2,1,0:T(8,128)(2,1)S(1)}, u32[]{:S(2)}) copy-start(bf16[2,2,280,1536]{3,2,1,0:T(8,128)(2,1)S(1)} %convolution_convert_fusion.3) | copy-start | bytes 10321924
  353.9 394.0 %collective-permute-start.4 = (bf16[2,280,1536]{2,1,0:T(8,128)(2,1)}, bf16[2,280,1536]{2,1,0:T(8,128)(2,1)}, u32[]{:S(2)}, u32[]{:S(2)}) collective-permute-start(bf16[2,280,1536]{2,1,0:T(8,128)(2,1)} %dynamic-slice_bitcast_fusion.2), channel_id=1, source_target_pairs={{0,1},{1,0},{2,3},{3,2},{4,5},{5,4},{6,7},{7,6},{8,9},{9,8},{10,11... | collective-permute-start | bytes 5160968 | tf_op jit(solution)/shard_map/ppermute | solution.py:695
  364.9 18.6 %copy-start.8 = (bf16[1536,2048]{1,0:T(8,128)(2,1)S(1)}, bf16[1536,2048]{1,0:T(8,128)(2,1)}, u32[]{:S(2)}) copy-start(bf16[1536,2048]{1,0:T(8,128)(2,1)} %copy.69) | copy-start | bytes 18874372
  393.6 345.2 %collective-permute-start.2 = (bf16[2,8,48,1120]{3,2,1,0:T(8,128)(2,1)}, bf16[2,8,48,1120]{3,2,1,0:T(8,128)(2,1)}, u32[]{:S(2)}, u32[]{:S(2)}) collective-permute-start(bf16[2,8,48,1120]{3,2,1,0:T(8,128)(2,1)} %dynamic-slice_bitcast_fusion), channel_id=1, source_target_pairs={{0,1},{1,0},{2,3},{3,2},{4,5},{5,4},{6,7},{7,6},{8,9},{9,8},{10,11... | collective-permute-start | bytes 5160968 | tf_op jit(solution)/shard_map/ppermute | solution.py:695
  406.2 19.4 %copy-start.67 = (bf16[2,8,2,48,1120]{4,3,2,1,0:T(8,128)(2,1)S(1)}, bf16[2,8,2,48,1120]{4,3,2,1,0:T(8,128)(2,1)}, u32[]{:S(2)}) copy-start(bf16[2,8,2,48,1120]{4,3,2,1,0:T(8,128)(2,1)} %get-tuple-element.55) | copy-start | bytes 10321924
  406.2 339.2 %collective-permute-start = (bf16[2,8,48,1120]{3,2,1,0:T(8,128)(2,1)}, bf16[2,8,48,1120]{3,2,1,0:T(8,128)(2,1)}, u32[]{:S(2)}, u32[]{:S(2)}) collective-permute-start(bf16[2,8,48,1120]{3,2,1,0:T(8,128)(2,1)} %dynamic-slice_bitcast_fusion.1), channel_id=1, source_target_pairs={{0,1},{1,0},{2,3},{3,2},{4,5},{5,4},{6,7},{7,6},{8,9},{9,8},{10,11... | collective-permute-start | bytes 5160968 | tf_op jit(solution)/shard_map/ppermute | solution.py:695
  425.5 13.3 %copy-start.66 = (bf16[2,8,2,48,1120]{4,3,2,1,0:T(8,128)(2,1)S(1)}, bf16[2,8,2,48,1120]{4,3,2,1,0:T(8,128)(2,1)}, u32[]{:S(2)}) copy-start(bf16[2,8,2,48,1120]{4,3,2,1,0:T(8,128)(2,1)} %get-tuple-element.54) | copy-start | bytes 10321924
  451.4 36.7 %copy-start.2 = (f32[256,1536]{1,0:T(8,128)S(1)}, f32[256,1536]{1,0:T(8,128)}, u32[]{:S(2)}) copy-start(f32[256,1536]{1,0:T(8,128)} %copy-done.1) | copy-start | bytes 4718596
  451.4 36.7 %copy-start.43 = (f32[1536]{0:T(1024)S(1)}, f32[1536]{0:T(1024)}, u32[]{:S(2)}) copy-start(f32[1536]{0:T(1024)} %copy-done.42) | copy-start | bytes 18436
  451.4 36.7 %copy-start.52 = (f32[256]{0:T(256)S(1)}, f32[256]{0:T(256)}, u32[]{:S(2)}) copy-start(f32[256]{0:T(256)} %copy-done.51) | copy-start | bytes 3076
  673.9 57.4 %copy-start.54 = (f32[2,128]{1,0:T(2,128)S(1)}, f32[2,128]{1,0:T(2,128)}, u32[]{:S(2)}) copy-start(f32[2,128]{1,0:T(2,128)} %copy-done.53) | copy-start | bytes 3076
  741.9 79.2 %collective-permute-start.3 = (bf16[8,48,1120]{2,1,0:T(8,128)(2,1)S(1)}, bf16[8,48,1120]{2,1,0:T(8,128)(2,1)S(1)}, u32[]{:S(2)}, u32[]{:S(2)}) collective-permute-start(bf16[8,48,1120]{2,1,0:T(8,128)(2,1)S(1)} %dynamic-slice_bitcast_fusion.3), channel_id=1, source_target_pairs={{0,16},{16,0},{1,17},{17,1},{2,18},{18,2},{3,19},{19,3},{4,20},{20... | collective-permute-start | bytes 2580488 | tf_op jit(solution)/shard_map/ppermute | solution.py:694
  747.6 92.5 %collective-permute-start.1 = (bf16[8,48,1120]{2,1,0:T(8,128)(2,1)S(1)}, bf16[8,48,1120]{2,1,0:T(8,128)(2,1)S(1)}, u32[]{:S(2)}, u32[]{:S(2)}) collective-permute-start(bf16[8,48,1120]{2,1,0:T(8,128)(2,1)S(1)} %dynamic-slice_bitcast_fusion.4), channel_id=1, source_target_pairs={{0,16},{16,0},{1,17},{17,1},{2,18},{18,2},{3,19},{19,3},{4,20},{20... | collective-permute-start | bytes 2580488 | tf_op jit(solution)/shard_map/ppermute | solution.py:694
  749.8 72.4 %copy-start.7 = (bf16[2,280,1536]{2,1,0:T(8,128)(2,1)}, bf16[2,280,1536]{2,1,0:T(8,128)(2,1)S(1)}, u32[]{:S(2)}) copy-start(bf16[2,280,1536]{2,1,0:T(8,128)(2,1)S(1)} %fusion.23) | copy-start | bytes 5160964
  750.9 140.3 %collective-permute-start.5 = (bf16[280,1536]{1,0:T(8,128)(2,1)}, bf16[280,1536]{1,0:T(8,128)(2,1)}, u32[]{:S(2)}, u32[]{:S(2)}) collective-permute-start(bf16[280,1536]{1,0:T(8,128)(2,1)} %dynamic-slice_bitcast_fusion.5), channel_id=1, source_target_pairs={{0,16},{16,0},{1,17},{17,1},{2,18},{18,2},{3,19},{19,3},{4,20},{20... | collective-permute-start | bytes 2580488 | tf_op jit(solution)/shard_map/ppermute | solution.py:694
  (54 other events, 170.8 us)

commit v3 on v2

--- a/solution.py
+++ b/solution.py
@@ -32,20 +32,7 @@
     freqs = 1.0 / THETA ** (jnp.arange(0, head_size, 2, dtype=F32) / head_size)
     angles = offsets.astype(F32)[:, None] * freqs[None, :]
     cosine, sine = jnp.cos(angles), jnp.sin(angles)
-    return (jnp.concatenate([cosine, cosine], axis=1), jnp.concatenate([sine, sine], axis=1))
-
-
-def apply_rotary(values, cosine_table, sine_table):
-    half = values.shape[-1] // 2
-    turned = jnp.concatenate([-values[..., half:], values[..., :half]], axis=-1)
-    return values * cosine_table[:, None, :] + turned * sine_table[:, None, :]
-
-
-def inverse_rotary(grads, cosine_table, sine_table):
-    half = grads.shape[-1] // 2
-    scaled = grads * sine_table[:, None, :]
-    turned = jnp.concatenate([scaled[..., half:], -scaled[..., :half]], axis=-1)
-    return grads * cosine_table[:, None, :] + turned
+    return (jnp.concatenate([cosine, cosine], axis=1), jnp.concatenate([-sine, sine], axis=1))
 
 
 def rms_forward(rows, gain):
@@ -116,7 +103,7 @@
     lse_ref[0] = top + jnp.log(total)
 
 
-def attend_forward(meta, queries, stack, span):
+def attend_forward(number, meta, queries, stack, span):
     pieces, rows, _ = stack.shape
     width = queries.shape[1]
     part = width // KEY_VALUE_HEADS
@@ -124,7 +111,7 @@
         num_scalar_prefetch=1,
         grid=(KEY_VALUE_HEADS,),
         in_specs=[
-            pl.BlockSpec((rows, part), lambda g, m: (0, g)),
+            pl.BlockSpec((rows, part), lambda g, m: (number, g)),
             pl.BlockSpec((pieces, rows, HEAD_WIDTH), lambda g, m: (0, 0, g)),
             pl.BlockSpec((pieces, rows, HEAD_WIDTH), lambda g, m: (0, 0, KEY_VALUE_HEADS + g)),
             pl.BlockSpec((8, GROUP * rows), lambda g, m: (0, 0)),
@@ -149,85 +136,167 @@
 
 
 def attend_backward_kernel(
-    meta, q_ref, do_ref, k_ref, v_ref, span_ref, lse_ref, dq_ref, dk_ref, dv_ref, p_ref, dp_ref
+    meta, q_ref, do_ref, kv_ref, span_ref, lse_ref, cos_ref, sin_ref, dq_ref, dkv_ref, p_ref, dp_ref
 ):
     rows = q_ref.shape[0]
     wide = GROUP * rows
-    cols = [slice(h * HEAD_WIDTH, (h + 1) * HEAD_WIDTH) for h in range(GROUP)]
-    queries = jnp.concatenate([q_ref[:, c] for c in cols], axis=0)
-    grads = jnp.concatenate([do_ref[:, c] for c in cols], axis=0)
     first, last = span_ref[0:1, :], span_ref[1:2, :]
-    lse = lse_ref[0]
     local = lax.broadcasted_iota(jnp.int32, (rows, 1), 0)
     low = meta[0]
-    dk_ref[...] = jnp.zeros_like(dk_ref)
-    dv_ref[...] = jnp.zeros_like(dv_ref)
-
-    def collect(block, delta):
-        scores = dot(k_ref[block], queries, ((1,), (1,))) * SCALE
-        index = block * rows + local
-        probs = jnp.where((index >= first) & (index <= last), jnp.exp(scores - lse), 0.0)
-        grad_probs = dot(v_ref[block], grads, ((1,), (1,)))
-        p_ref[block - low] = probs
-        dp_ref[block - low] = grad_probs
-        return delta + jnp.sum(probs * grad_probs, axis=0, keepdims=True)
-
-    delta = lax.fori_loop(low, meta[1] + 1, collect, jnp.zeros((1, wide), F32))
-
-    def spread(block, accum):
-        probs = p_ref[block - low]
-        grad_scores = (probs * (dp_ref[block - low] - delta)).astype(BF16)
-        dk_ref[block] = (mat_dot(grad_scores, queries) * SCALE).astype(BF16)
-        dv_ref[block] = mat_dot(probs.astype(BF16), grads).astype(BF16)
-        return accum + dot(k_ref[block], grad_scores, ((0,), (0,)))
-
-    accum = lax.fori_loop(low, meta[1] + 1, spread, jnp.zeros((HEAD_WIDTH, wide), F32))
-    grad_queries = (accum * SCALE).T
-    for h in range(GROUP):
-        dq_ref[:, cols[h]] = grad_queries[h * rows : (h + 1) * rows]
-
-
-def attend_backward(meta, queries, grads, stack, span, lse):
-    pieces, rows, _ = stack.shape
+    cosine, sine = cos_ref[...], sin_ref[...]
+    dkv_ref[...] = jnp.zeros_like(dkv_ref)
+    for group in range(KEY_VALUE_HEADS):
+        heads = range(group * GROUP, (group + 1) * GROUP)
+        cols = [slice(h * HEAD_WIDTH, (h + 1) * HEAD_WIDTH) for h in heads]
+        key_cols = slice(group * HEAD_WIDTH, (group + 1) * HEAD_WIDTH)
+        start = (KEY_VALUE_HEADS + group) * HEAD_WIDTH
+        value_cols = slice(start, start + HEAD_WIDTH)
+        queries = jnp.concatenate([q_ref[:, c] for c in cols], axis=0)
+        grads = jnp.concatenate([do_ref[:, c] for c in cols], axis=0)
+        lse = lse_ref[group]
+
+        def collect(block, delta):
+            scores = dot(kv_ref[block, :, key_cols], queries, ((1,), (1,))) * SCALE
+            index = block * rows + local
+            probs = jnp.where((index >= first) & (index <= last), jnp.exp(scores - lse), 0.0)
+            grad_probs = dot(kv_ref[block, :, value_cols], grads, ((1,), (1,)))
+            p_ref[block - low] = probs
+            dp_ref[block - low] = grad_probs
+            return delta + jnp.sum(probs * grad_probs, axis=0, keepdims=True)
+
+        delta = lax.fori_loop(low, meta[1] + 1, collect, jnp.zeros((1, wide), F32))
+
+        def spread(block, accum):
+            probs = p_ref[block - low]
+            grad_scores = (probs * (dp_ref[block - low] - delta)).astype(BF16)
+            dkv_ref[block, :, key_cols] = (mat_dot(grad_scores, queries) * SCALE).astype(BF16)
+            dkv_ref[block, :, value_cols] = mat_dot(probs.astype(BF16), grads).astype(BF16)
+            return accum + dot(kv_ref[block, :, key_cols], grad_scores, ((0,), (0,)))
+
+        accum = lax.fori_loop(low, meta[1] + 1, spread, jnp.zeros((HEAD_WIDTH, wide), F32))
+        grad_queries = (accum * SCALE).T
+        for h in range(GROUP):
+            part = grad_queries[h * rows : (h + 1) * rows]
+            turned = pltpu.roll(part, HEAD_WIDTH // 2, 1)
+            dq_ref[:, cols[h]] = (part * cosine - turned * sine).astype(BF16)
+
+
+def attend_backward(number, meta, queries, grads, stack, span, lse, cosine, sine):
+    pieces, rows, wide = stack.shape
     width = queries.shape[1]
-    part = width // KEY_VALUE_HEADS
     most = pieces // 2 + 1
-    head = (pieces, rows, HEAD_WIDTH)
+
+    def own(columns):
+        return pl.BlockSpec((rows, columns), lambda i, m: (number, 0))
+
+    def whole(shape):
+        return pl.BlockSpec(shape, lambda i, m: (0,) * len(shape))
+
     spec = pltpu.PrefetchScalarGridSpec(
         num_scalar_prefetch=1,
-        grid=(KEY_VALUE_HEADS,),
+        grid=(1,),
         in_specs=[
-            pl.BlockSpec((rows, part), lambda g, m: (0, g)),
-            pl.BlockSpec((rows, part), lambda g, m: (0, g)),
-            pl.BlockSpec(head, lambda g, m: (0, 0, g)),
-            pl.BlockSpec(head, lambda g, m: (0, 0, KEY_VALUE_HEADS + g)),
-            pl.BlockSpec((8, GROUP * rows), lambda g, m: (0, 0)),
-            pl.BlockSpec((1, 1, GROUP * rows), lambda g, m: (g, 0, 0)),
+            own(width),
+            own(width),
+            whole(stack.shape),
+            whole(span.shape),
+            whole(lse.shape),
+            own(HEAD_WIDTH),
+            own(HEAD_WIDTH),
         ],
-        out_specs=[
-            pl.BlockSpec((rows, part), lambda g, m: (0, g)),
-            pl.BlockSpec(head, lambda g, m: (0, 0, g)),
-            pl.BlockSpec(head, lambda g, m: (0, 0, g)),
-        ],
+        out_specs=[whole((rows, width)), whole(stack.shape)],
         scratch_shapes=[
             pltpu.VMEM((most, rows, GROUP * rows), F32),
             pltpu.VMEM((most, rows, GROUP * rows), F32),
         ],
     )
-    kv_shape = jax.ShapeDtypeStruct((pieces, rows, KEY_VALUE_HEADS * HEAD_WIDTH), BF16)
     return pl.pallas_call(
         attend_backward_kernel,
         grid_spec=spec,
-        out_shape=(jax.ShapeDtypeStruct((rows, width), F32), kv_shape, kv_shape),
+        out_shape=(
+            jax.ShapeDtypeStruct((rows, width), BF16),
+            jax.ShapeDtypeStruct(stack.shape, BF16),
+        ),
         cost_estimate=pl.CostEstimate(
-            flops=10 * rows * rows * 6 * width, bytes_accessed=stack.size * 4, transcendentals=0
+            flops=0, bytes_accessed=COST, transcendentals=0
         ),
         name="attend_backward",
-    )(meta, queries, grads, stack, stack, span, lse)
+    )(meta, queries, grads, stack, span, lse, cosine, sine)
+
+
+def rotate_kernel(turned_heads, splits, sign, pre_ref, bias_ref, cos_ref, sin_ref, *outs):
+    cosine, sine = cos_ref[...], sin_ref[...] * sign
+    for head in range(pre_ref.shape[1] // HEAD_WIDTH):
+        cols = slice(head * HEAD_WIDTH, (head + 1) * HEAD_WIDTH)
+        part = pre_ref[:, cols] + bias_ref[:, cols]
+        if head in turned_heads:
+            part = part * cosine + pltpu.roll(part, HEAD_WIDTH // 2, 1) * sine
+        part = part.astype(BF16)
+        for (top, height, left, wide), out in zip(splits, outs):
+            if left <= head * HEAD_WIDTH < left + wide:
+                at = head * HEAD_WIDTH - left
+                out[:, at : at + HEAD_WIDTH] = part[top : top + height]
+
+
+def rotate(pre, bias, cosine, sine, turned_heads, splits, sign):
+    return pl.pallas_call(
+        functools.partial(rotate_kernel, tuple(turned_heads), splits, sign),
+        out_shape=tuple(
+            jax.ShapeDtypeStruct((height, wide), BF16) for _, height, _, wide in splits
+        ),
+        cost_estimate=pl.CostEstimate(flops=0, bytes_accessed=8 * pre.size, transcendentals=0),
+        name="rotate",
+    )(pre, bias, cosine, sine)
+
+
+def cut_kernel(far, whole, *refs):
+    count = len(refs) // 2
+    for source, out in zip(refs[:count], refs[count:]):
+        small = (out if whole else source).shape[1] // (8 * far)
+        for h in range(far):
+            for g in range(8):
+                left, right = (h * 8 + g) * small, h * small
+                if whole:
+                    out[:, left : left + small] = source[g, :, right : right + small].astype(F32)
+                else:
+                    out[g, :, right : right + small] = source[:, left : left + small]
+
+
+def cut_columns(far, whole, arrays):
+    shapes = []
+    for array in arrays:
+        if whole:
+            shapes.append(jax.ShapeDtypeStruct((array.shape[1], 8 * array.shape[2]), F32))
+        else:
+            shape = (8, array.shape[0], array.shape[1] // 8)
+            shapes.append(jax.ShapeDtypeStruct(shape, array.dtype))
+    return pl.pallas_call(
+        functools.partial(cut_kernel, far, whole),
+        out_shape=tuple(shapes),
+        name="join_columns" if whole else "cut_columns",
+    )(*arrays)
 
 
 MESH = pl.DeviceIdType.MESH
+PARTS, AHEAD = 4, 2
+COST = 1024
 ANY = pl.BlockSpec(memory_space=pl.ANY)
+
+
+class Local:
+    def __init__(self, source, buffer, target, sems):
+        self.load = pltpu.make_async_copy(source, buffer, sems.at[0])
+        self.store = pltpu.make_async_copy(buffer, target, sems.at[1])
+
+    def start(self):
+        self.load.start()
+
+    def turn(self):
+        self.load.wait()
+        self.store.start()
+
+    def wait(self):
+        self.store.wait()
 
 
 class Copies:
@@ -264,9 +333,13 @@
     return {axis: 1 - lax.axis_index(axis) for axis in axes}
 
 
+def corners():
+    return [flip("p", "y"), flip("p", "c"), flip("y", "c"), flip("p", "y", "c")]
+
+
 def gather_steps(kind, far, copies, source, out, local):
     ih, ip, iy, ic, ix = (lax.axis_index(name) for name in ("h", "p", "y", "c", "x"))
-    every = kind == "all"
+    every = kind in ("all", "all_y")
 
     def block(h, p, y=iy, x=ix):
         return out.at[h, p, y, ic, x] if every else out.at[h, p, y, ic]
@@ -276,7 +349,7 @@
     count = len(pieces)
     arrivals, plane, cross, core = [None] * count, [None] * count, [None] * count, [None] * count
     columns = source.shape[-1]
-    half = columns // 2 if columns % 256 == 0 else columns
+    half = columns // 2 if columns % 256 == 0 and kind == "all" else columns
 
     def cut(ref, first):
         if half == columns:
@@ -320,7 +393,7 @@
         yield
 
 
-def group_steps(far, copies, source, out, local):
+def group_steps(far, copies, source, out, local, delay):
     ip, iy, ic = (lax.axis_index(name) for name in ("p", "y", "c"))
     half = source.shape[0] // 2
     top, low = pl.ds(0, half), pl.ds(half, half)
@@ -332,6 +405,8 @@
         return copies.start(ref, ref, flip(axis))
 
     local.start()
+    for _ in range(delay):
+        yield
     first = [
         copies.start(source.at[top], rows(ip, iy, top), flip("y")),
         copies.start(source.at[low], rows(ip, iy, low), flip("p")),
@@ -363,28 +438,40 @@
     local.wait()
 
 
-def pair_steps(far, copies, source, out, local, place):
+def pair_steps(far, copies, parts, place, local, delay):
     ih, ix = lax.axis_index("h"), lax.axis_index("x")
     local.start()
-    arrived = [copies.start(source, place(ih, ix), other_h(far, k)) for k in range(1, far)]
-    sent = [copies.start(source, place(ih, ix), flip("x"))]
+    for _ in range(delay):
+        yield
+    arrived, sent = [], []
+
+    def send(i):
+        if i < len(parts):
+            target = place(ih, ix, i)
+            arrived.append([copies.start(parts[i], target, other_h(far, k)) for k in range(1, far)])
+            sent.append(copies.start(parts[i], target, flip("x")))
+
+    for i in range(AHEAD):
+        send(i)
+    for i in range(len(parts)):
+        yield
+        send(i + AHEAD)
+        for k in range(1, far):
+            arrived[i][k - 1].wait_recv()
+            ref = place(lax.rem(ih - k + far, far), ix, i)
+            sent.append(copies.start(ref, ref, flip("x")))
     yield
-    for k in range(1, far):
-        arrived[k - 1].wait_recv()
-        ref = place(lax.rem(ih - k + far, far), ix)
-        sent.append(copies.start(ref, ref, flip("x")))
-        yield
-    for _ in range(far + 1):
-        yield
     for copy in sent:
         copy.wait_recv()
     local.wait()
 
 
-def spread_steps(far, copies, source, out, local):
+def spread_steps(far, copies, source, out, local, delay):
     ip, iy, ic = (lax.axis_index(name) for name in ("p", "y", "c"))
     me = (ip * 2 + iy) * 2 + ic
     local.start()
+    for _ in range(delay):
+        yield
     started = []
     for j in (1, 2, 4, 3, 5, 6, 7):
         p = 1 - ip if j & 4 else ip
@@ -404,38 +491,57 @@
 def move_kernel(kinds, far, *refs):
     count = len(kinds)
     sources, outs = refs[:count], refs[count : 2 * count]
-    send_sems, recv_sems, local_sems = refs[2 * count :]
+    buffers = refs[2 * count : 3 * count]
+    send_sems, recv_sems, local_sems = refs[3 * count :]
+    locals_ = []
+
+    def local_copy(i, source, target):
+        locals_.append(Local(source, buffers[i], target, local_sems.at[i]))
+        return locals_[-1]
+
     ih, ip, iy, ic, ix = (lax.axis_index(name) for name in ("h", "p", "y", "c", "x"))
     partners = [flip("p"), flip("y"), flip("c")]
     if set(kinds) - {"spread", "group"}:
         partners += [other_h(far, k) for k in range(1, far)]
-    if "all" in kinds or "pair" in kinds or "pair8" in kinds:
+    if set(kinds) - {"seq", "group", "spread"}:
         partners.append(flip("x"))
     if "spread" in kinds:
-        partners += [flip("p", "y"), flip("p", "c"), flip("y", "c"), flip("p", "y", "c")]
+        partners += corners()
     greet(partners)
     copies = Copies(send_sems, recv_sems)
     running = []
     for i, kind in enumerate(kinds):
         if kind == "spread":
             me = (ip * 2 + iy) * 2 + ic
-            local = pltpu.make_async_copy(sources[i].at[me], outs[i].at[me], local_sems.at[i])
-            running.append(spread_steps(far, copies, sources[i], outs[i], local))
+            local = local_copy(i, sources[i].at[me], outs[i].at[me])
+            running.append(spread_steps(far, copies, sources[i], outs[i], local, 0))
         elif kind == "group":
             place = outs[i].at[ip, iy, ic]
-            local = pltpu.make_async_copy(sources[i], place, local_sems.at[i])
-            running.append(group_steps(far, copies, sources[i], outs[i], local))
+            local = local_copy(i, sources[i], place)
+            delay = 3 if count > 1 else 0
+            running.append(group_steps(far, copies, sources[i], outs[i], local, delay))
         elif kind in ("pair", "pair8"):
-
-            def place(h, x, out=outs[i], wide=kind == "pair8"):
-                return out.at[h, :, x] if wide else out.at[h, x]
-
-            local = pltpu.make_async_copy(sources[i], place(ih, ix), local_sems.at[i])
-            running.append(pair_steps(far, copies, sources[i], outs[i], local, place))
+            local = outs[i].at[ih, :, ix] if kind == "pair8" else outs[i].at[ih, ix]
+            local = local_copy(i, sources[i], local)
+            step = (8 if kind == "pair8" else sources[i].shape[1]) // PARTS
+            cuts = [pl.ds(part * step, step) for part in range(PARTS)]
+            if kind == "pair8":
+                parts = [sources[i].at[c] for c in cuts]
+            else:
+                parts = [sources[i].at[:, c] for c in cuts]
+
+            def place(h, x, part, out=outs[i], cuts=cuts, wide=kind == "pair8"):
+                return out.at[h, cuts[part], x] if wide else out.at[h, x, :, cuts[part]]
+
+            wait = (PARTS - AHEAD + 1) * kinds[:i].count("pair8")
+            running.append(pair_steps(far, copies, parts, place, local, wait))
         else:
-            place = (ih, ip, iy, ic, ix) if kind == "all" else (ih, ip, iy, ic)
-            local = pltpu.make_async_copy(sources[i], outs[i].at[place], local_sems.at[i])
+            place = (ih, ip, iy, ic) if kind == "seq" else (ih, ip, iy, ic, ix)
+            local = local_copy(i, sources[i], outs[i].at[place])
             running.append(gather_steps(kind, far, copies, sources[i], outs[i], local))
+    running = [job for job in running if next(job, "end") != "end"]
+    for local in locals_:
+        local.turn()
     while running:
         running = [job for job in running if next(job, "end") != "end"]
     for copy in copies.started:
@@ -446,33 +552,36 @@
     shapes, total = [], 0
     pieces = 2 * far
     for kind, array in zip(kinds, arrays):
-        if kind == "all":
+        if kind in ("all", "all_y"):
             lead, total = (far, 2, 2, 2, fsdp), total + (far - 1) + far + 5 * pieces
         elif kind == "seq":
             lead, total = (far, 2, 2, 2), total + (far - 1) + far + 2 * pieces
         elif kind == "group":
             lead, total = (2, 2, 2), total + 13
         elif kind == "pair":
-            lead, total = (far, fsdp), total + 2 * far - 1
+            lead, total = (far, fsdp), total + PARTS * (2 * far - 1)
         elif kind == "pair8":
-            lead, total = (far, 8, fsdp), total + 2 * far - 1
+            lead, total = (far, 8, fsdp), total + PARTS * (2 * far - 1)
         else:
             lead, total = (), total + 7
         tail = array.shape[1:] if kind == "pair8" else array.shape
         shapes.append(jax.ShapeDtypeStruct(lead + tail, array.dtype))
-    size = sum(s.size * s.dtype.itemsize for s in shapes)
     return pl.pallas_call(
         functools.partial(move_kernel, kinds, far),
         out_shape=tuple(shapes),
         in_specs=[ANY] * len(arrays),
         out_specs=tuple([ANY] * len(arrays)),
         scratch_shapes=[
+            pltpu.VMEM(a.shape[1:] if kind == "spread" else a.shape, a.dtype)
+            for kind, a in zip(kinds, arrays)
+        ]
+        + [
             pltpu.SemaphoreType.DMA((total,)),
             pltpu.SemaphoreType.DMA((total,)),
-            pltpu.SemaphoreType.DMA((len(arrays),)),
+            pltpu.SemaphoreType.DMA((len(arrays), 2)),
         ],
         compiler_params=pltpu.CompilerParams(collective_id=number, has_side_effects=True),
-        cost_estimate=pl.CostEstimate(flops=0, bytes_accessed=8 * size, transcendentals=0),
+        cost_estimate=pl.CostEstimate(flops=0, bytes_accessed=COST, transcendentals=0),
         name=name,
     )(*arrays)
 
@@ -485,15 +594,17 @@
             ((pl.ds(0, half), slice(None)), (half, columns), ("p", "y")),
             ((pl.ds(half, half), slice(None)), (half, columns), ("y", "p")),
         ]
-    if kind == "seq":
-        return ("h", "p", "y"), [((slice(None), slice(None)), tail, ("y", "p", "h"))]
+    if kind in ("seq", "seq_turned"):
+        order = ("y", "p", "h") if kind == "seq" else ("p", "y", "h")
+        return ("h", "p", "y"), [((slice(None), slice(None)), tail, order)]
     names = ("h", "p", "y", "x")
     if columns % 256:
         return names, [((slice(None), slice(None)), tail, ("x", "y", "p", "h"))]
-    half = columns // 2
+    count = 4 if columns % 512 == 0 else 2
+    step = columns // count
+    orders = (("x", "y", "p", "h"), ("y", "x", "p", "h")) if kind == "all" else (("x", "y", "p", "h"),) * 2
     return names, [
-        ((slice(None), pl.ds(0, half)), (rows, half), ("x", "y", "p", "h")),
-        ((slice(None), pl.ds(half, half)), (rows, half), ("y", "x", "p", "h")),
+        ((slice(None), pl.ds(i * step, step)), (rows, step), orders[i % 2]) for i in range(count)
     ]
 
 
@@ -516,7 +627,7 @@
     place = {name: lax.axis_index(name) for name in ("h", "p", "y", "x")}
     ic = lax.axis_index("c")
     length = {"h": far, "p": 2, "y": 2, "x": fsdp}
-    core_dim = {"group": 2, "seq": 3, "all": 3}[kind]
+    core_dim = 2 if kind == "group" else 3
     names, parts = reduce_plan(kind, far, fsdp, out.shape)
     jobs, position = [], 0
     for cut, small, order in parts:
@@ -529,7 +640,7 @@
         return source.at[tuple(lead) + cut]
 
     def add(sums, brought, fixed, left, target=None, also=()):
-        sizes = [1 if n in fixed_now else length[n] for n in left for fixed_now in (also,)]
+        sizes = [1 if n in also else length[n] for n in left]
         total = 1
         for size in sizes:
             total *= size
@@ -611,14 +722,23 @@
     scratch = refs[2 * n : -3]
     send_sems, recv_sems, local_sems = refs[-3:]
     partners = [flip("p"), flip("y"), flip("c")]
-    if set(kinds) - {"group"}:
+    if set(kinds) - {"group", "spread"}:
         partners += [other_h(far, k) for k in range(1, far)]
-    if "all" in kinds:
+    if "all" in kinds or "all_x" in kinds:
         partners.append(flip("x"))
+    if "spread" in kinds:
+        partners += corners()
     greet(partners)
     copies = Copies(send_sems, recv_sems)
     running, position = [], 0
     for i, kind in enumerate(kinds):
+        if kind == "spread":
+            me = (lax.axis_index("p") * 2 + lax.axis_index("y")) * 2 + lax.axis_index("c")
+            local = pltpu.make_async_copy(
+                sources[i].at[me], outs[i].at[me], local_sems.at[i, 0]
+            )
+            running.append(spread_steps(far, copies, sources[i], outs[i], local, 1))
+            continue
         part = scratch[position : position + counts[i]]
         position += counts[i]
         running.append(
@@ -635,6 +755,11 @@
 def reduce(name, number, far, fsdp, kinds, arrays):
     shapes, scratch, counts, total = [], [], [], 0
     for kind, array in zip(kinds, arrays):
+        if kind == "spread":
+            shapes.append(jax.ShapeDtypeStruct(array.shape, array.dtype))
+            counts.append(0)
+            total += 7
+            continue
         tail = array.shape[-2:]
         parts = reduce_plan(kind, far, fsdp, tail)[1]
         own = reduce_shapes(kind, far, fsdp, tail, array.dtype)
@@ -642,20 +767,21 @@
         scratch += [pltpu.VMEM(shape, array.dtype) for shape in own]
         shapes.append(jax.ShapeDtypeStruct(tail, F32))
         total += sum(1 + len(order) + (far - 2 if "h" in order else 0) for _, _, order in parts)
-    size = sum(a.size * a.dtype.itemsize for a in arrays)
     return pl.pallas_call(
         functools.partial(reduce_kernel, kinds, far, fsdp, tuple(counts)),
         out_shape=tuple(shapes),
         in_specs=[ANY] * len(arrays),
-        out_specs=tuple([pl.BlockSpec(memory_space=pltpu.VMEM)] * len(arrays)),
+        out_specs=tuple(
+            ANY if kind == "spread" else pl.BlockSpec(memory_space=pltpu.VMEM) for kind in kinds
+        ),
         scratch_shapes=scratch
         + [
             pltpu.SemaphoreType.DMA((total,)),
             pltpu.SemaphoreType.DMA((total,)),
-            pltpu.SemaphoreType.DMA((len(arrays), 2)),
+            pltpu.SemaphoreType.DMA((len(arrays), 4)),
         ],
         compiler_params=pltpu.CompilerParams(collective_id=number, has_side_effects=True),
-        cost_estimate=pl.CostEstimate(flops=0, bytes_accessed=8 * size, transcendentals=0),
+        cost_estimate=pl.CostEstimate(flops=0, bytes_accessed=COST, transcendentals=0),
         name=name,
     )(*arrays)
 
@@ -699,9 +825,7 @@
 
     slice_width = hidden_width // 8
 
-    def slices(matrix):
-        parts = matrix.reshape(shard, far, 8, hidden_width // (8 * far))
-        return parts.transpose(2, 0, 1, 3).reshape(8, shard, slice_width)
+    gate_cut, up_cut = cut_columns(far, False, (gate_weight, up_weight))
 
     vectors = jnp.concatenate(
         [attn_gain, query_bias, key_bias_vector, value_bias_vector, mlp_gain]
@@ -714,10 +838,10 @@
         fsdp,
         ("all", "all", "spread", "spread", "pair"),
         (
-            jnp.concatenate([key_matrix, value_matrix, query_weight], axis=1),
+            jnp.concatenate([query_weight, key_matrix, value_matrix], axis=1),
             vectors,
-            slices(gate_weight),
-            slices(up_weight),
+            gate_cut,
+            up_cut,
             down_weight,
         ),
     )
@@ -755,40 +879,27 @@
     normed, recip_one = rms_forward(rows, gain_attn)
     normed_low = normed.astype(BF16)
     pre = mat_dot(normed_low, w_qkv)
-    kv_pre = pre[:, : 2 * kv_width]
-    key_rotated = apply_rotary(
-        (kv_pre[:, :kv_width] + b_key).reshape(-1, KEY_VALUE_HEADS, HEAD_WIDTH),
-        cosine_table,
-        sine_table,
-    ).reshape(-1, kv_width)
-    own_kv = jnp.concatenate([key_rotated, kv_pre[:, kv_width:] + b_value], axis=1).astype(BF16)
+    heads = range(QUERY_HEADS + KEY_VALUE_HEADS)
+    splits = ((0, micro * token_rows, 0, width),) + tuple(
+        (m * token_rows, token_rows, width, 2 * kv_width) for m in range(micro)
+    )
+    biases = jnp.concatenate([b_query, b_key, b_value])[None]
+    query_rotated, *own_kv = rotate(pre, biases, cosine_table, sine_table, heads, splits, 1.0)
     moved = move(
         "gather_second",
         1,
         far,
         fsdp,
-        ("seq",) * micro + ("all", "pair8", "pair8", "group"),
-        tuple(own_kv[m * token_rows : (m + 1) * token_rows] for m in range(micro))
-        + (output_weight, gate_parts, up_parts, upstream_low),
+        ("seq",) * micro + ("all_y", "pair8", "pair8", "group"),
+        tuple(own_kv) + (output_weight, gate_parts, up_parts, upstream_low),
     )
     stacks = [part.reshape(seq, token_rows, 2 * kv_width) for part in moved[:micro]]
     w_output = moved[micro].reshape(width, width)
     w_gate, w_up = (part.reshape(width, slice_width) for part in moved[micro + 1 : micro + 3])
     upstream_all = moved[micro + 3].reshape(-1, width)
-    query_rotated = (
-        apply_rotary(
-            (pre[:, 2 * kv_width :] + b_query).reshape(-1, QUERY_HEADS, HEAD_WIDTH),
-            cosine_table,
-            sine_table,
-        )
-        .astype(BF16)
-        .reshape(-1, width)
-    )
-
     attended, lses = [], []
     for m in range(micro):
-        part = slice(m * token_rows, (m + 1) * token_rows)
-        result, lse = attend_forward(metas[m], query_rotated[part], stacks[m], spans[m])
+        result, lse = attend_forward(m, metas[m], query_rotated, stacks[m], spans[m])
         attended.append(result)
         lses.append(lse)
     attended = jnp.concatenate(attended, axis=0)
@@ -806,114 +917,131 @@
     grad_gate = (grad_hidden * up_pre * sigma * (1.0 + gate_pre * (1.0 - sigma))).astype(BF16)
     grad_up = (grad_hidden * activated).astype(BF16)
     group = (2, 2, 2, micro * token_rows, width)
-    grad_two = (cols_dot(grad_gate, w_gate) + cols_dot(grad_up, w_up)).astype(BF16)
-    final = mat_dot(hidden, w_down).astype(BF16)
-
-    def paired(grad, axis):
+
+    def over_x(grad, axis, other):
         grad = grad.astype(BF16)
-        kept = pick(grad, ix, axis).astype(F32) + hop(pick(grad, 1 - ix, axis), "x").astype(F32)
-        kept = kept.astype(BF16)
+        sent, other = lax.optimization_barrier((pick(grad, 1 - ix, axis), other))
+        kept = pick(grad, ix, axis).astype(F32) + hop(sent, "x").astype(F32)
+        return kept.astype(BF16), other
+
+    def over_h(kept):
         total = pick(kept, ih, 0).astype(F32)
         for k in range(1, far):
             total = total + hop(pick(kept, (ih + k) % far, 0), "h", k).astype(F32)
         return total
 
     eight = (far, 8, fsdp, shard, slice_width)
-    gate_sum = paired(rows_dot(tokens, grad_gate).reshape(eight), 2).astype(BF16)
-    up_sum = paired(rows_dot(tokens, grad_up).reshape(eight), 2).astype(BF16)
-    down_part = paired(rows_dot(hidden, upstream_all).reshape(far, fsdp, -1, width), 1)
+    down_part, _ = over_x(
+        rows_dot(hidden, upstream_all).reshape(far, fsdp, -1, width), 1, upstream_all
+    )
+    gate_sum, grad_up_last = over_x(rows_dot(tokens, grad_gate).reshape(eight), 2, grad_up)
+    up_sum = over_x(rows_dot(tokens, grad_up_last).reshape(eight), 2, ())[0]
+    grad_two = (cols_dot(grad_gate, w_gate) + cols_dot(grad_up, w_up)).astype(BF16)
 
     (grad_two,) = reduce("reduce_tokens", 3, far, fsdp, ("group",), (grad_two.reshape(group),))
     grad_norm, gain_mlp_sum = rms_backward(middle, recip_two, gain_mlp, grad_two)
     grad_middle = upstream_low.astype(F32) + grad_norm
     grad_branch = grad_middle.astype(BF16)
+    grad_branch, gate_sum, up_sum, hidden = lax.optimization_barrier(
+        (grad_branch, gate_sum, up_sum, hidden)
+    )
+    final = mat_dot(hidden, w_down).astype(BF16)
+    gate_sum = over_h(gate_sum).astype(BF16)
+    up_sum = over_h(up_sum).astype(BF16)
     grad_attended = cols_dot(grad_branch, w_output).astype(BF16)
     grad_kvs, grad_query = [], []
     for m in range(micro):
-        part = slice(m * token_rows, (m + 1) * token_rows)
-        query_part, grad_keys, grad_values = attend_backward(
-            metas[m], query_rotated[part], grad_attended[part], stacks[m], spans[m], lses[m]
+        query_part, grad_kv = attend_backward(
+            m,
+            metas[m],
+            query_rotated,
+            grad_attended,
+            stacks[m],
+            spans[m],
+            lses[m],
+            cosine_table,
+            sine_table,
         )
-        stacked = jnp.concatenate([grad_keys, grad_values], axis=2)
-        grad_kvs.append(stacked.reshape(far, 2, 2, 2, token_rows, 2 * kv_width))
+        grad_kvs.append(grad_kv.reshape(far, 2, 2, 2, token_rows, 2 * kv_width))
         grad_query.append(query_part)
 
     blocks = (far, 2, 2, 2, fsdp, shard)
+    grad_kvs[0], gate_sum = lax.optimization_barrier((grad_kvs[0], gate_sum))
     g_output = rows_dot(attended, grad_branch).astype(BF16)
     reduced = reduce(
         "reduce_second",
         4,
         far,
         fsdp,
-        ("seq",) * micro + ("all", "group"),
+        tuple("seq_turned" if m % 2 else "seq" for m in range(micro)) + ("all_x", "group"),
         tuple(grad_kvs) + (g_output.reshape(blocks + (width,)), final.reshape(group)),
     )
-    grad_kvs, output_part = reduced[:micro], reduced[micro]
+    grad_kvs, output_part = list(reduced[:micro]), reduced[micro]
+    grad_kvs[0], down_part = lax.optimization_barrier((grad_kvs[0], down_part))
+    down_part = over_h(down_part)
     results = (middle + reduced[micro + 1]).astype(BF16)
-    grad_query = (
-        inverse_rotary(
-            jnp.concatenate(grad_query, axis=0).reshape(-1, QUERY_HEADS, HEAD_WIDTH),
-            cosine_table,
-            sine_table,
-        )
-        .reshape(-1, width)
-        .astype(BF16)
-    )
+    grad_query = jnp.concatenate(grad_query, axis=0)
     grad_kv = jnp.concatenate(grad_kvs, axis=0)
-    grad_key = inverse_rotary(
-        grad_kv[:, :kv_width].reshape(-1, KEY_VALUE_HEADS, HEAD_WIDTH), cosine_table, sine_table
-    ).reshape(-1, kv_width)
-    grad_kv = jnp.concatenate([grad_key, grad_kv[:, kv_width:]], axis=1).astype(BF16)
-    grad_normed = cols_dot(jnp.concatenate([grad_kv, grad_query], axis=1), w_qkv)
+    (grad_kv,) = rotate(
+        grad_kv,
+        jnp.zeros((1, 2 * kv_width), F32),
+        cosine_table,
+        sine_table,
+        range(KEY_VALUE_HEADS),
+        ((0, micro * token_rows, 0, 2 * kv_width),),
+        -1.0,
+    )
+    grad_pre = jnp.concatenate([grad_query, grad_kv], axis=1)
+    grad_normed = cols_dot(grad_pre, w_qkv)
     grad_rows, gain_attn_sum = rms_backward(rows, recip_one, gain_attn, grad_normed)
     input_grad = grad_middle + grad_rows
-    g_qkv = rows_dot(normed_low, jnp.concatenate([grad_kv, grad_query], axis=1)).astype(BF16)
-    bias_query = jnp.sum(grad_query.astype(F32), axis=0)
-    bias_kv = jnp.sum(grad_kv.astype(F32), axis=0)
+    g_qkv = rows_dot(normed_low, grad_pre).astype(BF16)
+    bias_sum = jnp.sum(grad_pre.astype(F32), axis=0)
     vector_sums = jnp.concatenate(
         [
             v.reshape(devices, -1)
             for v in (
                 gain_attn_sum,
-                bias_query,
-                bias_kv[:kv_width],
-                bias_kv[kv_width:],
+                bias_sum[:width],
+                bias_sum[width : width + kv_width],
+                bias_sum[width + kv_width :],
                 gain_mlp_sum,
             )
         ],
         axis=1,
     )
     vector_sums = jnp.pad(vector_sums, ((0, 0), (0, 1024 - vector_sums.shape[1])))
-    qkv_part, vector_part = reduce(
+    qkv_part, vector_part, gate_sum, up_sum = reduce(
         "reduce_last",
         5,
         far,
         fsdp,
-        ("all", "all"),
-        (g_qkv.reshape(blocks + (-1,)), vector_sums.reshape(far, 2, 2, 2, fsdp, 8, 128)),
-    )
-    kv_part, query_part = qkv_part[:, : 2 * kv_width], qkv_part[:, 2 * kv_width :]
+        ("all", "all", "spread", "spread"),
+        (
+            g_qkv.reshape(blocks + (-1,)),
+            vector_sums.reshape(far, 2, 2, 2, fsdp, 8, 128),
+            gate_sum,
+            up_sum,
+        ),
+    )
     vector_part = vector_part.reshape(-1)
-    gate_sum, up_sum = move("spread_last", 6, far, fsdp, ("spread", "spread"), (gate_sum, up_sum))
-
-    def joined(part):
-        part = part.reshape(8, shard, far, -1).transpose(1, 2, 0, 3)
-        return part.reshape(shard, hidden_width).astype(F32)
+
+    gate_grad, up_grad = cut_columns(far, True, (gate_sum, up_sum))
 
     return (
         results.reshape(1, micro, token_rows, width),
         input_grad.reshape(1, micro, token_rows, width),
         vector_part[cuts[0] : cuts[1]],
-        query_part,
+        qkv_part[:, :width],
         vector_part[cuts[1] : cuts[2]],
-        kv_part[:, :kv_width],
+        qkv_part[:, width : width + kv_width],
         vector_part[cuts[2] : cuts[3]],
-        kv_part[:, kv_width:],
+        qkv_part[:, width + kv_width :],
         vector_part[cuts[3] : cuts[4]],
         output_part,
         vector_part[cuts[4] : cuts[5]],
-        joined(gate_sum),
-        joined(up_sum),
+        gate_grad,
+        up_grad,
         down_part,
     )
 

time: 903 us -> 729 us (0.81)
  Pallas kernels: 519 us -> 449 us
  waiting for transfers between devices: 85.4 us -> 21.2 us
  local copies, waits for them, and re-layouts: 89.5 us -> 33.7 us
  matrix products: 144 us -> 154 us
    ppermute x3, waiting for transfers between devices: 85.4 us -> 14.9 us  [hop(): lax.ppermute(array, 'h', [(i, (i + shift) % far) for i in range(far)])]
    pallas_call x4 -> x3, Pallas kernels: 297 us -> 232 us  [move(): pl.pallas_call(functools.partial(move_kernel, kinds, far), out_shape=tupl...]
    pallas_call x3, Pallas kernels: 203 us -> 184 us  [reduce(): pl.pallas_call(functools.partial(reduce_kernel, kinds, far, fsdp, tuple(c...]
    convert_element_type x6 -> x0, local copies, waits for them, and re-layouts: 15.8 us -> none  [joined(): return part.reshape(shard, hidden_width).astype(F32)]
    convert_element_type x7, other arithmetic: 11.5 us -> 24.6 us  [the longest x1 9.64 us: body(): hidden = (activated * up_pre).astype(BF16)]
    pallas_call x0 -> x4, Pallas kernels: none -> 11.8 us  [the longest x2 6.79 us: cut_columns(): pl.pallas_call(functools.partial(cut_kernel, far, whole), out_shape=tuple...]
    unnamed x157 -> x67, local copies, waits for them, and re-layouts: 14.7 us -> 4 us
    concatenate x7 -> x1, local copies, waits for them, and re-layouts: 10.7 us -> 0.09 us  [body(): jnp.concatenate([v.reshape(devices, -1) for v in (gain_attn_sum, bias_sum...]
  transfers between devices with their start and end apart: 6 -> 6, of which waited for: 2 -> 2; matrix products, arithmetic and copies ran while one was open for 21% -> 19% of each run, Pallas kernels for 28% -> 28%
where the time goes in v3:
time: 729 us; the launch traced here: 722 us
  Pallas kernels  449 us (62%)
  matrix products  154 us (21%)
  other arithmetic  47.8 us (7%)
  local copies, waits for them, and re-layouts  33.7 us (5%)
  waiting for transfers between devices  21.2 us (3%)
  starting transfers between devices  14.3 us (2%)
    pallas_call x3, Pallas kernels, move(): pl.pallas_call(functools.partial(move_kernel, kinds, far), out_shape=tupl...  232 us
    pallas_call x3, Pallas kernels, reduce(): pl.pallas_call(functools.partial(reduce_kernel, kinds, far, fsdp, tuple(c...  184 us
    dot_general x15, matrix products, dot(): lax.dot_general(left, right, ((dims[0], dims[1]), ((), ())), preferred_el...  154 us
    ppermute x3, waiting for transfers between devices, hop(): lax.ppermute(array, 'h', [(i, (i + shift) % far) for i in range(far)])  14.9 us
  transfers between devices with their start and end apart: 6, of which 2 were waited for; matrix products, arithmetic and copies ran while one was open for 19% of the time, Pallas kernels for 28%

profile of v3, /device:TPU:0, one launch (start us, length us, event | category | flops | bytes accessed | tf_op | source)
XLA Modules:
  0.0 721.7 jit_solution(9521054954958345754)
XLA Ops:
  9.6 77.3 %gather_first.1 = (bf16[2,2,2,2,2,48,2048]{6,5,4,3,2,1,0:T(8,128)(2,1)}, f32[2,2,2,2,2,8,128]{6,5,4,3,2,1,0:T(8,128)}, bf16[8,48,1120]{2,1,0:T(8,128)(2,1)}, bf1...) custom-call(bf16[48,2048]{1,0:T(8,128)(2,1)} %pad_maximum_fusion.2.refs_0_, f32[8,128]{1,0:T(8,128)} %bitcast_convert_fusion.refs_1_, ...), custom_call_target="tpu_custom_call" | custom-call | bytes 1024 | tf_op jit(solution)/shard_map/gather_first/pallas_call | solution.py:569
  103.9 113.9 %gather_second.1 = (bf16[2,2,2,2,128,512]{5,4,3,2,1,0:T(8,128)(2,1)}, bf16[2,2,2,2,128,512]{5,4,3,2,1,0:T(8,128)(2,1)}, bf16[2,2,2,2,2,48,1536]{6,5,4,3,2,1,0:T(...) custom-call(bf16[128,512]{1,0:T(8,128)(2,1)} %get-tuple-element.64.r, ...), custom_call_target="tpu_custom_call" | custom-call | bytes 1024 | tf_op jit(solution)/shard_map/gather_second/pallas_call | solution.py:569
  233.9 40.5 %gather_tokens.1 = bf16[2,2,2,256,1536]{4,3,2,1,0:T(8,128)(2,1)} custom-call(bf16[256,1536]{1,0:T(8,128)(2,1)} %multiply_convert_fusion.3.refs_0_), custom_call_target="tpu_custom_call" | custom-call | bytes 1024 | tf_op jit(solution)/shard_map/gather_tokens/pallas_call | solution.py:569
  274.4 13.0 %fusion.51 = f32[2048,1120]{0,1:T(8,128)} fusion(bf16[2048,1536]{1,0:T(8,128)(2,1)} %bitcast.237, bf16[1120,1536]{1,0:T(8,128)(2,1)} %bitcast.245), kind=kOutput, calls=%fused_computation.127 | convolution fusion | flops 7046430720 | bytes 18907136 | tf_op jit(solution)/shard_map/dot_general | solution.py:53
  287.5 9.9 %fusion.52 = f32[2048,1120]{0,1:T(8,128)} fusion(bf16[2048,1536]{1,0:T(8,128)(2,1)S(1)} %bitcast.195, bf16[1536,1120]{1,0:T(8,128)(2,1)S(1)} %bitcast.243), kind=kOutput, calls=%fused_computation.128 | convolution fusion | flops 7046430720 | bytes 18907136 | tf_op jit(solution)/shard_map/dot_general | solution.py:53
  297.4 24.0 %multiply_convert_fusion = (bf16[2048,1120]{0,1:T(8,128)(2,1)}, bf16[2048,1120]{0,1:T(8,128)(2,1)}, bf16[2048,1120]{0,1:T(8,128)(2,1)}, f32[2048,1120]{0,1:T(8,128)}) fusion(f32[2048,1120]{0,1:T(8,128)} %fusion.52, f32[2048,1120]{0,1:T(8,128)} %fusion.51, bf16[2048,1536]{1,0:T(8,128)(2,1)} %bitcast.193, bf16[1536,1120]{1,0:T(8,128)(2,1)} %bitcast.241), kind=kOutput, calls=%fused_computation.8 | convolution fusion | flops 7080837120 | bytes 51019776 | tf_op jit(solution)/shard_map/dot_general | solution.py:53
  321.4 9.6 %fusion = bf16[1120,2048]{1,0:T(8,128)(2,1)} fusion(f32[2048,1120]{0,1:T(8,128)} %get-tuple-element.151, f32[2048,1120]{0,1:T(8,128)} %fusion.52), kind=kLoop, calls=%fused_computation.2 | loop fusion | flops 13762560 | bytes 22937600 | tf_op jit(solution)/shard_map/convert_element_type | solution.py:915
  331.0 12.1 %convolution_convert_fusion.3 = bf16[2,2,280,1536]{3,2,1,0:T(8,128)(2,1)} fusion(bf16[2,2,280,2048]{3,2,1,0:T(8,128)(2,1)} %bitcast.207, bf16[2048,1536,1,1]{1,0,3,2:T(8,128)(2,1)} %bitcast.238), kind=kOutput, calls=%fused_computation.24 | convolution fusion | flops 7048151040 | bytes 14319616 | tf_op jit(solution)/shard_map/dot_general | solution.py:53
  347.3 8.7 %copy.35 = bf16[1536,2048]{1,0:T(8,128)(2,1)} copy(bf16[1536,2048]{0,1:T(8,128)(2,1)} %bitcast.194) | data formatting | bytes 12582912 | tf_op jit(solution)/shard_map/dot_general | solution.py:53
  356.0 12.0 %fusion.11 = bf16[2,8,2,48,1120]{4,3,1,0,2:T(8,128)(2,1)S(1)} fusion(bf16[2048,1120]{0,1:T(8,128)(2,1)} %get-tuple-element.113, bf16[2,8,2,48,2048]{4,3,2,1,0:T(8,128)(2,1)} %bitcast.203), kind=kOutput, calls=%fused_computation.22 | convolution fusion | flops 7048151040 | bytes 14319616 | tf_op jit(solution)/shard_map/dot_general | solution.py:53
  369.4 11.1 %fusion.16 = bf16[2,8,2,48,1120]{4,3,1,0,2:T(8,128)(2,1)S(1)} fusion(bf16[2048,1120]{0,1:T(8,128)(2,1)} %get-tuple-element.78, bf16[2,8,2,48,2048]{4,3,2,1,0:T(8,128)(2,1)S(1)} %bitcast.204), kind=kOutput, calls=%fused_computation.23 | convolution fusion | flops 7048151040 | bytes 14319616 | tf_op jit(solution)/shard_map/dot_general | solution.py:53
  384.5 12.9 %fusion.53 = f32[2048,1536]{1,0:T(8,128)} fusion(bf16[2048,1120]{0,1:T(8,128)(2,1)} %get-tuple-element.113, bf16[1536,1120]{1,0:T(8,128)(2,1)S(1)} %bitcast.244), kind=kOutput, calls=%fused_computation.129 | convolution fusion | flops 7046430720 | bytes 20611072 | tf_op jit(solution)/shard_map/dot_general | solution.py:53
  397.5 13.9 %add_convert_fusion = bf16[2048,1536]{1,0:T(8,128)(2,1)} fusion(f32[2048,1536]{1,0:T(8,128)} %fusion.53, bf16[2048,1120]{0,1:T(8,128)(2,1)} %get-tuple-element.78, bf16[1536,1120]{1,0:T(8,128)(2,1)S(1)} %bitcast.242), kind=kOutput, calls=%fused_computation | convolution fusion | flops 7052722176 | bytes 26902528 | tf_op jit(solution)/shard_map/dot_general | solution.py:53
  411.3 37.0 %reduce_tokens.1 = f32[256,1536]{1,0:T(8,128)} custom-call(bf16[2,2,2,256,1536]{4,3,2,1,0:T(8,128)(2,1)} %bitcast.206), custom_call_target="tpu_custom_call" | custom-call | bytes 1024 | tf_op jit(solution)/shard_map/reduce_tokens/pallas_call | solution.py:770
  455.6 6.3 collective-permute-done
  472.2 6.2 attend_backward.3
  478.4 6.1 attend_backward.2
  485.5 8.8 %collective-permute-start.4 = (bf16[8,48,1120]{2,1,0:T(8,128)(2,1)}, bf16[8,48,1120]{2,1,0:T(8,128)(2,1)}, u32[]{:S(2)}, u32[]{:S(2)}) collective-permute-start(bf16[8,48,1120]{2,1,0:T(8,128)(2,1)} %dynamic-slice_bitcast_fusion.3), channel_id=1, source_target_pairs={{0,16},{16,0},{1,17},{17,1},{2,18},{18,2},{3,19},{19,3},{4,20},{20... | collective-permute-start | bytes 2580488 | tf_op jit(solution)/shard_map/ppermute | solution.py:820
  494.4 13.6 %convolution_convert_fusion = bf16[2048,1536]{1,0:T(8,128)(2,1)} fusion(bf16[2048,1120]{0,1:T(8,128)(2,1)} %get-tuple-element.86, bf16[1120,1536]{1,0:T(8,128)(2,1)} %bitcast.246), kind=kOutput, calls=%fused_computation.13 | convolution fusion | flops 7049576448 | bytes 14319616 | tf_op jit(solution)/shard_map/dot_general | solution.py:53
  514.8 14.9 %collective-permute-done.2 = bf16[8,48,1120]{2,1,0:T(8,128)(2,1)} collective-permute-done((bf16[8,48,1120]{2,1,0:T(8,128)(2,1)}, bf16[8,48,1120]{2,1,0:T(8,128)(2,1)}, u32[]{:S(2)}, u32[]{:S(2)}) %collective-permute-start.2) | collective-permute-done | bytes 860192 | tf_op jit(solution)/shard_map/ppermute | solution.py:820
  532.1 81.1 %reduce_second.1 = (f32[128,512]{1,0:T(8,128)}, f32[128,512]{1,0:T(8,128)}, f32[48,1536]{1,0:T(8,128)}, f32[256,1536]{1,0:T(8,128)}) custom-call(bf16[2,2,2,2,128,512]{5,4,3,2,1,0:T(8,128)(2,1)} %bitcast.210, bf16[2,2,2,2,128,512]{5,4,3,2,1,0:T(8,128)(2,1)} %bitcast.209, bf16[2,2,2,2,2,48,1536]{6,5,4,3,2,1,0:T(8,128)(2,1)} %bitcast.192, ...), custom_call_target="tpu_custom_call" | custom-call | bytes 1024 | tf_op jit(solution)/shard_map/reduce_second/pallas_call | solution.py:770
  621.4 6.7 fusion.36
  629.0 5.9 convolution_convert_fusion.1
  637.2 66.0 %reduce_last.1 = (f32[48,2048]{1,0:T(8,128)}, f32[8,128]{1,0:T(8,128)}, bf16[8,48,1120]{2,1,0:T(8,128)(2,1)}, bf16[8,48,1120]{2,1,0:T(8,128)(2,1)}) custom-call(bf16[2,2,2,2,2,48,2048]{6,5,4,3,2,1,0:T(8,128)(2,1)} %bitcast.191, f32[2,2,2,2,2,8,128]{6,5,4,3,2,1,0:T(8,128)} %bitcast.214, bf16[8,48,1120]{2,1,0:T(8,128)(2,1)} %fusion.25.refs_2_, ...), custom_call_target="tpu_custom_call" | custom-call | bytes 1024 | tf_op jit(solution)/shard_map/reduce_last/pallas_call | solution.py:770
  (154 shorter events, 108.1 us)
Async XLA Ops:
  0.6 87.4 %copy-start.23 = (s32[1,2,4]{2,1,0:T(2,128)S(1)}, s32[1,2,4]{2,1,0:T(2,128)}, u32[]{:S(2)}) copy-start(s32[1,2,4]{2,1,0:T(2,128)} %param.16) | copy-start | bytes 100
  0.7 88.6 %copy-start.4 = (bf16[1,2,128,1536]{3,2,1,0:T(8,128)(2,1)S(1)}, bf16[1,2,128,1536]{3,2,1,0:T(8,128)(2,1)}, u32[]{:S(2)}) copy-start(bf16[1,2,128,1536]{3,2,1,0:T(8,128)(2,1)} %param.15) | copy-start | bytes 2359300
  89.2 9.6 %copy-start.19 = (f32[1536]{0:T(1024)}, f32[1536]{0:T(1024)S(1)}, u32[]{:S(2)}) copy-start(f32[1536]{0:T(1024)S(1)} %mul.240) | copy-start | bytes 18436
  274.4 13.1 %copy-start = (bf16[2,2,2,256,1536]{4,3,2,1,0:T(8,128)(2,1)S(1)}, bf16[2,2,2,256,1536]{4,3,2,1,0:T(8,128)(2,1)}, u32[]{:S(2)}) copy-start(bf16[2,2,2,256,1536]{4,3,2,1,0:T(8,128)(2,1)} %gather_tokens.1) | copy-start | bytes 18874372
  274.4 13.1 %copy-start.26 = (bf16[2,8,2,48,1120]{4,3,2,1,0:T(8,128)(2,1)S(1)}, bf16[2,8,2,48,1120]{4,3,2,1,0:T(8,128)(2,1)}, u32[]{:S(2)}) copy-start(bf16[2,8,2,48,1120]{4,3,2,1,0:T(8,128)(2,1)} %get-tuple-element.76) | copy-start | bytes 10321924
  345.9 165.7 %collective-permute-start.3 = (bf16[2,280,1536]{2,1,0:T(8,128)(2,1)}, bf16[2,280,1536]{2,1,0:T(8,128)(2,1)}, u32[]{:S(2)}, u32[]{:S(2)}) collective-permute-start(bf16[2,280,1536]{2,1,0:T(8,128)(2,1)} %dynamic-slice_bitcast_fusion.2), channel_id=1, source_target_pairs={{0,1},{1,0},{2,3},{3,2},{4,5},{5,4},{6,7},{7,6},{8,9},{9,8},{10,11... | collective-permute-start | bytes 5160968 | tf_op jit(solution)/shard_map/ppermute | solution.py:821
  356.0 13.5 %copy-start.7 = (bf16[1536,2048]{1,0:T(8,128)(2,1)S(1)}, bf16[1536,2048]{1,0:T(8,128)(2,1)}, u32[]{:S(2)}) copy-start(bf16[1536,2048]{1,0:T(8,128)(2,1)} %copy.35) | copy-start | bytes 18874372
  368.0 12.6 %copy-start.8 = (bf16[2,8,2,48,1120]{4,3,1,0,2:T(8,128)(2,1)}, bf16[2,8,2,48,1120]{4,3,1,0,2:T(8,128)(2,1)S(1)}, u32[]{:S(2)}) copy-start(bf16[2,8,2,48,1120]{4,3,1,0,2:T(8,128)(2,1)S(1)} %fusion.11) | copy-start | bytes 10321924
  380.6 16.9 %copy-start.10 = (bf16[2,8,2,48,1120]{4,3,1,0,2:T(8,128)(2,1)}, bf16[2,8,2,48,1120]{4,3,1,0,2:T(8,128)(2,1)S(1)}, u32[]{:S(2)}) copy-start(bf16[2,8,2,48,1120]{4,3,1,0,2:T(8,128)(2,1)S(1)} %fusion.16) | copy-start | bytes 10321924
  382.0 15.5 %copy-start.25 = (bf16[2,8,2,48,1120]{4,3,2,1,0:T(8,128)(2,1)S(1)}, bf16[2,8,2,48,1120]{4,3,2,1,0:T(8,128)(2,1)}, u32[]{:S(2)}) copy-start(bf16[2,8,2,48,1120]{4,3,2,1,0:T(8,128)(2,1)} %get-tuple-element.75) | copy-start | bytes 10321924
  382.0 71.4 %collective-permute-start.1 = (bf16[2,8,48,1120]{3,2,1,0:T(8,128)(2,1)}, bf16[2,8,48,1120]{3,2,1,0:T(8,128)(2,1)}, u32[]{:S(2)}, u32[]{:S(2)}) collective-permute-start(bf16[2,8,48,1120]{3,2,1,0:T(8,128)(2,1)} %dynamic-slice_bitcast_fusion), channel_id=1, source_target_pairs={{0,1},{1,0},{2,3},{3,2},{4,5},{5,4},{6,7},{7,6},{8,9},{9,8},{10,11... | collective-permute-start | bytes 5160968 | tf_op jit(solution)/shard_map/ppermute | solution.py:821
  382.6 79.3 %collective-permute-start = (bf16[2,8,48,1120]{3,2,1,0:T(8,128)(2,1)}, bf16[2,8,48,1120]{3,2,1,0:T(8,128)(2,1)}, u32[]{:S(2)}, u32[]{:S(2)}) collective-permute-start(bf16[2,8,48,1120]{3,2,1,0:T(8,128)(2,1)} %dynamic-slice_bitcast_fusion.1), channel_id=1, source_target_pairs={{0,1},{1,0},{2,3},{3,2},{4,5},{5,4},{6,7},{7,6},{8,9},{9,8},{10,11... | collective-permute-start | bytes 5160968 | tf_op jit(solution)/shard_map/ppermute | solution.py:821
  411.3 39.0 %copy-start.22 = (f32[2,128]{1,0:T(2,128)S(1)}, f32[2,128]{1,0:T(2,128)}, u32[]{:S(2)}) copy-start(f32[2,128]{1,0:T(2,128)} %copy-done.21) | copy-start | bytes 3076
  453.3 10.5 %copy-start.15 = (bf16[256,1536]{1,0:T(8,128)(2,1)}, bf16[256,1536]{1,0:T(8,128)(2,1)S(1)}, u32[]{:S(2)}) copy-start(bf16[256,1536]{1,0:T(8,128)(2,1)S(1)} %get-tuple-element.79) | copy-start | bytes 2359300
  453.3 8.6 %copy-start.9 = (bf16[2,8,2,48,1120]{4,3,1,0,2:T(8,128)(2,1)S(1)}, bf16[2,8,2,48,1120]{4,3,1,0,2:T(8,128)(2,1)}, u32[]{:S(2)}) copy-start(bf16[2,8,2,48,1120]{4,3,1,0,2:T(8,128)(2,1)} %copy-done.8) | copy-start | bytes 10321924
  470.2 59.6 %collective-permute-start.2 = (bf16[8,48,1120]{2,1,0:T(8,128)(2,1)}, bf16[8,48,1120]{2,1,0:T(8,128)(2,1)}, u32[]{:S(2)}, u32[]{:S(2)}) collective-permute-start(bf16[8,48,1120]{2,1,0:T(8,128)(2,1)} %dynamic-slice_bitcast_fusion.4), channel_id=1, source_target_pairs={{0,16},{16,0},{1,17},{17,1},{2,18},{18,2},{3,19},{19,3},{4,20},{20... | collective-permute-start | bytes 2580488 | tf_op jit(solution)/shard_map/ppermute | solution.py:820
  485.5 22.4 %copy-start.14 = (bf16[256,1536]{1,0:T(8,128)(2,1)S(1)}, bf16[256,1536]{1,0:T(8,128)(2,1)}, u32[]{:S(2)}) copy-start(bf16[256,1536]{1,0:T(8,128)(2,1)} %copy-done.13) | copy-start | bytes 2359300
  485.5 22.4 %copy-start.16 = (bf16[256,1536]{1,0:T(8,128)(2,1)S(1)}, bf16[256,1536]{1,0:T(8,128)(2,1)}, u32[]{:S(2)}) copy-start(bf16[256,1536]{1,0:T(8,128)(2,1)} %copy-done.15) | copy-start | bytes 2359300
  485.5 149.4 %collective-permute-start.4 = (bf16[8,48,1120]{2,1,0:T(8,128)(2,1)}, bf16[8,48,1120]{2,1,0:T(8,128)(2,1)}, u32[]{:S(2)}, u32[]{:S(2)}) collective-permute-start(bf16[8,48,1120]{2,1,0:T(8,128)(2,1)} %dynamic-slice_bitcast_fusion.3), channel_id=1, source_target_pairs={{0,16},{16,0},{1,17},{17,1},{2,18},{18,2},{3,19},{19,3},{4,20},{20... | collective-permute-start | bytes 2580488 | tf_op jit(solution)/shard_map/ppermute | solution.py:820
  511.6 18.1 %copy-start.3 = (bf16[2,8,48,1120]{3,2,1,0:T(8,128)(2,1)S(1)}, bf16[2,8,48,1120]{3,2,1,0:T(8,128)(2,1)}, u32[]{:S(2)}) copy-start(bf16[2,8,48,1120]{3,2,1,0:T(8,128)(2,1)} %copy-done.2) | copy-start | bytes 5160964
  613.2 8.2 %copy-start.20 = (f32[1536]{0:T(1024)S(1)}, f32[1536]{0:T(1024)}, u32[]{:S(2)}) copy-start(f32[1536]{0:T(1024)} %copy-done.19) | copy-start | bytes 18436
  613.2 8.2 %copy-start.24 = (f32[256]{0:T(256)S(1)}, f32[256]{0:T(256)}, u32[]{:S(2)}) copy-start(f32[256]{0:T(256)} %get-tuple-element.132) | copy-start | bytes 3076
  615.4 102.5 %collective-permute-start.5 = (bf16[280,1536]{1,0:T(8,128)(2,1)}, bf16[280,1536]{1,0:T(8,128)(2,1)}, u32[]{:S(2)}, u32[]{:S(2)}) collective-permute-start(bf16[280,1536]{1,0:T(8,128)(2,1)} %dynamic-slice_bitcast_fusion.5), channel_id=1, source_target_pairs={{0,16},{16,0},{1,17},{17,1},{2,18},{18,2},{3,19},{19,3},{4,20},{20... | collective-permute-start | bytes 2580488 | tf_op jit(solution)/shard_map/ppermute | solution.py:820
  703.2 11.2 %copy-start.5 = (bf16[1,2,128,1536]{3,2,1,0:T(8,128)(2,1)S(1)}, bf16[1,2,128,1536]{3,2,1,0:T(8,128)(2,1)}, u32[]{:S(2)}) copy-start(bf16[1,2,128,1536]{3,2,1,0:T(8,128)(2,1)} %param.15) | copy-start | bytes 2359300
  (10 other events, 39.1 us)

commit v4 on v3

--- a/solution.py
+++ b/solution.py
@@ -222,6 +222,67 @@
         ),
         name="attend_backward",
     )(meta, queries, grads, stack, span, lse, cosine, sine)
+
+
+def hidden_kernel(
+    token_ref,
+    grad_ref,
+    gate_ref,
+    up_ref,
+    down_ref,
+    token_turned_ref,
+    hidden_ref,
+    turned_ref,
+    dgate_ref,
+    dup_ref,
+):
+    tokens = token_ref[...]
+    token_turned_ref[...] = tokens.T
+    gate_pre = mat_dot(tokens, gate_ref[...])
+    up_pre = mat_dot(tokens, up_ref[...])
+    grad_hidden = cols_dot(grad_ref[...], down_ref[...])
+    sigma = jax.nn.sigmoid(gate_pre)
+    activated = gate_pre * sigma
+    hidden = activated * up_pre
+    hidden_ref[...] = hidden.astype(BF16)
+    turned_ref[...] = hidden.T.astype(BF16)
+    dgate_ref[...] = (grad_hidden * up_pre * sigma * (1.0 + gate_pre * (1.0 - sigma))).astype(BF16)
+    dup_ref[...] = (grad_hidden * activated).astype(BF16)
+
+
+def hidden_units(rows, tokens, grads, w_gate, w_up, w_down):
+    total, width = tokens.shape
+    units = w_gate.shape[1]
+
+    def tile(columns):
+        return pl.BlockSpec((rows, columns), lambda i: (i, 0))
+
+    def fixed(array):
+        return pl.BlockSpec(array.shape, lambda i: (0, 0))
+
+    return pl.pallas_call(
+        hidden_kernel,
+        grid=(total // rows,),
+        in_specs=[tile(width), tile(width), fixed(w_gate), fixed(w_up), fixed(w_down)],
+        out_specs=[
+            pl.BlockSpec((width, rows), lambda i: (0, i)),
+            tile(units),
+            pl.BlockSpec((units, rows), lambda i: (0, i)),
+            tile(units),
+            tile(units),
+        ],
+        out_shape=(
+            jax.ShapeDtypeStruct((width, total), BF16),
+            jax.ShapeDtypeStruct((total, units), BF16),
+            jax.ShapeDtypeStruct((units, total), BF16),
+            jax.ShapeDtypeStruct((total, units), BF16),
+            jax.ShapeDtypeStruct((total, units), BF16),
+        ),
+        cost_estimate=pl.CostEstimate(
+            flops=6 * total * width * units, bytes_accessed=8 * total * width, transcendentals=0
+        ),
+        name="hidden_units",
+    )(tokens, grads, w_gate, w_up, w_down)
 
 
 def rotate_kernel(turned_heads, splits, sign, pre_ref, bias_ref, cos_ref, sin_ref, *outs):
@@ -908,14 +969,9 @@
     (tokens,) = move("gather_tokens", 2, far, fsdp, ("group",), (normed_two.astype(BF16),))
     tokens = tokens.reshape(-1, width)
 
-    gate_pre = mat_dot(tokens, w_gate)
-    up_pre = mat_dot(tokens, w_up)
-    sigma = jax.nn.sigmoid(gate_pre)
-    activated = gate_pre * sigma
-    hidden = (activated * up_pre).astype(BF16)
-    grad_hidden = cols_dot(upstream_all, w_down)
-    grad_gate = (grad_hidden * up_pre * sigma * (1.0 + gate_pre * (1.0 - sigma))).astype(BF16)
-    grad_up = (grad_hidden * activated).astype(BF16)
+    tokens_turned, hidden, hidden_turned, grad_gate, grad_up = hidden_units(
+        micro * token_rows, tokens, upstream_all, w_gate, w_up, w_down
+    )
     group = (2, 2, 2, micro * token_rows, width)
 
     def over_x(grad, axis, other):
@@ -931,21 +987,16 @@
         return total
 
     eight = (far, 8, fsdp, shard, slice_width)
-    down_part, _ = over_x(
-        rows_dot(hidden, upstream_all).reshape(far, fsdp, -1, width), 1, upstream_all
-    )
-    gate_sum, grad_up_last = over_x(rows_dot(tokens, grad_gate).reshape(eight), 2, grad_up)
-    up_sum = over_x(rows_dot(tokens, grad_up_last).reshape(eight), 2, ())[0]
+    turned = tokens_turned.reshape(far, 8, fsdp, shard, -1)
+    gate_sum, grad_up_last = over_x(dot(turned, grad_gate, ((4,), (0,))), 2, grad_up)
+    up_sum, _ = over_x(dot(turned, grad_up_last, ((4,), (0,))), 2, ())
     grad_two = (cols_dot(grad_gate, w_gate) + cols_dot(grad_up, w_up)).astype(BF16)
 
     (grad_two,) = reduce("reduce_tokens", 3, far, fsdp, ("group",), (grad_two.reshape(group),))
     grad_norm, gain_mlp_sum = rms_backward(middle, recip_two, gain_mlp, grad_two)
     grad_middle = upstream_low.astype(F32) + grad_norm
     grad_branch = grad_middle.astype(BF16)
-    grad_branch, gate_sum, up_sum, hidden = lax.optimization_barrier(
-        (grad_branch, gate_sum, up_sum, hidden)
-    )
-    final = mat_dot(hidden, w_down).astype(BF16)
+    grad_branch, gate_sum, up_sum = lax.optimization_barrier((grad_branch, gate_sum, up_sum))
     gate_sum = over_h(gate_sum).astype(BF16)
     up_sum = over_h(up_sum).astype(BF16)
     grad_attended = cols_dot(grad_branch, w_output).astype(BF16)
@@ -966,7 +1017,13 @@
         grad_query.append(query_part)
 
     blocks = (far, 2, 2, 2, fsdp, shard)
-    grad_kvs[0], gate_sum = lax.optimization_barrier((grad_kvs[0], gate_sum))
+    grad_kvs, gate_sum, hidden, hidden_turned = lax.optimization_barrier(
+        (grad_kvs, gate_sum, hidden, hidden_turned)
+    )
+    down_part, _ = over_x(
+        mat_dot(hidden_turned, upstream_all).reshape(far, fsdp, -1, width), 1, ()
+    )
+    final = mat_dot(hidden, w_down).astype(BF16)
     g_output = rows_dot(attended, grad_branch).astype(BF16)
     reduced = reduce(
         "reduce_second",

time: 729 us -> 714 us (0.979)
  matrix products: 154 us -> 102 us
  Pallas kernels: 449 us -> 481 us
  waiting for transfers between devices: 21.2 us -> 40.5 us
  other arithmetic: 47.8 us -> 34.9 us
    dot_general x15 -> x12, matrix products: 154 us -> 102 us  [dot(): lax.dot_general(left, right, ((dims[0], dims[1]), ((), ())), preferred_el...]
    pallas_call x0 -> x1, Pallas kernels: none -> 33.3 us  [hidden_units(): pl.pallas_call(hidden_kernel, grid=(total // rows,), in_specs=[tile(width...]
    ppermute x3, waiting for transfers between devices: 14.9 us -> 33.3 us  [hop(): lax.ppermute(array, 'h', [(i, (i + shift) % far) for i in range(far)])]
    convert_element_type x1 -> x0, other arithmetic: 9.64 us -> none  [body(): hidden = (activated * up_pre).astype(BF16)]
    dot_general x1 -> x0, local copies, waits for them, and re-layouts: 8.68 us -> none  [dot(): lax.dot_general(left, right, ((dims[0], dims[1]), ((), ())), preferred_el...]
  transfers between devices with their start and end apart: 6 -> 6, of which waited for: 2 -> 2; matrix products, arithmetic and copies ran while one was open for 19% -> 14% of each run, Pallas kernels for 28% -> 29%
where the time goes in v4:
time: 714 us; the launch traced here: 707 us
  Pallas kernels  481 us (67%)
  matrix products  102 us (14%)
  waiting for transfers between devices  40.5 us (6%)
  local copies, waits for them, and re-layouts  36.5 us (5%)
  other arithmetic  34.9 us (5%)
  starting transfers between devices  11.4 us (2%)
    pallas_call x3, Pallas kernels, move(): pl.pallas_call(functools.partial(move_kernel, kinds, far), out_shape=tupl...  229 us
    pallas_call x3, Pallas kernels, reduce(): pl.pallas_call(functools.partial(reduce_kernel, kinds, far, fsdp, tuple(c...  185 us
    dot_general x12, matrix products, dot(): lax.dot_general(left, right, ((dims[0], dims[1]), ((), ())), preferred_el...  102 us
    ppermute x3, waiting for transfers between devices, hop(): lax.ppermute(array, 'h', [(i, (i + shift) % far) for i in range(far)])  33.3 us
    pallas_call x1, Pallas kernels, hidden_units(): pl.pallas_call(hidden_kernel, grid=(total // rows,), in_specs=[tile(width...  33.3 us
  transfers between devices with their start and end apart: 6, of which 2 were waited for; matrix products, arithmetic and copies ran while one was open for 14% of the time, Pallas kernels for 29%

profile of v4, /device:TPU:0, one launch (start us, length us, event | category | flops | bytes accessed | tf_op | source)
XLA Modules:
  0.0 707.4 jit_solution(880725642730447297)
XLA Ops:
  9.6 77.3 %gather_first.1 = (bf16[2,2,2,2,2,48,2048]{6,5,4,3,2,1,0:T(8,128)(2,1)}, f32[2,2,2,2,2,8,128]{6,5,4,3,2,1,0:T(8,128)}, bf16[8,48,1120]{2,1,0:T(8,128)(2,1)}, bf1...) custom-call(bf16[48,2048]{1,0:T(8,128)(2,1)} %pad_maximum_fusion.2.refs_0_, f32[8,128]{1,0:T(8,128)} %bitcast_convert_fusion.refs_1_, ...), custom_call_target="tpu_custom_call" | custom-call | bytes 1024 | tf_op jit(solution)/shard_map/gather_first/pallas_call | solution.py:630
  92.9 5.9 fusion.45.pre_ref
  103.9 113.9 %gather_second.1 = (bf16[2,2,2,2,128,512]{5,4,3,2,1,0:T(8,128)(2,1)}, bf16[2,2,2,2,128,512]{5,4,3,2,1,0:T(8,128)(2,1)}, bf16[2,2,2,2,2,48,1536]{6,5,4,3,2,1,0:T(...) custom-call(bf16[128,512]{1,0:T(8,128)(2,1)} %get-tuple-element.70.r, ...), custom_call_target="tpu_custom_call" | custom-call | bytes 1024 | tf_op jit(solution)/shard_map/gather_second/pallas_call | solution.py:630
  217.8 4.7 attend_forward.2
  223.6 4.3 attend_forward.3
  234.2 37.8 %gather_tokens.1 = bf16[2,2,2,256,1536]{4,3,2,1,0:T(8,128)(2,1)} custom-call(bf16[256,1536]{1,0:T(8,128)(2,1)} %multiply_convert_fusion.refs_0_), custom_call_target="tpu_custom_call" | custom-call | bytes 1024 | tf_op jit(solution)/shard_map/gather_tokens/pallas_call | solution.py:630
  272.0 33.3 %hidden_units.1 = (bf16[1536,2048]{1,0:T(8,128)(2,1)}, bf16[2048,1120]{1,0:T(8,128)(2,1)}, bf16[1120,2048]{1,0:T(8,128)(2,1)}, bf16[2048,1120]{1,0:T(8,128)(2,1)}, bf16[2048,1120]{1,0:T(8,128)(2,1)}) custom-call(bf16[2048,1536]{1,0:T(8,128)(2,1)} %bitcast.175, bf16[2048,1536]{1,0:T(8,128)(2,1)} %bitcast.207, bf16[1536,1120]{1,0:T(8,128)(2,1)} %bitcast.213, ...), custom_call_target="tpu_custom_call" | custom-call | flops 21139292160 | bytes 25165824 | tf_op jit(solution)/shard_map/hidden_units/pallas_call | solution.py:263
  305.3 13.0 %fusion.6 = bf16[2,8,2,48,1120]{4,3,1,0,2:T(8,128)(2,1)} fusion(bf16[2048,1120]{1,0:T(8,128)(2,1)} %get-tuple-element.83, bf16[2,8,2,48,2048]{4,3,2,1,0:T(8,128)(2,1)} %bitcast.217), kind=kOutput, calls=%fused_computation.10 | convolution fusion | flops 7048151040 | bytes 14319616 | tf_op jit(solution)/shard_map/dot_general | solution.py:53
  321.3 12.0 %fusion.11 = bf16[2,8,2,48,1120]{4,3,1,0,2:T(8,128)(2,1)S(1)} fusion(bf16[2048,1120]{1,0:T(8,128)(2,1)} %get-tuple-element.87, bf16[2,8,2,48,2048]{4,3,2,1,0:T(8,128)(2,1)} %bitcast.218), kind=kOutput, calls=%fused_computation.11 | convolution fusion | flops 7048151040 | bytes 14319616 | tf_op jit(solution)/shard_map/dot_general | solution.py:53
  340.6 11.0 %fusion.46 = f32[2048,1536]{1,0:T(8,128)} fusion(bf16[2048,1120]{1,0:T(8,128)(2,1)S(1)} %bitcast.223, bf16[1536,1120]{1,0:T(8,128)(2,1)S(1)} %bitcast.214), kind=kOutput, calls=%fused_computation.115 | convolution fusion | flops 7046430720 | bytes 20611072 | tf_op jit(solution)/shard_map/dot_general | solution.py:53
  351.6 13.8 %add_convert_fusion = bf16[2048,1536]{1,0:T(8,128)(2,1)} fusion(f32[2048,1536]{1,0:T(8,128)} %fusion.46, bf16[2048,1120]{1,0:T(8,128)(2,1)} %get-tuple-element.87, bf16[1536,1120]{1,0:T(8,128)(2,1)S(1)} %bitcast.212), kind=kOutput, calls=%fused_computation | convolution fusion | flops 7052722176 | bytes 26902528 | tf_op jit(solution)/shard_map/dot_general | solution.py:53
  365.4 37.0 %reduce_tokens.1 = f32[256,1536]{1,0:T(8,128)} custom-call(bf16[2,2,2,256,1536]{4,3,2,1,0:T(8,128)(2,1)} %bitcast.177), custom_call_target="tpu_custom_call" | custom-call | bytes 1024 | tf_op jit(solution)/shard_map/reduce_tokens/pallas_call | solution.py:831
  410.8 7.2 %collective-permute-done = bf16[2,8,48,1120]{3,2,1,0:T(8,128)(2,1)} collective-permute-done((bf16[2,8,48,1120]{3,2,1,0:T(8,128)(2,1)}, bf16[2,8,48,1120]{3,2,1,0:T(8,128)(2,1)}, u32[]{:S(2)}, u32[]{:S(2)}) %collective-permute-start) | collective-permute-done | bytes 1720352 | tf_op jit(solution)/shard_map/ppermute | solution.py:882
  422.8 4.7 convolution_convert_fusion.4.do_ref
  427.4 6.4 attend_backward.3
  433.8 6.1 attend_backward.2
  440.9 4.9 collective-permute-start.4
  449.4 33.3 %collective-permute-done.2 = bf16[8,48,1120]{2,1,0:T(8,128)(2,1)} collective-permute-done((bf16[8,48,1120]{2,1,0:T(8,128)(2,1)}, bf16[8,48,1120]{2,1,0:T(8,128)(2,1)}, u32[]{:S(2)}, u32[]{:S(2)}) %collective-permute-start.2) | collective-permute-done | bytes 860192 | tf_op jit(solution)/shard_map/ppermute | solution.py:881
  485.0 10.9 %convolution_convert_fusion.3 = bf16[2,2,280,1536]{3,2,1,0:T(8,128)(2,1)S(1)} fusion(bf16[2,2,280,2048]{3,2,1,0:T(8,128)(2,1)} %bitcast.219, bf16[2048,1536,1,1]{1,0,3,2:T(8,128)(2,1)} %bitcast.208), kind=kOutput, calls=%fused_computation.12 | convolution fusion | flops 7048151040 | bytes 14319616 | tf_op jit(solution)/shard_map/dot_general | solution.py:53
  500.3 10.2 %convolution_convert_fusion.1 = bf16[2048,1536]{1,0:T(8,128)(2,1)} fusion(bf16[2048,1120]{1,0:T(8,128)(2,1)S(1)} %bitcast.221, bf16[1120,1536]{1,0:T(8,128)(2,1)S(1)} %bitcast.216), kind=kOutput, calls=%fused_computation.2 | convolution fusion | flops 7049576448 | bytes 14319616 | tf_op jit(solution)/shard_map/dot_general | solution.py:53
  510.6 81.7 %reduce_second.1 = (f32[128,512]{1,0:T(8,128)}, f32[128,512]{1,0:T(8,128)}, f32[48,1536]{1,0:T(8,128)}, f32[256,1536]{1,0:T(8,128)}) custom-call(bf16[2,2,2,2,128,512]{5,4,3,2,1,0:T(8,128)(2,1)} %bitcast.180, bf16[2,2,2,2,128,512]{5,4,3,2,1,0:T(8,128)(2,1)} %bitcast.179, bf16[2,2,2,2,2,48,1536]{6,5,4,3,2,1,0:T(8,128)(2,1)} %bitcast.167, ...), custom_call_target="tpu_custom_call" | custom-call | bytes 1024 | tf_op jit(solution)/shard_map/reduce_second/pallas_call | solution.py:831
  607.4 6.9 fusion.31
  618.6 5.6 convolution_convert_fusion
  624.2 66.3 %reduce_last.1 = (f32[48,2048]{1,0:T(8,128)}, f32[8,128]{1,0:T(8,128)}, bf16[8,48,1120]{2,1,0:T(8,128)(2,1)}, bf16[8,48,1120]{2,1,0:T(8,128)(2,1)}) custom-call(bf16[2,2,2,2,2,48,2048]{6,5,4,3,2,1,0:T(8,128)(2,1)} %bitcast.166, f32[2,2,2,2,2,8,128]{6,5,4,3,2,1,0:T(8,128)} %bitcast.184, bf16[8,48,1120]{2,1,0:T(8,128)(2,1)} %fusion.20.refs_2_, ...), custom_call_target="tpu_custom_call" | custom-call | bytes 1024 | tf_op jit(solution)/shard_map/reduce_last/pallas_call | solution.py:831
  (164 shorter events, 97.4 us)
Async XLA Ops:
  7.8 80.2 %copy-start.23 = (s32[1,2,4]{2,1,0:T(2,128)S(1)}, s32[1,2,4]{2,1,0:T(2,128)}, u32[]{:S(2)}) copy-start(s32[1,2,4]{2,1,0:T(2,128)} %param.16) | copy-start | bytes 100
  7.8 81.4 %copy-start.3 = (bf16[1,2,128,1536]{3,2,1,0:T(8,128)(2,1)S(1)}, bf16[1,2,128,1536]{3,2,1,0:T(8,128)(2,1)}, u32[]{:S(2)}) copy-start(bf16[1,2,128,1536]{3,2,1,0:T(8,128)(2,1)} %param.15) | copy-start | bytes 2359300
  89.2 9.6 %copy-start.21 = (f32[1536]{0:T(1024)}, f32[1536]{0:T(1024)S(1)}, u32[]{:S(2)}) copy-start(f32[1536]{0:T(1024)S(1)} %mul.213) | copy-start | bytes 18436
  318.3 22.3 %slice-start.2 = ((s8[4718592]{0:T(1024)(128)(4,1)}), s8[4194304]{0:T(1024)(128)(4,1)S(1)}, s32[]{:S(2)}) async-start(s8[4718592]{0:T(1024)(128)(4,1)} %bitcast.222), calls=%async_computation.2 | async-start | bytes 8388608
  321.3 19.3 %slice-start.3 = ((s8[4718592]{0:T(1024)(128)(4,1)}), s8[524288]{0:T(1024)(128)(4,1)S(1)}, s32[]{:S(2)}) async-start(s8[4718592]{0:T(1024)(128)(4,1)} %bitcast.222), calls=%async_computation.3 | async-start | bytes 1048576
  336.4 15.2 %copy-start.27 = (bf16[2,8,2,48,1120]{4,3,2,1,0:T(8,128)(2,1)S(1)}, bf16[2,8,2,48,1120]{4,3,2,1,0:T(8,128)(2,1)}, u32[]{:S(2)}) copy-start(bf16[2,8,2,48,1120]{4,3,2,1,0:T(8,128)(2,1)} %get-tuple-element.81) | copy-start | bytes 10321924
  336.4 72.1 %collective-permute-start.1 = (bf16[2,8,48,1120]{3,2,1,0:T(8,128)(2,1)}, bf16[2,8,48,1120]{3,2,1,0:T(8,128)(2,1)}, u32[]{:S(2)}, u32[]{:S(2)}) collective-permute-start(bf16[2,8,48,1120]{3,2,1,0:T(8,128)(2,1)} %dynamic-slice_bitcast_fusion), channel_id=1, source_target_pairs={{0,1},{1,0},{2,3},{3,2},{4,5},{5,4},{6,7},{7,6},{8,9},{9,8},{10,11... | collective-permute-start | bytes 5160968 | tf_op jit(solution)/shard_map/ppermute | solution.py:882
  340.6 77.4 %collective-permute-start = (bf16[2,8,48,1120]{3,2,1,0:T(8,128)(2,1)}, bf16[2,8,48,1120]{3,2,1,0:T(8,128)(2,1)}, u32[]{:S(2)}, u32[]{:S(2)}) collective-permute-start(bf16[2,8,48,1120]{3,2,1,0:T(8,128)(2,1)} %dynamic-slice_bitcast_fusion.1), channel_id=1, source_target_pairs={{0,1},{1,0},{2,3},{3,2},{4,5},{5,4},{6,7},{7,6},{8,9},{9,8},{10,11... | collective-permute-start | bytes 5160968 | tf_op jit(solution)/shard_map/ppermute | solution.py:882
  408.5 14.3 %copy-start.12 = (bf16[256,1536]{1,0:T(8,128)(2,1)}, bf16[256,1536]{1,0:T(8,128)(2,1)S(1)}, u32[]{:S(2)}) copy-start(bf16[256,1536]{1,0:T(8,128)(2,1)S(1)} %get-tuple-element.88) | copy-start | bytes 2359300
  408.5 9.5 %copy-start.5 = (bf16[2,8,2,48,1120]{4,3,1,0,2:T(8,128)(2,1)S(1)}, bf16[2,8,2,48,1120]{4,3,1,0,2:T(8,128)(2,1)}, u32[]{:S(2)}) copy-start(bf16[2,8,2,48,1120]{4,3,1,0,2:T(8,128)(2,1)} %fusion.6) | copy-start | bytes 10321924
  422.1 60.6 %collective-permute-start.2 = (bf16[8,48,1120]{2,1,0:T(8,128)(2,1)}, bf16[8,48,1120]{2,1,0:T(8,128)(2,1)}, u32[]{:S(2)}, u32[]{:S(2)}) collective-permute-start(bf16[8,48,1120]{2,1,0:T(8,128)(2,1)} %dynamic-slice_bitcast_fusion.4), channel_id=1, source_target_pairs={{0,16},{16,0},{1,17},{17,1},{2,18},{18,2},{3,19},{19,3},{4,20},{20... | collective-permute-start | bytes 2580488 | tf_op jit(solution)/shard_map/ppermute | solution.py:881
  439.9 5.9 copy-start.13
  440.9 41.8 %copy-start.2 = (bf16[2,8,48,1120]{3,2,1,0:T(8,128)(2,1)S(1)}, bf16[2,8,48,1120]{3,2,1,0:T(8,128)(2,1)}, u32[]{:S(2)}) copy-start(bf16[2,8,48,1120]{3,2,1,0:T(8,128)(2,1)} %copy-done.1) | copy-start | bytes 5160964
  440.9 151.4 %collective-permute-start.4 = (bf16[8,48,1120]{2,1,0:T(8,128)(2,1)}, bf16[8,48,1120]{2,1,0:T(8,128)(2,1)}, u32[]{:S(2)}, u32[]{:S(2)}) collective-permute-start(bf16[8,48,1120]{2,1,0:T(8,128)(2,1)} %dynamic-slice_bitcast_fusion.3), channel_id=1, source_target_pairs={{0,16},{16,0},{1,17},{17,1},{2,18},{18,2},{3,19},{19,3},{4,20},{20... | collective-permute-start | bytes 2580488 | tf_op jit(solution)/shard_map/ppermute | solution.py:881
  445.8 54.0 %slice-start = ((s8[4718592]{0:T(1024)(128)(4,1)}), s8[4194304]{0:T(1024)(128)(4,1)S(1)}, s32[]{:S(2)}) async-start(s8[4718592]{0:T(1024)(128)(4,1)} %bitcast.220), calls=%async_computation | async-start | bytes 8388608
  485.0 14.9 %slice-start.1 = ((s8[4718592]{0:T(1024)(128)(4,1)}), s8[524288]{0:T(1024)(128)(4,1)S(1)}, s32[]{:S(2)}) async-start(s8[4718592]{0:T(1024)(128)(4,1)} %bitcast.220), calls=%async_computation.1 | async-start | bytes 1048576
  499.0 96.8 %collective-permute-start.3 = (bf16[2,280,1536]{2,1,0:T(8,128)(2,1)}, bf16[2,280,1536]{2,1,0:T(8,128)(2,1)}, u32[]{:S(2)}, u32[]{:S(2)}) collective-permute-start(bf16[2,280,1536]{2,1,0:T(8,128)(2,1)} %dynamic-slice_bitcast_fusion.2), channel_id=1, source_target_pairs={{0,1},{1,0},{2,3},{3,2},{4,5},{5,4},{6,7},{7,6},{8,9},{9,8},{10,11... | collective-permute-start | bytes 5160968 | tf_op jit(solution)/shard_map/ppermute | solution.py:882
  598.9 8.5 %copy-start.4 = (bf16[1,2,128,1536]{3,2,1,0:T(8,128)(2,1)S(1)}, bf16[1,2,128,1536]{3,2,1,0:T(8,128)(2,1)}, u32[]{:S(2)}) copy-start(bf16[1,2,128,1536]{3,2,1,0:T(8,128)(2,1)} %param.15) | copy-start | bytes 2359300
  599.9 103.6 %collective-permute-start.5 = (bf16[280,1536]{1,0:T(8,128)(2,1)}, bf16[280,1536]{1,0:T(8,128)(2,1)}, u32[]{:S(2)}, u32[]{:S(2)}) collective-permute-start(bf16[280,1536]{1,0:T(8,128)(2,1)} %dynamic-slice_bitcast_fusion.5), channel_id=1, source_target_pairs={{0,16},{16,0},{1,17},{17,1},{2,18},{18,2},{3,19},{19,3},{4,20},{20... | collective-permute-start | bytes 2580488 | tf_op jit(solution)/shard_map/ppermute | solution.py:881
  607.4 11.2 %copy-start.14 = (bf16[256,512]{1,0:T(8,128)(2,1)S(1)}, bf16[256,512]{1,0:T(8,128)(2,1)}, u32[]{:S(2)}) copy-start(bf16[256,512]{1,0:T(8,128)(2,1)} %rotate.3) | copy-start | bytes 786436
  624.2 69.2 %copy-start.26 = (f32[256]{0:T(256)S(1)}, f32[256]{0:T(256)}, u32[]{:S(2)}) copy-start(f32[256]{0:T(256)} %get-tuple-element.119) | copy-start | bytes 3076
  690.6 9.6 %copy-start.22 = (f32[1536]{0:T(1024)S(1)}, f32[1536]{0:T(1024)}, u32[]{:S(2)}) copy-start(f32[1536]{0:T(1024)} %copy-done.21) | copy-start | bytes 18436
  690.6 9.5 %copy-start.24 = (f32[256]{0:T(256)S(1)}, f32[256]{0:T(256)}, u32[]{:S(2)}) copy-start(f32[256]{0:T(256)} %get-tuple-element.141) | copy-start | bytes 3076
  690.6 9.5 %copy-start.25 = (f32[256]{0:T(256)S(1)}, f32[256]{0:T(256)}, u32[]{:S(2)}) copy-start(f32[256]{0:T(256)} %multiply_multiply_fusion) | copy-start | bytes 3076
  (16 other events, 57.0 us)

commit v5 on v4

--- a/solution.py
+++ b/solution.py
@@ -339,7 +339,7 @@
 
 
 MESH = pl.DeviceIdType.MESH
-PARTS, AHEAD = 4, 2
+PARTS = {"pair": 4, "pair8": 8}
 COST = 1024
 ANY = pl.BlockSpec(memory_space=pl.ANY)
 
@@ -512,11 +512,12 @@
             arrived.append([copies.start(parts[i], target, other_h(far, k)) for k in range(1, far)])
             sent.append(copies.start(parts[i], target, flip("x")))
 
-    for i in range(AHEAD):
+    ahead = len(parts) // 2
+    for i in range(ahead):
         send(i)
     for i in range(len(parts)):
         yield
-        send(i + AHEAD)
+        send(i + ahead)
         for k in range(1, far):
             arrived[i][k - 1].wait_recv()
             ref = place(lax.rem(ih - k + far, far), ix, i)
@@ -584,8 +585,8 @@
         elif kind in ("pair", "pair8"):
             local = outs[i].at[ih, :, ix] if kind == "pair8" else outs[i].at[ih, ix]
             local = local_copy(i, sources[i], local)
-            step = (8 if kind == "pair8" else sources[i].shape[1]) // PARTS
-            cuts = [pl.ds(part * step, step) for part in range(PARTS)]
+            step = (8 if kind == "pair8" else sources[i].shape[1]) // PARTS[kind]
+            cuts = [pl.ds(part * step, step) for part in range(PARTS[kind])]
             if kind == "pair8":
                 parts = [sources[i].at[c] for c in cuts]
             else:
@@ -594,7 +595,7 @@
             def place(h, x, part, out=outs[i], cuts=cuts, wide=kind == "pair8"):
                 return out.at[h, cuts[part], x] if wide else out.at[h, x, :, cuts[part]]
 
-            wait = (PARTS - AHEAD + 1) * kinds[:i].count("pair8")
+            wait = (PARTS[kind] // 2 + 1) * kinds[:i].count("pair8")
             running.append(pair_steps(far, copies, parts, place, local, wait))
         else:
             place = (ih, ip, iy, ic) if kind == "seq" else (ih, ip, iy, ic, ix)
@@ -620,9 +621,9 @@
         elif kind == "group":
             lead, total = (2, 2, 2), total + 13
         elif kind == "pair":
-            lead, total = (far, fsdp), total + PARTS * (2 * far - 1)
+            lead, total = (far, fsdp), total + PARTS[kind] * (2 * far - 1)
         elif kind == "pair8":
-            lead, total = (far, 8, fsdp), total + PARTS * (2 * far - 1)
+            lead, total = (far, 8, fsdp), total + PARTS[kind] * (2 * far - 1)
         else:
             lead, total = (), total + 7
         tail = array.shape[1:] if kind == "pair8" else array.shape
@@ -650,10 +651,10 @@
 def reduce_plan(kind, far, fsdp, tail):
     rows, columns = tail
     if kind == "group":
-        half = rows // 2
+        step = rows // 4
         return ("p", "y"), [
-            ((pl.ds(0, half), slice(None)), (half, columns), ("p", "y")),
-            ((pl.ds(half, half), slice(None)), (half, columns), ("y", "p")),
+            ((pl.ds(i * step, step), slice(None)), (step, columns), ("yp", "py")[i % 2])
+            for i in range(4)
         ]
     if kind in ("seq", "seq_turned"):
         order = ("y", "p", "h") if kind == "seq" else ("p", "y", "h")
@@ -897,7 +898,7 @@
         0,
         far,
         fsdp,
-        ("all", "all", "spread", "spread", "pair"),
+        ("all_y", "all", "spread", "spread", "pair"),
         (
             jnp.concatenate([query_weight, key_matrix, value_matrix], axis=1),
             vectors,
@@ -998,7 +999,6 @@
     grad_branch = grad_middle.astype(BF16)
     grad_branch, gate_sum, up_sum = lax.optimization_barrier((grad_branch, gate_sum, up_sum))
     gate_sum = over_h(gate_sum).astype(BF16)
-    up_sum = over_h(up_sum).astype(BF16)
     grad_attended = cols_dot(grad_branch, w_output).astype(BF16)
     grad_kvs, grad_query = [], []
     for m in range(micro):
@@ -1017,9 +1017,10 @@
         grad_query.append(query_part)
 
     blocks = (far, 2, 2, 2, fsdp, shard)
-    grad_kvs, gate_sum, hidden, hidden_turned = lax.optimization_barrier(
-        (grad_kvs, gate_sum, hidden, hidden_turned)
-    )
+    grad_kvs, gate_sum, up_sum, hidden, hidden_turned = lax.optimization_barrier(
+        (grad_kvs, gate_sum, up_sum, hidden, hidden_turned)
+    )
+    up_sum = over_h(up_sum).astype(BF16)
     down_part, _ = over_x(
         mat_dot(hidden_turned, upstream_all).reshape(far, fsdp, -1, width), 1, ()
     )
@@ -1030,13 +1031,13 @@
         4,
         far,
         fsdp,
-        tuple("seq_turned" if m % 2 else "seq" for m in range(micro)) + ("all_x", "group"),
-        tuple(grad_kvs) + (g_output.reshape(blocks + (width,)), final.reshape(group)),
-    )
-    grad_kvs, output_part = list(reduced[:micro]), reduced[micro]
+        ("group", "all_x") + tuple("seq_turned" if m % 2 else "seq" for m in range(micro)),
+        (final.reshape(group), g_output.reshape(blocks + (width,))) + tuple(grad_kvs),
+    )
+    grad_kvs, output_part = list(reduced[2:]), reduced[1]
     grad_kvs[0], down_part = lax.optimization_barrier((grad_kvs[0], down_part))
     down_part = over_h(down_part)
-    results = (middle + reduced[micro + 1]).astype(BF16)
+    results = (middle + reduced[0]).astype(BF16)
     grad_query = jnp.concatenate(grad_query, axis=0)
     grad_kv = jnp.concatenate(grad_kvs, axis=0)
     (grad_kv,) = rotate(

time: 714 us -> 718 us (level)
  Pallas kernels: 481 us -> 500 us
  waiting for transfers between devices: 40.5 us -> 27 us
    ppermute x3, waiting for transfers between devices: 33.3 us -> 15.2 us  [hop(): lax.ppermute(array, 'h', [(i, (i + shift) % far) for i in range(far)])]
    pallas_call x3, Pallas kernels: 229 us -> 239 us  [move(): pl.pallas_call(functools.partial(move_kernel, kinds, far), out_shape=tupl...]
    pallas_call x3, Pallas kernels: 185 us -> 194 us  [reduce(): pl.pallas_call(functools.partial(reduce_kernel, kinds, far, fsdp, tuple(c...]
  transfers between devices with their start and end apart: 6 -> 6, of which waited for: 2 -> 2; matrix products, arithmetic and copies ran while one was open for 14% -> 12% of each run, Pallas kernels for 29% -> 30%
where the time goes in v5:
time: 718 us; the launch traced here: 713 us
  Pallas kernels  500 us (70%)
  matrix products  104 us (14%)
  other arithmetic  35.1 us (5%)
  local copies, waits for them, and re-layouts  34.1 us (5%)
  waiting for transfers between devices  27 us (4%)
  starting transfers between devices  11.9 us (2%)
    pallas_call x3, Pallas kernels, move(): pl.pallas_call(functools.partial(move_kernel, kinds, far), out_shape=tupl...  239 us
    pallas_call x3, Pallas kernels, reduce(): pl.pallas_call(functools.partial(reduce_kernel, kinds, far, fsdp, tuple(c...  194 us
    dot_general x12, matrix products, dot(): lax.dot_general(left, right, ((dims[0], dims[1]), ((), ())), preferred_el...  104 us
    pallas_call x1, Pallas kernels, hidden_units(): pl.pallas_call(hidden_kernel, grid=(total // rows,), in_specs=[tile(width...  33.3 us
    ppermute x3, waiting for transfers between devices, hop(): lax.ppermute(array, 'h', [(i, (i + shift) % far) for i in range(far)])  15.2 us
  transfers between devices with their start and end apart: 6, of which 2 were waited for; matrix products, arithmetic and copies ran while one was open for 12% of the time, Pallas kernels for 30%

profile of v5, /device:TPU:0, one launch (start us, length us, event | category | flops | bytes accessed | tf_op | source)
XLA Modules:
  0.0 713.4 jit_solution(8085835960254674838)
XLA Ops:
  9.6 75.6 %gather_first.1 = (bf16[2,2,2,2,2,48,2048]{6,5,4,3,2,1,0:T(8,128)(2,1)}, f32[2,2,2,2,2,8,128]{6,5,4,3,2,1,0:T(8,128)}, bf16[8,48,1120]{2,1,0:T(8,128)(2,1)}, bf1...) custom-call(bf16[48,2048]{1,0:T(8,128)(2,1)} %pad_maximum_fusion.2.refs_0_, f32[8,128]{1,0:T(8,128)} %bitcast_convert_fusion.refs_1_, ...), custom_call_target="tpu_custom_call" | custom-call | bytes 1024 | tf_op jit(solution)/shard_map/gather_first/pallas_call | solution.py:631
  91.2 5.9 fusion.45.pre_ref
  102.2 129.5 %gather_second.1 = (bf16[2,2,2,2,128,512]{5,4,3,2,1,0:T(8,128)(2,1)}, bf16[2,2,2,2,128,512]{5,4,3,2,1,0:T(8,128)(2,1)}, bf16[2,2,2,2,2,48,1536]{6,5,4,3,2,1,0:T(...) custom-call(bf16[128,512]{1,0:T(8,128)(2,1)} %get-tuple-element.71.r, ...), custom_call_target="tpu_custom_call" | custom-call | bytes 1024 | tf_op jit(solution)/shard_map/gather_second/pallas_call | solution.py:631
  231.7 4.7 attend_forward.2
  248.1 34.2 %gather_tokens.1 = bf16[2,2,2,256,1536]{4,3,2,1,0:T(8,128)(2,1)} custom-call(bf16[256,1536]{1,0:T(8,128)(2,1)} %multiply_convert_fusion.refs_0_), custom_call_target="tpu_custom_call" | custom-call | bytes 1024 | tf_op jit(solution)/shard_map/gather_tokens/pallas_call | solution.py:631
  282.4 33.3 %hidden_units.1 = (bf16[1536,2048]{1,0:T(8,128)(2,1)}, bf16[2048,1120]{1,0:T(8,128)(2,1)}, bf16[1120,2048]{1,0:T(8,128)(2,1)}, bf16[2048,1120]{1,0:T(8,128)(2,1)}, bf16[2048,1120]{1,0:T(8,128)(2,1)}) custom-call(bf16[2048,1536]{1,0:T(8,128)(2,1)} %bitcast.175, bf16[2048,1536]{1,0:T(8,128)(2,1)} %bitcast.207, bf16[1536,1120]{1,0:T(8,128)(2,1)} %bitcast.213, ...), custom_call_target="tpu_custom_call" | custom-call | flops 21139292160 | bytes 25165824 | tf_op jit(solution)/shard_map/hidden_units/pallas_call | solution.py:263
  315.6 12.9 %fusion.6 = bf16[2,8,2,48,1120]{4,3,1,0,2:T(8,128)(2,1)} fusion(bf16[2048,1120]{1,0:T(8,128)(2,1)} %get-tuple-element.84, bf16[2,8,2,48,2048]{4,3,2,1,0:T(8,128)(2,1)} %bitcast.217), kind=kOutput, calls=%fused_computation.10 | convolution fusion | flops 7048151040 | bytes 14319616 | tf_op jit(solution)/shard_map/dot_general | solution.py:53
  331.6 12.0 %fusion.11 = bf16[2,8,2,48,1120]{4,3,1,0,2:T(8,128)(2,1)S(1)} fusion(bf16[2048,1120]{1,0:T(8,128)(2,1)} %get-tuple-element.88, bf16[2,8,2,48,2048]{4,3,2,1,0:T(8,128)(2,1)} %bitcast.218), kind=kOutput, calls=%fused_computation.11 | convolution fusion | flops 7048151040 | bytes 14319616 | tf_op jit(solution)/shard_map/dot_general | solution.py:53
  348.8 11.1 %fusion.46 = f32[2048,1536]{1,0:T(8,128)} fusion(bf16[2048,1120]{1,0:T(8,128)(2,1)S(1)} %bitcast.223, bf16[1536,1120]{1,0:T(8,128)(2,1)S(1)} %bitcast.214), kind=kOutput, calls=%fused_computation.115 | convolution fusion | flops 7046430720 | bytes 20611072 | tf_op jit(solution)/shard_map/dot_general | solution.py:53
  359.8 13.8 %add_convert_fusion = bf16[2048,1536]{1,0:T(8,128)(2,1)} fusion(f32[2048,1536]{1,0:T(8,128)} %fusion.46, bf16[2048,1120]{1,0:T(8,128)(2,1)} %get-tuple-element.88, bf16[1536,1120]{1,0:T(8,128)(2,1)S(1)} %bitcast.212), kind=kOutput, calls=%fused_computation | convolution fusion | flops 7052722176 | bytes 26902528 | tf_op jit(solution)/shard_map/dot_general | solution.py:53
  373.7 33.4 %reduce_tokens.1 = f32[256,1536]{1,0:T(8,128)} custom-call(bf16[2,2,2,256,1536]{4,3,2,1,0:T(8,128)(2,1)} %bitcast.176), custom_call_target="tpu_custom_call" | custom-call | bytes 1024 | tf_op jit(solution)/shard_map/reduce_tokens/pallas_call | solution.py:832
  414.0 11.9 %collective-permute-done = bf16[2,8,48,1120]{3,2,1,0:T(8,128)(2,1)} collective-permute-done((bf16[2,8,48,1120]{3,2,1,0:T(8,128)(2,1)}, bf16[2,8,48,1120]{3,2,1,0:T(8,128)(2,1)}, u32[]{:S(2)}, u32[]{:S(2)}) %collective-permute-start) | collective-permute-done | bytes 1720352 | tf_op jit(solution)/shard_map/ppermute | solution.py:883
  430.0 8.4 %collective-permute-start.2 = (bf16[8,48,1120]{2,1,0:T(8,128)(2,1)}, bf16[8,48,1120]{2,1,0:T(8,128)(2,1)}, u32[]{:S(2)}, u32[]{:S(2)}) collective-permute-start(bf16[8,48,1120]{2,1,0:T(8,128)(2,1)} %dynamic-slice_bitcast_fusion.4), channel_id=1, source_target_pairs={{0,16},{16,0},{1,17},{17,1},{2,18},{18,2},{3,19},{19,3},{4,20},{20... | collective-permute-start | bytes 2580488 | tf_op jit(solution)/shard_map/ppermute | solution.py:882
  439.6 4.9 convolution_convert_fusion.4.do_ref
  444.5 6.4 attend_backward.3
  450.9 6.1 attend_backward.2
  457.0 5.1 convolution_convert_fusion.1
  462.2 15.1 %collective-permute-done.2 = bf16[8,48,1120]{2,1,0:T(8,128)(2,1)} collective-permute-done((bf16[8,48,1120]{2,1,0:T(8,128)(2,1)}, bf16[8,48,1120]{2,1,0:T(8,128)(2,1)}, u32[]{:S(2)}, u32[]{:S(2)}) %collective-permute-start.2) | collective-permute-done | bytes 860192 | tf_op jit(solution)/shard_map/ppermute | solution.py:882
  479.6 10.9 %convolution_convert_fusion.3 = bf16[2,2,280,1536]{3,2,1,0:T(8,128)(2,1)S(1)} fusion(bf16[2,2,280,2048]{3,2,1,0:T(8,128)(2,1)} %bitcast.219, bf16[2048,1536,1,1]{1,0,3,2:T(8,128)(2,1)} %bitcast.208), kind=kOutput, calls=%fused_computation.12 | convolution fusion | flops 7048151040 | bytes 14319616 | tf_op jit(solution)/shard_map/dot_general | solution.py:53
  494.4 10.2 %convolution_convert_fusion.2 = bf16[2048,1536]{1,0:T(8,128)(2,1)} fusion(bf16[2048,1120]{1,0:T(8,128)(2,1)S(1)} %bitcast.221, bf16[1120,1536]{1,0:T(8,128)(2,1)S(1)} %bitcast.216), kind=kOutput, calls=%fused_computation.3 | convolution fusion | flops 7049576448 | bytes 14319616 | tf_op jit(solution)/shard_map/dot_general | solution.py:53
  504.6 91.8 %reduce_second.1 = (f32[256,1536]{1,0:T(8,128)}, f32[48,1536]{1,0:T(8,128)}, f32[128,512]{1,0:T(8,128)}, f32[128,512]{1,0:T(8,128)}) custom-call(bf16[2,2,2,256,1536]{4,3,2,1,0:T(8,128)(2,1)} %bitcast.177, bf16[2,2,2,2,2,48,1536]{6,5,4,3,2,1,0:T(8,128)(2,1)} %bitcast.167, bf16[2,2,2,2,128,512]{5,4,3,2,1,0:T(8,128)(2,1)} %bitcast.180, ...), custom_call_target="tpu_custom_call" | custom-call | bytes 1024 | tf_op jit(solution)/shard_map/reduce_second/pallas_call | solution.py:832
  611.0 7.0 fusion.31
  622.3 5.6 convolution_convert_fusion
  627.9 68.6 %reduce_last.1 = (f32[48,2048]{1,0:T(8,128)}, f32[8,128]{1,0:T(8,128)}, bf16[8,48,1120]{2,1,0:T(8,128)(2,1)}, bf16[8,48,1120]{2,1,0:T(8,128)(2,1)}) custom-call(bf16[2,2,2,2,2,48,2048]{6,5,4,3,2,1,0:T(8,128)(2,1)} %bitcast.166, f32[2,2,2,2,2,8,128]{6,5,4,3,2,1,0:T(8,128)} %bitcast.184, bf16[8,48,1120]{2,1,0:T(8,128)(2,1)} %fusion.20.refs_2_, ...), custom_call_target="tpu_custom_call" | custom-call | bytes 1024 | tf_op jit(solution)/shard_map/reduce_last/pallas_call | solution.py:832
  (158 shorter events, 93.0 us)
Async XLA Ops:
  7.8 78.5 %copy-start.20 = (s32[1,2,4]{2,1,0:T(2,128)S(1)}, s32[1,2,4]{2,1,0:T(2,128)}, u32[]{:S(2)}) copy-start(s32[1,2,4]{2,1,0:T(2,128)} %param.16) | copy-start | bytes 100
  7.8 79.7 %copy-start.3 = (bf16[1,2,128,1536]{3,2,1,0:T(8,128)(2,1)S(1)}, bf16[1,2,128,1536]{3,2,1,0:T(8,128)(2,1)}, u32[]{:S(2)}) copy-start(bf16[1,2,128,1536]{3,2,1,0:T(8,128)(2,1)} %param.15) | copy-start | bytes 2359300
  87.5 9.5 %copy-start.18 = (f32[1536]{0:T(1024)}, f32[1536]{0:T(1024)S(1)}, u32[]{:S(2)}) copy-start(f32[1536]{0:T(1024)S(1)} %mul.213) | copy-start | bytes 18436
  328.6 20.2 %slice-start.2 = ((s8[4718592]{0:T(1024)(128)(4,1)}), s8[4194304]{0:T(1024)(128)(4,1)S(1)}, s32[]{:S(2)}) async-start(s8[4718592]{0:T(1024)(128)(4,1)} %bitcast.222), calls=%async_computation.2 | async-start | bytes 8388608
  331.6 17.2 %slice-start.3 = ((s8[4718592]{0:T(1024)(128)(4,1)}), s8[524288]{0:T(1024)(128)(4,1)S(1)}, s32[]{:S(2)}) async-start(s8[4718592]{0:T(1024)(128)(4,1)} %bitcast.222), calls=%async_computation.3 | async-start | bytes 1048576
  346.7 13.1 %copy-start.24 = (bf16[2,8,2,48,1120]{4,3,2,1,0:T(8,128)(2,1)S(1)}, bf16[2,8,2,48,1120]{4,3,2,1,0:T(8,128)(2,1)}, u32[]{:S(2)}) copy-start(bf16[2,8,2,48,1120]{4,3,2,1,0:T(8,128)(2,1)} %get-tuple-element.82) | copy-start | bytes 10321924
  346.7 64.3 %collective-permute-start.1 = (bf16[2,8,48,1120]{3,2,1,0:T(8,128)(2,1)}, bf16[2,8,48,1120]{3,2,1,0:T(8,128)(2,1)}, u32[]{:S(2)}, u32[]{:S(2)}) collective-permute-start(bf16[2,8,48,1120]{3,2,1,0:T(8,128)(2,1)} %dynamic-slice_bitcast_fusion), channel_id=1, source_target_pairs={{0,1},{1,0},{2,3},{3,2},{4,5},{5,4},{6,7},{7,6},{8,9},{9,8},{10,11... | collective-permute-start | bytes 5160968 | tf_op jit(solution)/shard_map/ppermute | solution.py:883
  346.8 79.1 %collective-permute-start = (bf16[2,8,48,1120]{3,2,1,0:T(8,128)(2,1)}, bf16[2,8,48,1120]{3,2,1,0:T(8,128)(2,1)}, u32[]{:S(2)}, u32[]{:S(2)}) collective-permute-start(bf16[2,8,48,1120]{3,2,1,0:T(8,128)(2,1)} %dynamic-slice_bitcast_fusion.1), channel_id=1, source_target_pairs={{0,1},{1,0},{2,3},{3,2},{4,5},{5,4},{6,7},{7,6},{8,9},{9,8},{10,11... | collective-permute-start | bytes 5160968 | tf_op jit(solution)/shard_map/ppermute | solution.py:883
  411.1 14.8 %copy-start.5 = (bf16[2,8,2,48,1120]{4,3,1,0,2:T(8,128)(2,1)S(1)}, bf16[2,8,2,48,1120]{4,3,1,0,2:T(8,128)(2,1)}, u32[]{:S(2)}) copy-start(bf16[2,8,2,48,1120]{4,3,1,0,2:T(8,128)(2,1)} %fusion.6) | copy-start | bytes 10321924
  430.0 47.3 %collective-permute-start.2 = (bf16[8,48,1120]{2,1,0:T(8,128)(2,1)}, bf16[8,48,1120]{2,1,0:T(8,128)(2,1)}, u32[]{:S(2)}, u32[]{:S(2)}) collective-permute-start(bf16[8,48,1120]{2,1,0:T(8,128)(2,1)} %dynamic-slice_bitcast_fusion.4), channel_id=1, source_target_pairs={{0,16},{16,0},{1,17},{17,1},{2,18},{18,2},{3,19},{19,3},{4,20},{20... | collective-permute-start | bytes 2580488 | tf_op jit(solution)/shard_map/ppermute | solution.py:882
  457.0 20.3 %copy-start.2 = (bf16[2,8,48,1120]{3,2,1,0:T(8,128)(2,1)S(1)}, bf16[2,8,48,1120]{3,2,1,0:T(8,128)(2,1)}, u32[]{:S(2)}) copy-start(bf16[2,8,48,1120]{3,2,1,0:T(8,128)(2,1)} %copy-done.1) | copy-start | bytes 5160964
  457.0 37.2 %slice-start = ((s8[4718592]{0:T(1024)(128)(4,1)}), s8[4194304]{0:T(1024)(128)(4,1)S(1)}, s32[]{:S(2)}) async-start(s8[4718592]{0:T(1024)(128)(4,1)} %bitcast.220), calls=%async_computation | async-start | bytes 8388608
  479.6 14.7 %slice-start.1 = ((s8[4718592]{0:T(1024)(128)(4,1)}), s8[524288]{0:T(1024)(128)(4,1)S(1)}, s32[]{:S(2)}) async-start(s8[4718592]{0:T(1024)(128)(4,1)} %bitcast.220), calls=%async_computation.1 | async-start | bytes 1048576
  491.8 109.6 %collective-permute-start.3 = (bf16[2,280,1536]{2,1,0:T(8,128)(2,1)}, bf16[2,280,1536]{2,1,0:T(8,128)(2,1)}, u32[]{:S(2)}, u32[]{:S(2)}) collective-permute-start(bf16[2,280,1536]{2,1,0:T(8,128)(2,1)} %dynamic-slice_bitcast_fusion.2), channel_id=1, source_target_pairs={{0,1},{1,0},{2,3},{3,2},{4,5},{5,4},{6,7},{7,6},{8,9},{9,8},{10,11... | collective-permute-start | bytes 5160968 | tf_op jit(solution)/shard_map/ppermute | solution.py:883
  494.3 104.8 %collective-permute-start.4 = (bf16[8,48,1120]{2,1,0:T(8,128)(2,1)}, bf16[8,48,1120]{2,1,0:T(8,128)(2,1)}, u32[]{:S(2)}, u32[]{:S(2)}) collective-permute-start(bf16[8,48,1120]{2,1,0:T(8,128)(2,1)} %dynamic-slice_bitcast_fusion.3), channel_id=1, source_target_pairs={{0,16},{16,0},{1,17},{17,1},{2,18},{18,2},{3,19},{19,3},{4,20},{20... | collective-permute-start | bytes 2580488 | tf_op jit(solution)/shard_map/ppermute | solution.py:882
  596.4 4.9 copy-start.9
  603.4 4.4 copy-start.13
  603.4 7.6 %copy-start.4 = (bf16[1,2,128,1536]{3,2,1,0:T(8,128)(2,1)S(1)}, bf16[1,2,128,1536]{3,2,1,0:T(8,128)(2,1)}, u32[]{:S(2)}) copy-start(bf16[1,2,128,1536]{3,2,1,0:T(8,128)(2,1)} %param.15) | copy-start | bytes 2359300
  604.4 105.2 %collective-permute-start.5 = (bf16[280,1536]{1,0:T(8,128)(2,1)}, bf16[280,1536]{1,0:T(8,128)(2,1)}, u32[]{:S(2)}, u32[]{:S(2)}) collective-permute-start(bf16[280,1536]{1,0:T(8,128)(2,1)} %dynamic-slice_bitcast_fusion.5), channel_id=1, source_target_pairs={{0,16},{16,0},{1,17},{17,1},{2,18},{18,2},{3,19},{19,3},{4,20},{20... | collective-permute-start | bytes 2580488 | tf_op jit(solution)/shard_map/ppermute | solution.py:882
  611.0 11.3 %copy-start.12 = (bf16[256,512]{1,0:T(8,128)(2,1)S(1)}, bf16[256,512]{1,0:T(8,128)(2,1)}, u32[]{:S(2)}) copy-start(bf16[256,512]{1,0:T(8,128)(2,1)} %rotate.3) | copy-start | bytes 786436
  627.9 71.5 %copy-start.23 = (f32[256]{0:T(256)S(1)}, f32[256]{0:T(256)}, u32[]{:S(2)}) copy-start(f32[256]{0:T(256)} %get-tuple-element.121) | copy-start | bytes 3076
  696.5 9.6 %copy-start.19 = (f32[1536]{0:T(1024)S(1)}, f32[1536]{0:T(1024)}, u32[]{:S(2)}) copy-start(f32[1536]{0:T(1024)} %copy-done.18) | copy-start | bytes 18436
  696.5 9.6 %copy-start.21 = (f32[256]{0:T(256)S(1)}, f32[256]{0:T(256)}, u32[]{:S(2)}) copy-start(f32[256]{0:T(256)} %get-tuple-element.143) | copy-start | bytes 3076
  696.5 9.6 %copy-start.22 = (f32[256]{0:T(256)S(1)}, f32[256]{0:T(256)}, u32[]{:S(2)}) copy-start(f32[256]{0:T(256)} %multiply_multiply_fusion) | copy-start | bytes 3076
  (13 other events, 38.1 us)

commit v6 on v5

--- a/solution.py
+++ b/solution.py
@@ -339,7 +339,7 @@
 
 
 MESH = pl.DeviceIdType.MESH
-PARTS = {"pair": 4, "pair8": 8}
+PARTS = 4
 COST = 1024
 ANY = pl.BlockSpec(memory_space=pl.ANY)
 
@@ -499,25 +499,21 @@
     local.wait()
 
 
-def pair_steps(far, copies, parts, place, local, delay):
+def pair_steps(far, copies, parts, place, local, number):
     ih, ix = lax.axis_index("h"), lax.axis_index("x")
     local.start()
-    for _ in range(delay):
+    count = len(parts)
+    sent = [copies.start(parts[i], place(ih, ix, i), flip("x")) for i in range(count)]
+    for _ in range(1 + number):
         yield
-    arrived, sent = [], []
-
-    def send(i):
-        if i < len(parts):
-            target = place(ih, ix, i)
-            arrived.append([copies.start(parts[i], target, other_h(far, k)) for k in range(1, far)])
-            sent.append(copies.start(parts[i], target, flip("x")))
-
-    ahead = len(parts) // 2
-    for i in range(ahead):
-        send(i)
-    for i in range(len(parts)):
+    arrived = [
+        [copies.start(parts[i], place(ih, ix, i), other_h(far, k)) for k in range(1, far)]
+        for i in range(count)
+    ]
+    for _ in range((count - 1) * number):
         yield
-        send(i + ahead)
+    for i in range(count):
+        yield
         for k in range(1, far):
             arrived[i][k - 1].wait_recv()
             ref = place(lax.rem(ih - k + far, far), ix, i)
@@ -580,13 +576,12 @@
         elif kind == "group":
             place = outs[i].at[ip, iy, ic]
             local = local_copy(i, sources[i], place)
-            delay = 3 if count > 1 else 0
-            running.append(group_steps(far, copies, sources[i], outs[i], local, delay))
+            running.append(group_steps(far, copies, sources[i], outs[i], local, 0))
         elif kind in ("pair", "pair8"):
             local = outs[i].at[ih, :, ix] if kind == "pair8" else outs[i].at[ih, ix]
             local = local_copy(i, sources[i], local)
-            step = (8 if kind == "pair8" else sources[i].shape[1]) // PARTS[kind]
-            cuts = [pl.ds(part * step, step) for part in range(PARTS[kind])]
+            step = (8 if kind == "pair8" else sources[i].shape[1]) // PARTS
+            cuts = [pl.ds(part * step, step) for part in range(PARTS)]
             if kind == "pair8":
                 parts = [sources[i].at[c] for c in cuts]
             else:
@@ -595,8 +590,8 @@
             def place(h, x, part, out=outs[i], cuts=cuts, wide=kind == "pair8"):
                 return out.at[h, cuts[part], x] if wide else out.at[h, x, :, cuts[part]]
 
-            wait = (PARTS[kind] // 2 + 1) * kinds[:i].count("pair8")
-            running.append(pair_steps(far, copies, parts, place, local, wait))
+            number = kinds[:i].count("pair8")
+            running.append(pair_steps(far, copies, parts, place, local, number))
         else:
             place = (ih, ip, iy, ic) if kind == "seq" else (ih, ip, iy, ic, ix)
             local = local_copy(i, sources[i], outs[i].at[place])
@@ -621,9 +616,9 @@
         elif kind == "group":
             lead, total = (2, 2, 2), total + 13
         elif kind == "pair":
-            lead, total = (far, fsdp), total + PARTS[kind] * (2 * far - 1)
+            lead, total = (far, fsdp), total + PARTS * (2 * far - 1)
         elif kind == "pair8":
-            lead, total = (far, 8, fsdp), total + PARTS[kind] * (2 * far - 1)
+            lead, total = (far, 8, fsdp), total + PARTS * (2 * far - 1)
         else:
             lead, total = (), total + 7
         tail = array.shape[1:] if kind == "pair8" else array.shape
@@ -1017,10 +1012,9 @@
         grad_query.append(query_part)
 
     blocks = (far, 2, 2, 2, fsdp, shard)
-    grad_kvs, gate_sum, up_sum, hidden, hidden_turned = lax.optimization_barrier(
-        (grad_kvs, gate_sum, up_sum, hidden, hidden_turned)
-    )
-    up_sum = over_h(up_sum).astype(BF16)
+    grad_kvs, gate_sum, hidden, hidden_turned = lax.optimization_barrier(
+        (grad_kvs, gate_sum, hidden, hidden_turned)
+    )
     down_part, _ = over_x(
         mat_dot(hidden_turned, upstream_all).reshape(far, fsdp, -1, width), 1, ()
     )
@@ -1035,8 +1029,8 @@
         (final.reshape(group), g_output.reshape(blocks + (width,))) + tuple(grad_kvs),
     )
     grad_kvs, output_part = list(reduced[2:]), reduced[1]
-    grad_kvs[0], down_part = lax.optimization_barrier((grad_kvs[0], down_part))
-    down_part = over_h(down_part)
+    grad_kvs[0], up_sum = lax.optimization_barrier((grad_kvs[0], up_sum))
+    up_sum = over_h(up_sum).astype(BF16)
     results = (middle + reduced[0]).astype(BF16)
     grad_query = jnp.concatenate(grad_query, axis=0)
     grad_kv = jnp.concatenate(grad_kvs, axis=0)
@@ -1054,6 +1048,8 @@
     grad_rows, gain_attn_sum = rms_backward(rows, recip_one, gain_attn, grad_normed)
     input_grad = grad_middle + grad_rows
     g_qkv = rows_dot(normed_low, grad_pre).astype(BF16)
+    g_qkv, up_sum, down_part = lax.optimization_barrier((g_qkv, up_sum, down_part))
+    down_part = over_h(down_part)
     bias_sum = jnp.sum(grad_pre.astype(F32), axis=0)
     vector_sums = jnp.concatenate(
         [

time: 718 us -> 724 us (level)
  waiting for transfers between devices: 27 us -> 48.9 us
    ppermute x3, waiting for transfers between devices: 15.2 us -> 36.9 us  [hop(): lax.ppermute(array, 'h', [(i, (i + shift) % far) for i in range(far)])]
    pallas_call x3, Pallas kernels: 194 us -> 185 us  [reduce(): pl.pallas_call(functools.partial(reduce_kernel, kinds, far, fsdp, tuple(c...]
  transfers between devices with their start and end apart: 6 -> 6, of which waited for: 2 -> 3; matrix products, arithmetic and copies ran while one was open for 12% -> 10% of each run, Pallas kernels for 30% -> 28%
where the time goes in v6:
time: 724 us; the launch traced here: 718 us
  Pallas kernels  494 us (68%)
  matrix products  101 us (14%)
  waiting for transfers between devices  48.9 us (7%)
  other arithmetic  29 us (4%)
  local copies, waits for them, and re-layouts  28.9 us (4%)
  starting transfers between devices  14.6 us (2%)
    pallas_call x3, Pallas kernels, move(): pl.pallas_call(functools.partial(move_kernel, kinds, far), out_shape=tupl...  242 us
    pallas_call x3, Pallas kernels, reduce(): pl.pallas_call(functools.partial(reduce_kernel, kinds, far, fsdp, tuple(c...  185 us
    dot_general x12, matrix products, dot(): lax.dot_general(left, right, ((dims[0], dims[1]), ((), ())), preferred_el...  101 us
    ppermute x3, waiting for transfers between devices, hop(): lax.ppermute(array, 'h', [(i, (i + shift) % far) for i in range(far)])  36.9 us
    pallas_call x1, Pallas kernels, hidden_units(): pl.pallas_call(hidden_kernel, grid=(total // rows,), in_specs=[tile(width...  33.3 us
  transfers between devices with their start and end apart: 6, of which 3 were waited for; matrix products, arithmetic and copies ran while one was open for 10% of the time, Pallas kernels for 28%

profile of v6, /device:TPU:0, one launch (start us, length us, event | category | flops | bytes accessed | tf_op | source)
XLA Modules:
  0.0 717.9 jit_solution(6664874384204104767)
XLA Ops:
  9.6 80.4 %gather_first.1 = (bf16[2,2,2,2,2,48,2048]{6,5,4,3,2,1,0:T(8,128)(2,1)}, f32[2,2,2,2,2,8,128]{6,5,4,3,2,1,0:T(8,128)}, bf16[8,48,1120]{2,1,0:T(8,128)(2,1)}, bf1...) custom-call(bf16[48,2048]{1,0:T(8,128)(2,1)} %pad_maximum_fusion.2.refs_0_, f32[8,128]{1,0:T(8,128)} %bitcast_convert_fusion.refs_1_, ...), custom_call_target="tpu_custom_call" | custom-call | bytes 1024 | tf_op jit(solution)/shard_map/gather_first/pallas_call | solution.py:626
  95.9 5.9 fusion.45.pre_ref
  106.9 128.9 %gather_second.1 = (bf16[2,2,2,2,128,512]{5,4,3,2,1,0:T(8,128)(2,1)}, bf16[2,2,2,2,128,512]{5,4,3,2,1,0:T(8,128)(2,1)}, bf16[2,2,2,2,2,48,1536]{6,5,4,3,2,1,0:T(...) custom-call(bf16[128,512]{1,0:T(8,128)(2,1)} %get-tuple-element.73.r, ...), custom_call_target="tpu_custom_call" | custom-call | bytes 1024 | tf_op jit(solution)/shard_map/gather_second/pallas_call | solution.py:626
  235.9 4.7 attend_forward.2
  252.2 32.9 %gather_tokens.1 = bf16[2,2,2,256,1536]{4,3,2,1,0:T(8,128)(2,1)} custom-call(bf16[256,1536]{1,0:T(8,128)(2,1)} %multiply_convert_fusion.refs_0_), custom_call_target="tpu_custom_call" | custom-call | bytes 1024 | tf_op jit(solution)/shard_map/gather_tokens/pallas_call | solution.py:626
  285.1 33.3 %hidden_units.1 = (bf16[1536,2048]{1,0:T(8,128)(2,1)}, bf16[2048,1120]{1,0:T(8,128)(2,1)}, bf16[1120,2048]{1,0:T(8,128)(2,1)}, bf16[2048,1120]{1,0:T(8,128)(2,1)}, bf16[2048,1120]{1,0:T(8,128)(2,1)}) custom-call(bf16[2048,1536]{1,0:T(8,128)(2,1)} %bitcast.175, bf16[2048,1536]{1,0:T(8,128)(2,1)} %bitcast.207, bf16[1536,1120]{1,0:T(8,128)(2,1)} %bitcast.213, ...), custom_call_target="tpu_custom_call" | custom-call | flops 21139292160 | bytes 25165824 | tf_op jit(solution)/shard_map/hidden_units/pallas_call | solution.py:263
  318.4 12.9 %fusion.6 = bf16[2,8,2,48,1120]{4,3,1,0,2:T(8,128)(2,1)} fusion(bf16[2048,1120]{1,0:T(8,128)(2,1)} %get-tuple-element.86, bf16[2,8,2,48,2048]{4,3,2,1,0:T(8,128)(2,1)} %bitcast.217), kind=kOutput, calls=%fused_computation.10 | convolution fusion | flops 7048151040 | bytes 14319616 | tf_op jit(solution)/shard_map/dot_general | solution.py:53
  334.4 12.0 %fusion.11 = bf16[2,8,2,48,1120]{4,3,1,0,2:T(8,128)(2,1)S(1)} fusion(bf16[2048,1120]{1,0:T(8,128)(2,1)} %get-tuple-element.90, bf16[2,8,2,48,2048]{4,3,2,1,0:T(8,128)(2,1)} %bitcast.218), kind=kOutput, calls=%fused_computation.11 | convolution fusion | flops 7048151040 | bytes 14319616 | tf_op jit(solution)/shard_map/dot_general | solution.py:53
  351.6 11.0 %fusion.46 = f32[2048,1536]{1,0:T(8,128)} fusion(bf16[2048,1120]{1,0:T(8,128)(2,1)S(1)} %bitcast.223, bf16[1536,1120]{1,0:T(8,128)(2,1)S(1)} %bitcast.214), kind=kOutput, calls=%fused_computation.115 | convolution fusion | flops 7046430720 | bytes 20611072 | tf_op jit(solution)/shard_map/dot_general | solution.py:53
  362.6 13.8 %add_convert_fusion = bf16[2048,1536]{1,0:T(8,128)(2,1)} fusion(f32[2048,1536]{1,0:T(8,128)} %fusion.46, bf16[2048,1120]{1,0:T(8,128)(2,1)} %get-tuple-element.90, bf16[1536,1120]{1,0:T(8,128)(2,1)S(1)} %bitcast.212), kind=kOutput, calls=%fused_computation | convolution fusion | flops 7052722176 | bytes 26902528 | tf_op jit(solution)/shard_map/dot_general | solution.py:53
  376.3 33.4 %reduce_tokens.1 = f32[256,1536]{1,0:T(8,128)} custom-call(bf16[2,2,2,256,1536]{4,3,2,1,0:T(8,128)(2,1)} %bitcast.176), custom_call_target="tpu_custom_call" | custom-call | bytes 1024 | tf_op jit(solution)/shard_map/reduce_tokens/pallas_call | solution.py:827
  416.7 11.9 %collective-permute-done = bf16[2,8,48,1120]{3,2,1,0:T(8,128)(2,1)} collective-permute-done((bf16[2,8,48,1120]{3,2,1,0:T(8,128)(2,1)}, bf16[2,8,48,1120]{3,2,1,0:T(8,128)(2,1)}, u32[]{:S(2)}, u32[]{:S(2)}) %collective-permute-start) | collective-permute-done | bytes 1720352 | tf_op jit(solution)/shard_map/ppermute | solution.py:878
  432.8 12.0 %collective-permute-start.2 = (bf16[8,48,1120]{2,1,0:T(8,128)(2,1)}, bf16[8,48,1120]{2,1,0:T(8,128)(2,1)}, u32[]{:S(2)}, u32[]{:S(2)}) collective-permute-start(bf16[8,48,1120]{2,1,0:T(8,128)(2,1)} %dynamic-slice_bitcast_fusion.4), channel_id=1, source_target_pairs={{0,16},{16,0},{1,17},{17,1},{2,18},{18,2},{3,19},{19,3},{4,20},{20... | collective-permute-start | bytes 2580488 | tf_op jit(solution)/shard_map/ppermute | solution.py:877
  444.9 4.9 convolution_convert_fusion.4.do_ref
  449.8 6.4 attend_backward.3
  456.2 6.1 attend_backward.2
  462.3 5.1 convolution_convert_fusion.1
  467.4 16.0 %collective-permute-done.2 = bf16[8,48,1120]{2,1,0:T(8,128)(2,1)} collective-permute-done((bf16[8,48,1120]{2,1,0:T(8,128)(2,1)}, bf16[8,48,1120]{2,1,0:T(8,128)(2,1)}, u32[]{:S(2)}, u32[]{:S(2)}) %collective-permute-start.2) | collective-permute-done | bytes 860192 | tf_op jit(solution)/shard_map/ppermute | solution.py:877
  485.7 10.9 %convolution_convert_fusion.3 = bf16[2,2,280,1536]{3,2,1,0:T(8,128)(2,1)S(1)} fusion(bf16[2,2,280,2048]{3,2,1,0:T(8,128)(2,1)} %bitcast.219, bf16[2048,1536,1,1]{1,0,3,2:T(8,128)(2,1)} %bitcast.208), kind=kOutput, calls=%fused_computation.12 | convolution fusion | flops 7048151040 | bytes 14319616 | tf_op jit(solution)/shard_map/dot_general | solution.py:53
  500.9 10.2 %convolution_convert_fusion.2 = bf16[2048,1536]{1,0:T(8,128)(2,1)} fusion(bf16[2048,1120]{1,0:T(8,128)(2,1)S(1)} %bitcast.221, bf16[1120,1536]{1,0:T(8,128)(2,1)S(1)} %bitcast.216), kind=kOutput, calls=%fused_computation.3 | convolution fusion | flops 7049576448 | bytes 14319616 | tf_op jit(solution)/shard_map/dot_general | solution.py:53
  511.2 85.7 %reduce_second.1 = (f32[256,1536]{1,0:T(8,128)}, f32[48,1536]{1,0:T(8,128)}, f32[128,512]{1,0:T(8,128)}, f32[128,512]{1,0:T(8,128)}) custom-call(bf16[2,2,2,256,1536]{4,3,2,1,0:T(8,128)(2,1)} %bitcast.177, bf16[2,2,2,2,2,48,1536]{6,5,4,3,2,1,0:T(8,128)(2,1)} %bitcast.167, bf16[2,2,2,2,128,512]{5,4,3,2,1,0:T(8,128)(2,1)} %bitcast.180, ...), custom_call_target="tpu_custom_call" | custom-call | bytes 1024 | tf_op jit(solution)/shard_map/reduce_second/pallas_call | solution.py:827
  603.2 5.2 fusion.31
  614.8 20.9 %collective-permute-done.3 = bf16[8,48,1120]{2,1,0:T(8,128)(2,1)} collective-permute-done((bf16[8,48,1120]{2,1,0:T(8,128)(2,1)}, bf16[8,48,1120]{2,1,0:T(8,128)(2,1)}, u32[]{:S(2)}, u32[]{:S(2)}) %collective-permute-start.3) | collective-permute-done | bytes 860192 | tf_op jit(solution)/shard_map/ppermute | solution.py:877
  641.2 66.0 %reduce_last.1 = (f32[48,2048]{1,0:T(8,128)}, f32[8,128]{1,0:T(8,128)}, bf16[8,48,1120]{2,1,0:T(8,128)(2,1)}, bf16[8,48,1120]{2,1,0:T(8,128)(2,1)}) custom-call(bf16[2,2,2,2,2,48,2048]{6,5,4,3,2,1,0:T(8,128)(2,1)} %bitcast.166, f32[2,2,2,2,2,8,128]{6,5,4,3,2,1,0:T(8,128)} %bitcast.184, bf16[8,48,1120]{2,1,0:T(8,128)(2,1)} %fusion.20.refs_2_, ...), custom_call_target="tpu_custom_call" | custom-call | bytes 1024 | tf_op jit(solution)/shard_map/reduce_last/pallas_call | solution.py:827
  (160 shorter events, 85.3 us)
Async XLA Ops:
  7.8 83.2 %copy-start.22 = (s32[1,2,4]{2,1,0:T(2,128)S(1)}, s32[1,2,4]{2,1,0:T(2,128)}, u32[]{:S(2)}) copy-start(s32[1,2,4]{2,1,0:T(2,128)} %param.16) | copy-start | bytes 100
  7.8 84.4 %copy-start.3 = (bf16[1,2,128,1536]{3,2,1,0:T(8,128)(2,1)S(1)}, bf16[1,2,128,1536]{3,2,1,0:T(8,128)(2,1)}, u32[]{:S(2)}) copy-start(bf16[1,2,128,1536]{3,2,1,0:T(8,128)(2,1)} %param.15) | copy-start | bytes 2359300
  92.3 9.5 %copy-start.20 = (f32[1536]{0:T(1024)}, f32[1536]{0:T(1024)S(1)}, u32[]{:S(2)}) copy-start(f32[1536]{0:T(1024)S(1)} %mul.213) | copy-start | bytes 18436
  331.3 20.2 %slice-start.2 = ((s8[4718592]{0:T(1024)(128)(4,1)}), s8[4194304]{0:T(1024)(128)(4,1)S(1)}, s32[]{:S(2)}) async-start(s8[4718592]{0:T(1024)(128)(4,1)} %bitcast.222), calls=%async_computation.2 | async-start | bytes 8388608
  334.4 17.2 %slice-start.3 = ((s8[4718592]{0:T(1024)(128)(4,1)}), s8[524288]{0:T(1024)(128)(4,1)S(1)}, s32[]{:S(2)}) async-start(s8[4718592]{0:T(1024)(128)(4,1)} %bitcast.222), calls=%async_computation.3 | async-start | bytes 1048576
  349.5 13.1 %copy-start.25 = (bf16[2,8,2,48,1120]{4,3,2,1,0:T(8,128)(2,1)S(1)}, bf16[2,8,2,48,1120]{4,3,2,1,0:T(8,128)(2,1)}, u32[]{:S(2)}) copy-start(bf16[2,8,2,48,1120]{4,3,2,1,0:T(8,128)(2,1)} %get-tuple-element.84) | copy-start | bytes 10321924
  349.5 64.3 %collective-permute-start.1 = (bf16[2,8,48,1120]{3,2,1,0:T(8,128)(2,1)}, bf16[2,8,48,1120]{3,2,1,0:T(8,128)(2,1)}, u32[]{:S(2)}, u32[]{:S(2)}) collective-permute-start(bf16[2,8,48,1120]{3,2,1,0:T(8,128)(2,1)} %dynamic-slice_bitcast_fusion), channel_id=1, source_target_pairs={{0,1},{1,0},{2,3},{3,2},{4,5},{5,4},{6,7},{7,6},{8,9},{9,8},{10,11... | collective-permute-start | bytes 5160968 | tf_op jit(solution)/shard_map/ppermute | solution.py:878
  350.6 78.1 %collective-permute-start = (bf16[2,8,48,1120]{3,2,1,0:T(8,128)(2,1)}, bf16[2,8,48,1120]{3,2,1,0:T(8,128)(2,1)}, u32[]{:S(2)}, u32[]{:S(2)}) collective-permute-start(bf16[2,8,48,1120]{3,2,1,0:T(8,128)(2,1)} %dynamic-slice_bitcast_fusion.1), channel_id=1, source_target_pairs={{0,1},{1,0},{2,3},{3,2},{4,5},{5,4},{6,7},{7,6},{8,9},{9,8},{10,11... | collective-permute-start | bytes 5160968 | tf_op jit(solution)/shard_map/ppermute | solution.py:878
  413.8 14.9 %copy-start.6 = (bf16[2,8,2,48,1120]{4,3,1,0,2:T(8,128)(2,1)S(1)}, bf16[2,8,2,48,1120]{4,3,1,0,2:T(8,128)(2,1)}, u32[]{:S(2)}) copy-start(bf16[2,8,2,48,1120]{4,3,1,0,2:T(8,128)(2,1)} %fusion.6) | copy-start | bytes 10321924
  432.8 50.6 %collective-permute-start.2 = (bf16[8,48,1120]{2,1,0:T(8,128)(2,1)}, bf16[8,48,1120]{2,1,0:T(8,128)(2,1)}, u32[]{:S(2)}, u32[]{:S(2)}) collective-permute-start(bf16[8,48,1120]{2,1,0:T(8,128)(2,1)} %dynamic-slice_bitcast_fusion.4), channel_id=1, source_target_pairs={{0,16},{16,0},{1,17},{17,1},{2,18},{18,2},{3,19},{19,3},{4,20},{20... | collective-permute-start | bytes 2580488 | tf_op jit(solution)/shard_map/ppermute | solution.py:877
  462.3 21.1 %copy-start.2 = (bf16[2,8,48,1120]{3,2,1,0:T(8,128)(2,1)S(1)}, bf16[2,8,48,1120]{3,2,1,0:T(8,128)(2,1)}, u32[]{:S(2)}) copy-start(bf16[2,8,48,1120]{3,2,1,0:T(8,128)(2,1)} %copy-done.1) | copy-start | bytes 5160964
  462.3 37.9 %slice-start = ((s8[4718592]{0:T(1024)(128)(4,1)}), s8[4194304]{0:T(1024)(128)(4,1)S(1)}, s32[]{:S(2)}) async-start(s8[4718592]{0:T(1024)(128)(4,1)} %bitcast.220), calls=%async_computation | async-start | bytes 8388608
  485.7 14.5 %slice-start.1 = ((s8[4718592]{0:T(1024)(128)(4,1)}), s8[524288]{0:T(1024)(128)(4,1)S(1)}, s32[]{:S(2)}) async-start(s8[4718592]{0:T(1024)(128)(4,1)} %bitcast.220), calls=%async_computation.1 | async-start | bytes 1048576
  499.6 138.4 %collective-permute-start.4 = (bf16[2,280,1536]{2,1,0:T(8,128)(2,1)}, bf16[2,280,1536]{2,1,0:T(8,128)(2,1)}, u32[]{:S(2)}, u32[]{:S(2)}) collective-permute-start(bf16[2,280,1536]{2,1,0:T(8,128)(2,1)} %dynamic-slice_bitcast_fusion.2), channel_id=1, source_target_pairs={{0,1},{1,0},{2,3},{3,2},{4,5},{5,4},{6,7},{7,6},{8,9},{9,8},{10,11... | collective-permute-start | bytes 5160968 | tf_op jit(solution)/shard_map/ppermute | solution.py:878
  597.9 37.8 %collective-permute-start.3 = (bf16[8,48,1120]{2,1,0:T(8,128)(2,1)}, bf16[8,48,1120]{2,1,0:T(8,128)(2,1)}, u32[]{:S(2)}, u32[]{:S(2)}) collective-permute-start(bf16[8,48,1120]{2,1,0:T(8,128)(2,1)} %dynamic-slice_bitcast_fusion.3), channel_id=1, source_target_pairs={{0,16},{16,0},{1,17},{17,1},{2,18},{18,2},{3,19},{19,3},{4,20},{20... | collective-permute-start | bytes 2580488 | tf_op jit(solution)/shard_map/ppermute | solution.py:877
  598.7 4.5 copy-start.21
  598.7 4.5 copy-start.23
  603.2 5.3 copy-start.13
  603.2 5.3 copy-start.15
  608.5 4.7 copy-start.5
  613.2 24.9 %copy-start.10 = (bf16[2,2,280,1536]{3,2,1,0:T(8,128)(2,1)S(1)}, bf16[2,2,280,1536]{3,2,1,0:T(8,128)(2,1)}, u32[]{:S(2)}) copy-start(bf16[2,2,280,1536]{3,2,1,0:T(8,128)(2,1)} %copy-done.9) | copy-start | bytes 10321924
  640.0 75.2 %collective-permute-start.5 = (bf16[280,1536]{1,0:T(8,128)(2,1)S(1)}, bf16[280,1536]{1,0:T(8,128)(2,1)S(1)}, u32[]{:S(2)}, u32[]{:S(2)}) collective-permute-start(bf16[280,1536]{1,0:T(8,128)(2,1)S(1)} %dynamic-slice_bitcast_fusion.5), channel_id=1, source_target_pairs={{0,16},{16,0},{1,17},{17,1},{2,18},{18,2},{3,19},{19,3},{4,20},{20... | collective-permute-start | bytes 2580488 | tf_op jit(solution)/shard_map/ppermute | solution.py:877
  707.3 5.4 copy-start.24
  712.6 4.1 copy-start.17
  (14 other events, 34.1 us)

commit v7 on v4

--- a/solution.py
+++ b/solution.py
@@ -650,10 +650,10 @@
 def reduce_plan(kind, far, fsdp, tail):
     rows, columns = tail
     if kind == "group":
-        half = rows // 2
+        step = rows // 4
         return ("p", "y"), [
-            ((pl.ds(0, half), slice(None)), (half, columns), ("p", "y")),
-            ((pl.ds(half, half), slice(None)), (half, columns), ("y", "p")),
+            ((pl.ds(i * step, step), slice(None)), (step, columns), ("yp", "py")[i % 2])
+            for i in range(4)
         ]
     if kind in ("seq", "seq_turned"):
         order = ("y", "p", "h") if kind == "seq" else ("p", "y", "h")
@@ -897,7 +897,7 @@
         0,
         far,
         fsdp,
-        ("all", "all", "spread", "spread", "pair"),
+        ("all_y", "all", "spread", "spread", "pair"),
         (
             jnp.concatenate([query_weight, key_matrix, value_matrix], axis=1),
             vectors,
@@ -998,7 +998,6 @@
     grad_branch = grad_middle.astype(BF16)
     grad_branch, gate_sum, up_sum = lax.optimization_barrier((grad_branch, gate_sum, up_sum))
     gate_sum = over_h(gate_sum).astype(BF16)
-    up_sum = over_h(up_sum).astype(BF16)
     grad_attended = cols_dot(grad_branch, w_output).astype(BF16)
     grad_kvs, grad_query = [], []
     for m in range(micro):
@@ -1017,9 +1016,10 @@
         grad_query.append(query_part)
 
     blocks = (far, 2, 2, 2, fsdp, shard)
-    grad_kvs, gate_sum, hidden, hidden_turned = lax.optimization_barrier(
-        (grad_kvs, gate_sum, hidden, hidden_turned)
-    )
+    grad_kvs, gate_sum, up_sum, hidden, hidden_turned = lax.optimization_barrier(
+        (grad_kvs, gate_sum, up_sum, hidden, hidden_turned)
+    )
+    up_sum = over_h(up_sum).astype(BF16)
     down_part, _ = over_x(
         mat_dot(hidden_turned, upstream_all).reshape(far, fsdp, -1, width), 1, ()
     )

time: 714 us -> 698 us (0.978)
  waiting for transfers between devices: 40.5 us -> 27.2 us
    ppermute x3, waiting for transfers between devices: 33.3 us -> 15 us  [hop(): lax.ppermute(array, 'h', [(i, (i + shift) % far) for i in range(far)])]
  transfers between devices with their start and end apart: 6 -> 6, of which waited for: 2 -> 2; matrix products, arithmetic and copies ran while one was open for 14% -> 13% of each run, Pallas kernels for 29% -> 30%
where the time goes in v7:
time: 698 us; the launch traced here: 693 us
  Pallas kernels  475 us (68%)
  matrix products  103 us (15%)
  other arithmetic  35.1 us (5%)
  local copies, waits for them, and re-layouts  34.1 us (5%)
  waiting for transfers between devices  27.2 us (4%)
  starting transfers between devices  16.2 us (2%)
    pallas_call x3, Pallas kernels, move(): pl.pallas_call(functools.partial(move_kernel, kinds, far), out_shape=tupl...  222 us
    pallas_call x3, Pallas kernels, reduce(): pl.pallas_call(functools.partial(reduce_kernel, kinds, far, fsdp, tuple(c...  187 us
    dot_general x12, matrix products, dot(): lax.dot_general(left, right, ((dims[0], dims[1]), ((), ())), preferred_el...  103 us
    pallas_call x1, Pallas kernels, hidden_units(): pl.pallas_call(hidden_kernel, grid=(total // rows,), in_specs=[tile(width...  33.3 us
    ppermute x3, waiting for transfers between devices, hop(): lax.ppermute(array, 'h', [(i, (i + shift) % far) for i in range(far)])  15 us
  transfers between devices with their start and end apart: 6, of which 2 were waited for; matrix products, arithmetic and copies ran while one was open for 13% of the time, Pallas kernels for 30%

profile of v7, /device:TPU:0, one launch (start us, length us, event | category | flops | bytes accessed | tf_op | source)
XLA Modules:
  0.0 693.2 jit_solution(16763321840460412409)
XLA Ops:
  9.6 75.6 %gather_first.1 = (bf16[2,2,2,2,2,48,2048]{6,5,4,3,2,1,0:T(8,128)(2,1)}, f32[2,2,2,2,2,8,128]{6,5,4,3,2,1,0:T(8,128)}, bf16[8,48,1120]{2,1,0:T(8,128)(2,1)}, bf1...) custom-call(bf16[48,2048]{1,0:T(8,128)(2,1)} %pad_maximum_fusion.2.refs_0_, f32[8,128]{1,0:T(8,128)} %bitcast_convert_fusion.refs_1_, ...), custom_call_target="tpu_custom_call" | custom-call | bytes 1024 | tf_op jit(solution)/shard_map/gather_first/pallas_call | solution.py:630
  91.2 5.9 fusion.45.pre_ref
  102.2 112.3 %gather_second.1 = (bf16[2,2,2,2,128,512]{5,4,3,2,1,0:T(8,128)(2,1)}, bf16[2,2,2,2,128,512]{5,4,3,2,1,0:T(8,128)(2,1)}, bf16[2,2,2,2,2,48,1536]{6,5,4,3,2,1,0:T(...) custom-call(bf16[128,512]{1,0:T(8,128)(2,1)} %get-tuple-element.71.r, ...), custom_call_target="tpu_custom_call" | custom-call | bytes 1024 | tf_op jit(solution)/shard_map/gather_second/pallas_call | solution.py:630
  214.5 4.7 attend_forward.2
  230.8 34.1 %gather_tokens.1 = bf16[2,2,2,256,1536]{4,3,2,1,0:T(8,128)(2,1)} custom-call(bf16[256,1536]{1,0:T(8,128)(2,1)} %multiply_convert_fusion.refs_0_), custom_call_target="tpu_custom_call" | custom-call | bytes 1024 | tf_op jit(solution)/shard_map/gather_tokens/pallas_call | solution.py:630
  264.9 33.3 %hidden_units.1 = (bf16[1536,2048]{1,0:T(8,128)(2,1)}, bf16[2048,1120]{1,0:T(8,128)(2,1)}, bf16[1120,2048]{1,0:T(8,128)(2,1)}, bf16[2048,1120]{1,0:T(8,128)(2,1)}, bf16[2048,1120]{1,0:T(8,128)(2,1)}) custom-call(bf16[2048,1536]{1,0:T(8,128)(2,1)} %bitcast.175, bf16[2048,1536]{1,0:T(8,128)(2,1)} %bitcast.207, bf16[1536,1120]{1,0:T(8,128)(2,1)} %bitcast.213, ...), custom_call_target="tpu_custom_call" | custom-call | flops 21139292160 | bytes 25165824 | tf_op jit(solution)/shard_map/hidden_units/pallas_call | solution.py:263
  298.2 13.0 %fusion.6 = bf16[2,8,2,48,1120]{4,3,1,0,2:T(8,128)(2,1)} fusion(bf16[2048,1120]{1,0:T(8,128)(2,1)} %get-tuple-element.84, bf16[2,8,2,48,2048]{4,3,2,1,0:T(8,128)(2,1)} %bitcast.217), kind=kOutput, calls=%fused_computation.10 | convolution fusion | flops 7048151040 | bytes 14319616 | tf_op jit(solution)/shard_map/dot_general | solution.py:53
  314.2 12.0 %fusion.11 = bf16[2,8,2,48,1120]{4,3,1,0,2:T(8,128)(2,1)S(1)} fusion(bf16[2048,1120]{1,0:T(8,128)(2,1)} %get-tuple-element.88, bf16[2,8,2,48,2048]{4,3,2,1,0:T(8,128)(2,1)} %bitcast.218), kind=kOutput, calls=%fused_computation.11 | convolution fusion | flops 7048151040 | bytes 14319616 | tf_op jit(solution)/shard_map/dot_general | solution.py:53
  332.8 11.0 %fusion.46 = f32[2048,1536]{1,0:T(8,128)} fusion(bf16[2048,1120]{1,0:T(8,128)(2,1)S(1)} %bitcast.223, bf16[1536,1120]{1,0:T(8,128)(2,1)S(1)} %bitcast.214), kind=kOutput, calls=%fused_computation.115 | convolution fusion | flops 7046430720 | bytes 20611072 | tf_op jit(solution)/shard_map/dot_general | solution.py:53
  343.8 13.8 %add_convert_fusion = bf16[2048,1536]{1,0:T(8,128)(2,1)} fusion(f32[2048,1536]{1,0:T(8,128)} %fusion.46, bf16[2048,1120]{1,0:T(8,128)(2,1)} %get-tuple-element.88, bf16[1536,1120]{1,0:T(8,128)(2,1)S(1)} %bitcast.212), kind=kOutput, calls=%fused_computation | convolution fusion | flops 7052722176 | bytes 26902528 | tf_op jit(solution)/shard_map/dot_general | solution.py:53
  357.6 33.4 %reduce_tokens.1 = f32[256,1536]{1,0:T(8,128)} custom-call(bf16[2,2,2,256,1536]{4,3,2,1,0:T(8,128)(2,1)} %bitcast.176), custom_call_target="tpu_custom_call" | custom-call | bytes 1024 | tf_op jit(solution)/shard_map/reduce_tokens/pallas_call | solution.py:831
  397.9 12.2 %collective-permute-done = bf16[2,8,48,1120]{3,2,1,0:T(8,128)(2,1)} collective-permute-done((bf16[2,8,48,1120]{3,2,1,0:T(8,128)(2,1)}, bf16[2,8,48,1120]{3,2,1,0:T(8,128)(2,1)}, u32[]{:S(2)}, u32[]{:S(2)}) %collective-permute-start) | collective-permute-done | bytes 1720352 | tf_op jit(solution)/shard_map/ppermute | solution.py:882
  414.3 7.8 %collective-permute-start.2 = (bf16[8,48,1120]{2,1,0:T(8,128)(2,1)}, bf16[8,48,1120]{2,1,0:T(8,128)(2,1)}, u32[]{:S(2)}, u32[]{:S(2)}) collective-permute-start(bf16[8,48,1120]{2,1,0:T(8,128)(2,1)} %dynamic-slice_bitcast_fusion.4), channel_id=1, source_target_pairs={{0,16},{16,0},{1,17},{17,1},{2,18},{18,2},{3,19},{19,3},{4,20},{20... | collective-permute-start | bytes 2580488 | tf_op jit(solution)/shard_map/ppermute | solution.py:881
  423.3 4.9 convolution_convert_fusion.4.do_ref
  428.2 6.3 attend_backward.3
  434.5 6.2 attend_backward.2
  440.7 5.1 convolution_convert_fusion.2
  445.8 15.0 %collective-permute-done.2 = bf16[8,48,1120]{2,1,0:T(8,128)(2,1)} collective-permute-done((bf16[8,48,1120]{2,1,0:T(8,128)(2,1)}, bf16[8,48,1120]{2,1,0:T(8,128)(2,1)}, u32[]{:S(2)}, u32[]{:S(2)}) %collective-permute-start.2) | collective-permute-done | bytes 860192 | tf_op jit(solution)/shard_map/ppermute | solution.py:881
  463.1 10.9 %convolution_convert_fusion.3 = bf16[2,2,280,1536]{3,2,1,0:T(8,128)(2,1)S(1)} fusion(bf16[2,2,280,2048]{3,2,1,0:T(8,128)(2,1)} %bitcast.219, bf16[2048,1536,1,1]{1,0,3,2:T(8,128)(2,1)} %bitcast.208), kind=kOutput, calls=%fused_computation.12 | convolution fusion | flops 7048151040 | bytes 14319616 | tf_op jit(solution)/shard_map/dot_general | solution.py:53
  477.9 10.2 %convolution_convert_fusion.1 = bf16[2048,1536]{1,0:T(8,128)(2,1)} fusion(bf16[2048,1120]{1,0:T(8,128)(2,1)S(1)} %bitcast.221, bf16[1120,1536]{1,0:T(8,128)(2,1)S(1)} %bitcast.216), kind=kOutput, calls=%fused_computation.2 | convolution fusion | flops 7049576448 | bytes 14319616 | tf_op jit(solution)/shard_map/dot_general | solution.py:53
  488.1 88.3 %reduce_second.1 = (f32[128,512]{1,0:T(8,128)}, f32[128,512]{1,0:T(8,128)}, f32[48,1536]{1,0:T(8,128)}, f32[256,1536]{1,0:T(8,128)}) custom-call(bf16[2,2,2,2,128,512]{5,4,3,2,1,0:T(8,128)(2,1)} %bitcast.180, bf16[2,2,2,2,128,512]{5,4,3,2,1,0:T(8,128)(2,1)} %bitcast.179, bf16[2,2,2,2,2,48,1536]{6,5,4,3,2,1,0:T(8,128)(2,1)} %bitcast.167, ...), custom_call_target="tpu_custom_call" | custom-call | bytes 1024 | tf_op jit(solution)/shard_map/reduce_second/pallas_call | solution.py:831
  594.3 7.0 %fusion.31 = (f32[1536]{0:T(1024)}, f32[256]{0:T(256)}, bf16[256,1536]{1,0:T(8,128)(2,1)}, f32[256,1536]{1,0:T(8,128)}) fusion(bf16[1,2,128,1536]{3,2,1,0:T(8,128)(2,1)S(1)} %copy-done.4, f32[256]{0:T(256)} %get-tuple-element.143, f32[1536]{0:T(1024)} %copy-done.18, bf16[1536,2048]{1,0:T(8,128)(2,1)} %bitcast.206, bf16[256,512]{1,0:T(8,128)(2,1)} %rotate.3, ...), kind=kOutput, calls=%fused_computation.46 | convolution fusion | flops 1617688832 | bytes 10500096 | tf_op jit(solution)/shard_map/dot_general | solution.py:53
  605.6 5.6 convolution_convert_fusion
  611.2 65.1 %reduce_last.1 = (f32[48,2048]{1,0:T(8,128)}, f32[8,128]{1,0:T(8,128)}, bf16[8,48,1120]{2,1,0:T(8,128)(2,1)}, bf16[8,48,1120]{2,1,0:T(8,128)(2,1)}) custom-call(bf16[2,2,2,2,2,48,2048]{6,5,4,3,2,1,0:T(8,128)(2,1)} %bitcast.166, f32[2,2,2,2,2,8,128]{6,5,4,3,2,1,0:T(8,128)} %bitcast.184, bf16[8,48,1120]{2,1,0:T(8,128)(2,1)} %fusion.20.refs_2_, ...), custom_call_target="tpu_custom_call" | custom-call | bytes 1024 | tf_op jit(solution)/shard_map/reduce_last/pallas_call | solution.py:831
  (158 shorter events, 97.7 us)
Async XLA Ops:
  7.8 78.5 %copy-start.20 = (s32[1,2,4]{2,1,0:T(2,128)S(1)}, s32[1,2,4]{2,1,0:T(2,128)}, u32[]{:S(2)}) copy-start(s32[1,2,4]{2,1,0:T(2,128)} %param.16) | copy-start | bytes 100
  7.8 79.7 %copy-start.3 = (bf16[1,2,128,1536]{3,2,1,0:T(8,128)(2,1)S(1)}, bf16[1,2,128,1536]{3,2,1,0:T(8,128)(2,1)}, u32[]{:S(2)}) copy-start(bf16[1,2,128,1536]{3,2,1,0:T(8,128)(2,1)} %param.15) | copy-start | bytes 2359300
  87.5 9.5 %copy-start.18 = (f32[1536]{0:T(1024)}, f32[1536]{0:T(1024)S(1)}, u32[]{:S(2)}) copy-start(f32[1536]{0:T(1024)S(1)} %mul.213) | copy-start | bytes 18436
  311.2 21.6 %slice-start.2 = ((s8[4718592]{0:T(1024)(128)(4,1)}), s8[4194304]{0:T(1024)(128)(4,1)S(1)}, s32[]{:S(2)}) async-start(s8[4718592]{0:T(1024)(128)(4,1)} %bitcast.222), calls=%async_computation.2 | async-start | bytes 8388608
  314.2 18.6 %slice-start.3 = ((s8[4718592]{0:T(1024)(128)(4,1)}), s8[524288]{0:T(1024)(128)(4,1)S(1)}, s32[]{:S(2)}) async-start(s8[4718592]{0:T(1024)(128)(4,1)} %bitcast.222), calls=%async_computation.3 | async-start | bytes 1048576
  329.3 14.5 %copy-start.24 = (bf16[2,8,2,48,1120]{4,3,2,1,0:T(8,128)(2,1)S(1)}, bf16[2,8,2,48,1120]{4,3,2,1,0:T(8,128)(2,1)}, u32[]{:S(2)}) copy-start(bf16[2,8,2,48,1120]{4,3,2,1,0:T(8,128)(2,1)} %get-tuple-element.82) | copy-start | bytes 10321924
  329.3 65.7 %collective-permute-start.1 = (bf16[2,8,48,1120]{3,2,1,0:T(8,128)(2,1)}, bf16[2,8,48,1120]{3,2,1,0:T(8,128)(2,1)}, u32[]{:S(2)}, u32[]{:S(2)}) collective-permute-start(bf16[2,8,48,1120]{3,2,1,0:T(8,128)(2,1)} %dynamic-slice_bitcast_fusion), channel_id=1, source_target_pairs={{0,1},{1,0},{2,3},{3,2},{4,5},{5,4},{6,7},{7,6},{8,9},{9,8},{10,11... | collective-permute-start | bytes 5160968 | tf_op jit(solution)/shard_map/ppermute | solution.py:882
  332.7 77.4 %collective-permute-start = (bf16[2,8,48,1120]{3,2,1,0:T(8,128)(2,1)}, bf16[2,8,48,1120]{3,2,1,0:T(8,128)(2,1)}, u32[]{:S(2)}, u32[]{:S(2)}) collective-permute-start(bf16[2,8,48,1120]{3,2,1,0:T(8,128)(2,1)} %dynamic-slice_bitcast_fusion.1), channel_id=1, source_target_pairs={{0,1},{1,0},{2,3},{3,2},{4,5},{5,4},{6,7},{7,6},{8,9},{9,8},{10,11... | collective-permute-start | bytes 5160968 | tf_op jit(solution)/shard_map/ppermute | solution.py:882
  395.0 15.1 %copy-start.5 = (bf16[2,8,2,48,1120]{4,3,1,0,2:T(8,128)(2,1)S(1)}, bf16[2,8,2,48,1120]{4,3,1,0,2:T(8,128)(2,1)}, u32[]{:S(2)}) copy-start(bf16[2,8,2,48,1120]{4,3,1,0,2:T(8,128)(2,1)} %fusion.6) | copy-start | bytes 10321924
  414.3 46.5 %collective-permute-start.2 = (bf16[8,48,1120]{2,1,0:T(8,128)(2,1)}, bf16[8,48,1120]{2,1,0:T(8,128)(2,1)}, u32[]{:S(2)}, u32[]{:S(2)}) collective-permute-start(bf16[8,48,1120]{2,1,0:T(8,128)(2,1)} %dynamic-slice_bitcast_fusion.4), channel_id=1, source_target_pairs={{0,16},{16,0},{1,17},{17,1},{2,18},{18,2},{3,19},{19,3},{4,20},{20... | collective-permute-start | bytes 2580488 | tf_op jit(solution)/shard_map/ppermute | solution.py:881
  440.7 20.1 %copy-start.2 = (bf16[2,8,48,1120]{3,2,1,0:T(8,128)(2,1)S(1)}, bf16[2,8,48,1120]{3,2,1,0:T(8,128)(2,1)}, u32[]{:S(2)}) copy-start(bf16[2,8,48,1120]{3,2,1,0:T(8,128)(2,1)} %copy-done.1) | copy-start | bytes 5160964
  440.7 37.1 %slice-start = ((s8[4718592]{0:T(1024)(128)(4,1)}), s8[4194304]{0:T(1024)(128)(4,1)S(1)}, s32[]{:S(2)}) async-start(s8[4718592]{0:T(1024)(128)(4,1)} %bitcast.220), calls=%async_computation | async-start | bytes 8388608
  463.1 14.7 %slice-start.1 = ((s8[4718592]{0:T(1024)(128)(4,1)}), s8[524288]{0:T(1024)(128)(4,1)S(1)}, s32[]{:S(2)}) async-start(s8[4718592]{0:T(1024)(128)(4,1)} %bitcast.220), calls=%async_computation.1 | async-start | bytes 1048576
  475.3 106.0 %collective-permute-start.3 = (bf16[2,280,1536]{2,1,0:T(8,128)(2,1)}, bf16[2,280,1536]{2,1,0:T(8,128)(2,1)}, u32[]{:S(2)}, u32[]{:S(2)}) collective-permute-start(bf16[2,280,1536]{2,1,0:T(8,128)(2,1)} %dynamic-slice_bitcast_fusion.2), channel_id=1, source_target_pairs={{0,1},{1,0},{2,3},{3,2},{4,5},{5,4},{6,7},{7,6},{8,9},{9,8},{10,11... | collective-permute-start | bytes 5160968 | tf_op jit(solution)/shard_map/ppermute | solution.py:882
  477.7 101.3 %collective-permute-start.4 = (bf16[8,48,1120]{2,1,0:T(8,128)(2,1)}, bf16[8,48,1120]{2,1,0:T(8,128)(2,1)}, u32[]{:S(2)}, u32[]{:S(2)}) collective-permute-start(bf16[8,48,1120]{2,1,0:T(8,128)(2,1)} %dynamic-slice_bitcast_fusion.3), channel_id=1, source_target_pairs={{0,16},{16,0},{1,17},{17,1},{2,18},{18,2},{3,19},{19,3},{4,20},{20... | collective-permute-start | bytes 2580488 | tf_op jit(solution)/shard_map/ppermute | solution.py:881
  583.3 7.9 %copy-start.13 = (bf16[128,1536]{1,0:T(8,128)(2,1)S(1)}, bf16[128,1536]{1,0:T(8,128)(2,1)}, u32[]{:S(2)}) copy-start(bf16[128,1536]{1,0:T(8,128)(2,1)} %get-tuple-element.103) | copy-start | bytes 1179652
  583.3 7.8 %copy-start.14 = (bf16[128,1536]{1,0:T(8,128)(2,1)S(1)}, bf16[128,1536]{1,0:T(8,128)(2,1)}, u32[]{:S(2)}) copy-start(bf16[128,1536]{1,0:T(8,128)(2,1)} %get-tuple-element.102) | copy-start | bytes 1179652
  583.3 11.0 %copy-start.4 = (bf16[1,2,128,1536]{3,2,1,0:T(8,128)(2,1)S(1)}, bf16[1,2,128,1536]{3,2,1,0:T(8,128)(2,1)}, u32[]{:S(2)}) copy-start(bf16[1,2,128,1536]{3,2,1,0:T(8,128)(2,1)} %param.15) | copy-start | bytes 2359300
  584.3 105.1 %collective-permute-start.5 = (bf16[280,1536]{1,0:T(8,128)(2,1)}, bf16[280,1536]{1,0:T(8,128)(2,1)}, u32[]{:S(2)}, u32[]{:S(2)}) collective-permute-start(bf16[280,1536]{1,0:T(8,128)(2,1)} %dynamic-slice_bitcast_fusion.5), channel_id=1, source_target_pairs={{0,16},{16,0},{1,17},{17,1},{2,18},{18,2},{3,19},{19,3},{4,20},{20... | collective-permute-start | bytes 2580488 | tf_op jit(solution)/shard_map/ppermute | solution.py:881
  594.3 11.3 %copy-start.12 = (bf16[256,512]{1,0:T(8,128)(2,1)S(1)}, bf16[256,512]{1,0:T(8,128)(2,1)}, u32[]{:S(2)}) copy-start(bf16[256,512]{1,0:T(8,128)(2,1)} %rotate.3) | copy-start | bytes 786436
  611.2 68.0 %copy-start.23 = (f32[256]{0:T(256)S(1)}, f32[256]{0:T(256)}, u32[]{:S(2)}) copy-start(f32[256]{0:T(256)} %get-tuple-element.121) | copy-start | bytes 3076
  676.4 9.6 %copy-start.19 = (f32[1536]{0:T(1024)S(1)}, f32[1536]{0:T(1024)}, u32[]{:S(2)}) copy-start(f32[1536]{0:T(1024)} %copy-done.18) | copy-start | bytes 18436
  676.4 9.6 %copy-start.21 = (f32[256]{0:T(256)S(1)}, f32[256]{0:T(256)}, u32[]{:S(2)}) copy-start(f32[256]{0:T(256)} %get-tuple-element.143) | copy-start | bytes 3076
  676.4 9.6 %copy-start.22 = (f32[256]{0:T(256)S(1)}, f32[256]{0:T(256)}, u32[]{:S(2)}) copy-start(f32[256]{0:T(256)} %multiply_multiply_fusion) | copy-start | bytes 3076
  (13 other events, 47.0 us)

commit v8 on v7

--- a/solution.py
+++ b/solution.py
@@ -339,7 +339,7 @@
 
 
 MESH = pl.DeviceIdType.MESH
-PARTS, AHEAD = 4, 2
+PARTS, AHEAD = {"pair": 4, "pair8": 8}, 2
 COST = 1024
 ANY = pl.BlockSpec(memory_space=pl.ANY)
 
@@ -584,8 +584,8 @@
         elif kind in ("pair", "pair8"):
             local = outs[i].at[ih, :, ix] if kind == "pair8" else outs[i].at[ih, ix]
             local = local_copy(i, sources[i], local)
-            step = (8 if kind == "pair8" else sources[i].shape[1]) // PARTS
-            cuts = [pl.ds(part * step, step) for part in range(PARTS)]
+            step = (8 if kind == "pair8" else sources[i].shape[1]) // PARTS[kind]
+            cuts = [pl.ds(part * step, step) for part in range(PARTS[kind])]
             if kind == "pair8":
                 parts = [sources[i].at[c] for c in cuts]
             else:
@@ -594,7 +594,7 @@
             def place(h, x, part, out=outs[i], cuts=cuts, wide=kind == "pair8"):
                 return out.at[h, cuts[part], x] if wide else out.at[h, x, :, cuts[part]]
 
-            wait = (PARTS - AHEAD + 1) * kinds[:i].count("pair8")
+            wait = (PARTS[kind] - AHEAD + 1) * kinds[:i].count("pair8")
             running.append(pair_steps(far, copies, parts, place, local, wait))
         else:
             place = (ih, ip, iy, ic) if kind == "seq" else (ih, ip, iy, ic, ix)
@@ -620,9 +620,9 @@
         elif kind == "group":
             lead, total = (2, 2, 2), total + 13
         elif kind == "pair":
-            lead, total = (far, fsdp), total + PARTS * (2 * far - 1)
+            lead, total = (far, fsdp), total + PARTS[kind] * (2 * far - 1)
         elif kind == "pair8":
-            lead, total = (far, 8, fsdp), total + PARTS * (2 * far - 1)
+            lead, total = (far, 8, fsdp), total + PARTS[kind] * (2 * far - 1)
         else:
             lead, total = (), total + 7
         tail = array.shape[1:] if kind == "pair8" else array.shape

time: 698 us -> 720 us (1.032)
  Pallas kernels: 475 us -> 496 us
    pallas_call x3, Pallas kernels: 222 us -> 244 us  [move(): pl.pallas_call(functools.partial(move_kernel, kinds, far), out_shape=tupl...]
  transfers between devices with their start and end apart: 6 -> 6, of which waited for: 2 -> 2; matrix products, arithmetic and copies ran while one was open for 13% -> 12% of each run, Pallas kernels for 30% -> 29%
where the time goes in v8:
time: 720 us; the launch traced here: 711 us
  Pallas kernels  496 us (69%)
  matrix products  103 us (14%)
  other arithmetic  35.1 us (5%)
  local copies, waits for them, and re-layouts  33.9 us (5%)
  waiting for transfers between devices  23 us (3%)
  starting transfers between devices  18.6 us (3%)
    pallas_call x3, Pallas kernels, move(): pl.pallas_call(functools.partial(move_kernel, kinds, far), out_shape=tupl...  244 us
    pallas_call x3, Pallas kernels, reduce(): pl.pallas_call(functools.partial(reduce_kernel, kinds, far, fsdp, tuple(c...  186 us
    dot_general x12, matrix products, dot(): lax.dot_general(left, right, ((dims[0], dims[1]), ((), ())), preferred_el...  103 us
    pallas_call x1, Pallas kernels, hidden_units(): pl.pallas_call(hidden_kernel, grid=(total // rows,), in_specs=[tile(width...  33.3 us
    ppermute x3, starting transfers between devices, hop(): lax.ppermute(array, 'h', [(i, (i + shift) % far) for i in range(far)])  15.4 us
  transfers between devices with their start and end apart: 6, of which 2 were waited for; matrix products, arithmetic and copies ran while one was open for 12% of the time, Pallas kernels for 29%

profile of v8, /device:TPU:0, one launch (start us, length us, event | category | flops | bytes accessed | tf_op | source)
XLA Modules:
  0.0 711.4 jit_solution(16746145140676312418)
XLA Ops:
  9.6 75.6 %gather_first.1 = (bf16[2,2,2,2,2,48,2048]{6,5,4,3,2,1,0:T(8,128)(2,1)}, f32[2,2,2,2,2,8,128]{6,5,4,3,2,1,0:T(8,128)}, bf16[8,48,1120]{2,1,0:T(8,128)(2,1)}, bf1...) custom-call(bf16[48,2048]{1,0:T(8,128)(2,1)} %pad_maximum_fusion.2.refs_0_, f32[8,128]{1,0:T(8,128)} %bitcast_convert_fusion.refs_1_, ...), custom_call_target="tpu_custom_call" | custom-call | bytes 1024 | tf_op jit(solution)/shard_map/gather_first/pallas_call | solution.py:630
  91.2 5.9 fusion.45.pre_ref
  102.2 133.2 %gather_second.1 = (bf16[2,2,2,2,128,512]{5,4,3,2,1,0:T(8,128)(2,1)}, bf16[2,2,2,2,128,512]{5,4,3,2,1,0:T(8,128)(2,1)}, bf16[2,2,2,2,2,48,1536]{6,5,4,3,2,1,0:T(...) custom-call(bf16[128,512]{1,0:T(8,128)(2,1)} %get-tuple-element.71.r, ...), custom_call_target="tpu_custom_call" | custom-call | bytes 1024 | tf_op jit(solution)/shard_map/gather_second/pallas_call | solution.py:630
  235.4 4.7 attend_forward.2
  251.6 34.7 %gather_tokens.1 = bf16[2,2,2,256,1536]{4,3,2,1,0:T(8,128)(2,1)} custom-call(bf16[256,1536]{1,0:T(8,128)(2,1)} %multiply_convert_fusion.refs_0_), custom_call_target="tpu_custom_call" | custom-call | bytes 1024 | tf_op jit(solution)/shard_map/gather_tokens/pallas_call | solution.py:630
  286.4 33.3 %hidden_units.1 = (bf16[1536,2048]{1,0:T(8,128)(2,1)}, bf16[2048,1120]{1,0:T(8,128)(2,1)}, bf16[1120,2048]{1,0:T(8,128)(2,1)}, bf16[2048,1120]{1,0:T(8,128)(2,1)}, bf16[2048,1120]{1,0:T(8,128)(2,1)}) custom-call(bf16[2048,1536]{1,0:T(8,128)(2,1)} %bitcast.175, bf16[2048,1536]{1,0:T(8,128)(2,1)} %bitcast.207, bf16[1536,1120]{1,0:T(8,128)(2,1)} %bitcast.213, ...), custom_call_target="tpu_custom_call" | custom-call | flops 21139292160 | bytes 25165824 | tf_op jit(solution)/shard_map/hidden_units/pallas_call | solution.py:263
  319.6 13.0 %fusion.6 = bf16[2,8,2,48,1120]{4,3,1,0,2:T(8,128)(2,1)} fusion(bf16[2048,1120]{1,0:T(8,128)(2,1)} %get-tuple-element.84, bf16[2,8,2,48,2048]{4,3,2,1,0:T(8,128)(2,1)} %bitcast.217), kind=kOutput, calls=%fused_computation.10 | convolution fusion | flops 7048151040 | bytes 14319616 | tf_op jit(solution)/shard_map/dot_general | solution.py:53
  335.6 12.0 %fusion.11 = bf16[2,8,2,48,1120]{4,3,1,0,2:T(8,128)(2,1)S(1)} fusion(bf16[2048,1120]{1,0:T(8,128)(2,1)} %get-tuple-element.88, bf16[2,8,2,48,2048]{4,3,2,1,0:T(8,128)(2,1)} %bitcast.218), kind=kOutput, calls=%fused_computation.11 | convolution fusion | flops 7048151040 | bytes 14319616 | tf_op jit(solution)/shard_map/dot_general | solution.py:53
  352.9 11.0 %fusion.46 = f32[2048,1536]{1,0:T(8,128)} fusion(bf16[2048,1120]{1,0:T(8,128)(2,1)S(1)} %bitcast.223, bf16[1536,1120]{1,0:T(8,128)(2,1)S(1)} %bitcast.214), kind=kOutput, calls=%fused_computation.115 | convolution fusion | flops 7046430720 | bytes 20611072 | tf_op jit(solution)/shard_map/dot_general | solution.py:53
  364.0 13.8 %add_convert_fusion = bf16[2048,1536]{1,0:T(8,128)(2,1)} fusion(f32[2048,1536]{1,0:T(8,128)} %fusion.46, bf16[2048,1120]{1,0:T(8,128)(2,1)} %get-tuple-element.88, bf16[1536,1120]{1,0:T(8,128)(2,1)S(1)} %bitcast.212), kind=kOutput, calls=%fused_computation | convolution fusion | flops 7052722176 | bytes 26902528 | tf_op jit(solution)/shard_map/dot_general | solution.py:53
  377.8 33.4 %reduce_tokens.1 = f32[256,1536]{1,0:T(8,128)} custom-call(bf16[2,2,2,256,1536]{4,3,2,1,0:T(8,128)(2,1)} %bitcast.176), custom_call_target="tpu_custom_call" | custom-call | bytes 1024 | tf_op jit(solution)/shard_map/reduce_tokens/pallas_call | solution.py:831
  418.1 12.2 %collective-permute-done = bf16[2,8,48,1120]{3,2,1,0:T(8,128)(2,1)} collective-permute-done((bf16[2,8,48,1120]{3,2,1,0:T(8,128)(2,1)}, bf16[2,8,48,1120]{3,2,1,0:T(8,128)(2,1)}, u32[]{:S(2)}, u32[]{:S(2)}) %collective-permute-start) | collective-permute-done | bytes 1720352 | tf_op jit(solution)/shard_map/ppermute | solution.py:882
  434.4 8.6 %collective-permute-start.2 = (bf16[8,48,1120]{2,1,0:T(8,128)(2,1)}, bf16[8,48,1120]{2,1,0:T(8,128)(2,1)}, u32[]{:S(2)}, u32[]{:S(2)}) collective-permute-start(bf16[8,48,1120]{2,1,0:T(8,128)(2,1)} %dynamic-slice_bitcast_fusion.4), channel_id=1, source_target_pairs={{0,16},{16,0},{1,17},{17,1},{2,18},{18,2},{3,19},{19,3},{4,20},{20... | collective-permute-start | bytes 2580488 | tf_op jit(solution)/shard_map/ppermute | solution.py:881
  444.2 4.9 convolution_convert_fusion.4.do_ref
  449.1 6.3 attend_backward.3
  455.4 6.2 attend_backward.2
  461.6 5.1 convolution_convert_fusion.2
  466.7 10.8 %collective-permute-done.2 = bf16[8,48,1120]{2,1,0:T(8,128)(2,1)} collective-permute-done((bf16[8,48,1120]{2,1,0:T(8,128)(2,1)}, bf16[8,48,1120]{2,1,0:T(8,128)(2,1)}, u32[]{:S(2)}, u32[]{:S(2)}) %collective-permute-start.2) | collective-permute-done | bytes 860192 | tf_op jit(solution)/shard_map/ppermute | solution.py:881
  479.7 10.9 %convolution_convert_fusion.3 = bf16[2,2,280,1536]{3,2,1,0:T(8,128)(2,1)S(1)} fusion(bf16[2,2,280,2048]{3,2,1,0:T(8,128)(2,1)} %bitcast.219, bf16[2048,1536,1,1]{1,0,3,2:T(8,128)(2,1)} %bitcast.208), kind=kOutput, calls=%fused_computation.12 | convolution fusion | flops 7048151040 | bytes 14319616 | tf_op jit(solution)/shard_map/dot_general | solution.py:53
  497.4 10.2 %convolution_convert_fusion.1 = bf16[2048,1536]{1,0:T(8,128)(2,1)} fusion(bf16[2048,1120]{1,0:T(8,128)(2,1)S(1)} %bitcast.221, bf16[1120,1536]{1,0:T(8,128)(2,1)S(1)} %bitcast.216), kind=kOutput, calls=%fused_computation.2 | convolution fusion | flops 7049576448 | bytes 14319616 | tf_op jit(solution)/shard_map/dot_general | solution.py:53
  507.7 87.7 %reduce_second.1 = (f32[128,512]{1,0:T(8,128)}, f32[128,512]{1,0:T(8,128)}, f32[48,1536]{1,0:T(8,128)}, f32[256,1536]{1,0:T(8,128)}) custom-call(bf16[2,2,2,2,128,512]{5,4,3,2,1,0:T(8,128)(2,1)} %bitcast.180, bf16[2,2,2,2,128,512]{5,4,3,2,1,0:T(8,128)(2,1)} %bitcast.179, bf16[2,2,2,2,2,48,1536]{6,5,4,3,2,1,0:T(8,128)(2,1)} %bitcast.167, ...), custom_call_target="tpu_custom_call" | custom-call | bytes 1024 | tf_op jit(solution)/shard_map/reduce_second/pallas_call | solution.py:831
  613.2 7.0 fusion.31
  624.4 5.6 convolution_convert_fusion
  630.0 64.6 %reduce_last.1 = (f32[48,2048]{1,0:T(8,128)}, f32[8,128]{1,0:T(8,128)}, bf16[8,48,1120]{2,1,0:T(8,128)(2,1)}, bf16[8,48,1120]{2,1,0:T(8,128)(2,1)}) custom-call(bf16[2,2,2,2,2,48,2048]{6,5,4,3,2,1,0:T(8,128)(2,1)} %bitcast.166, f32[2,2,2,2,2,8,128]{6,5,4,3,2,1,0:T(8,128)} %bitcast.184, bf16[8,48,1120]{2,1,0:T(8,128)(2,1)} %fusion.20.refs_2_, ...), custom_call_target="tpu_custom_call" | custom-call | bytes 1024 | tf_op jit(solution)/shard_map/reduce_last/pallas_call | solution.py:831
  (158 shorter events, 99.2 us)
Async XLA Ops:
  7.8 78.5 %copy-start.20 = (s32[1,2,4]{2,1,0:T(2,128)S(1)}, s32[1,2,4]{2,1,0:T(2,128)}, u32[]{:S(2)}) copy-start(s32[1,2,4]{2,1,0:T(2,128)} %param.16) | copy-start | bytes 100
  7.8 79.7 %copy-start.3 = (bf16[1,2,128,1536]{3,2,1,0:T(8,128)(2,1)S(1)}, bf16[1,2,128,1536]{3,2,1,0:T(8,128)(2,1)}, u32[]{:S(2)}) copy-start(bf16[1,2,128,1536]{3,2,1,0:T(8,128)(2,1)} %param.15) | copy-start | bytes 2359300
  87.5 9.5 %copy-start.18 = (f32[1536]{0:T(1024)}, f32[1536]{0:T(1024)S(1)}, u32[]{:S(2)}) copy-start(f32[1536]{0:T(1024)S(1)} %mul.213) | copy-start | bytes 18436
  332.6 20.3 %slice-start.2 = ((s8[4718592]{0:T(1024)(128)(4,1)}), s8[4194304]{0:T(1024)(128)(4,1)S(1)}, s32[]{:S(2)}) async-start(s8[4718592]{0:T(1024)(128)(4,1)} %bitcast.222), calls=%async_computation.2 | async-start | bytes 8388608
  335.6 17.3 %slice-start.3 = ((s8[4718592]{0:T(1024)(128)(4,1)}), s8[524288]{0:T(1024)(128)(4,1)S(1)}, s32[]{:S(2)}) async-start(s8[4718592]{0:T(1024)(128)(4,1)} %bitcast.222), calls=%async_computation.3 | async-start | bytes 1048576
  350.7 13.3 %copy-start.24 = (bf16[2,8,2,48,1120]{4,3,2,1,0:T(8,128)(2,1)S(1)}, bf16[2,8,2,48,1120]{4,3,2,1,0:T(8,128)(2,1)}, u32[]{:S(2)}) copy-start(bf16[2,8,2,48,1120]{4,3,2,1,0:T(8,128)(2,1)} %get-tuple-element.82) | copy-start | bytes 10321924
  350.7 64.4 %collective-permute-start.1 = (bf16[2,8,48,1120]{3,2,1,0:T(8,128)(2,1)}, bf16[2,8,48,1120]{3,2,1,0:T(8,128)(2,1)}, u32[]{:S(2)}, u32[]{:S(2)}) collective-permute-start(bf16[2,8,48,1120]{3,2,1,0:T(8,128)(2,1)} %dynamic-slice_bitcast_fusion), channel_id=1, source_target_pairs={{0,1},{1,0},{2,3},{3,2},{4,5},{5,4},{6,7},{7,6},{8,9},{9,8},{10,11... | collective-permute-start | bytes 5160968 | tf_op jit(solution)/shard_map/ppermute | solution.py:882
  352.9 77.4 %collective-permute-start = (bf16[2,8,48,1120]{3,2,1,0:T(8,128)(2,1)}, bf16[2,8,48,1120]{3,2,1,0:T(8,128)(2,1)}, u32[]{:S(2)}, u32[]{:S(2)}) collective-permute-start(bf16[2,8,48,1120]{3,2,1,0:T(8,128)(2,1)} %dynamic-slice_bitcast_fusion.1), channel_id=1, source_target_pairs={{0,1},{1,0},{2,3},{3,2},{4,5},{5,4},{6,7},{7,6},{8,9},{9,8},{10,11... | collective-permute-start | bytes 5160968 | tf_op jit(solution)/shard_map/ppermute | solution.py:882
  415.1 15.1 %copy-start.5 = (bf16[2,8,2,48,1120]{4,3,1,0,2:T(8,128)(2,1)S(1)}, bf16[2,8,2,48,1120]{4,3,1,0,2:T(8,128)(2,1)}, u32[]{:S(2)}) copy-start(bf16[2,8,2,48,1120]{4,3,1,0,2:T(8,128)(2,1)} %fusion.6) | copy-start | bytes 10321924
  434.4 43.0 %collective-permute-start.2 = (bf16[8,48,1120]{2,1,0:T(8,128)(2,1)}, bf16[8,48,1120]{2,1,0:T(8,128)(2,1)}, u32[]{:S(2)}, u32[]{:S(2)}) collective-permute-start(bf16[8,48,1120]{2,1,0:T(8,128)(2,1)} %dynamic-slice_bitcast_fusion.4), channel_id=1, source_target_pairs={{0,16},{16,0},{1,17},{17,1},{2,18},{18,2},{3,19},{19,3},{4,20},{20... | collective-permute-start | bytes 2580488 | tf_op jit(solution)/shard_map/ppermute | solution.py:881
  461.6 15.8 %copy-start.2 = (bf16[2,8,48,1120]{3,2,1,0:T(8,128)(2,1)S(1)}, bf16[2,8,48,1120]{3,2,1,0:T(8,128)(2,1)}, u32[]{:S(2)}) copy-start(bf16[2,8,48,1120]{3,2,1,0:T(8,128)(2,1)} %copy-done.1) | copy-start | bytes 5160964
  461.6 35.8 %slice-start = ((s8[4718592]{0:T(1024)(128)(4,1)}), s8[4194304]{0:T(1024)(128)(4,1)S(1)}, s32[]{:S(2)}) async-start(s8[4718592]{0:T(1024)(128)(4,1)} %bitcast.220), calls=%async_computation | async-start | bytes 8388608
  479.7 17.7 %slice-start.1 = ((s8[4718592]{0:T(1024)(128)(4,1)}), s8[524288]{0:T(1024)(128)(4,1)S(1)}, s32[]{:S(2)}) async-start(s8[4718592]{0:T(1024)(128)(4,1)} %bitcast.220), calls=%async_computation.1 | async-start | bytes 1048576
  491.9 108.4 %collective-permute-start.3 = (bf16[2,280,1536]{2,1,0:T(8,128)(2,1)}, bf16[2,280,1536]{2,1,0:T(8,128)(2,1)}, u32[]{:S(2)}, u32[]{:S(2)}) collective-permute-start(bf16[2,280,1536]{2,1,0:T(8,128)(2,1)} %dynamic-slice_bitcast_fusion.2), channel_id=1, source_target_pairs={{0,1},{1,0},{2,3},{3,2},{4,5},{5,4},{6,7},{7,6},{8,9},{9,8},{10,11... | collective-permute-start | bytes 5160968 | tf_op jit(solution)/shard_map/ppermute | solution.py:882
  493.8 104.2 %collective-permute-start.4 = (bf16[8,48,1120]{2,1,0:T(8,128)(2,1)}, bf16[8,48,1120]{2,1,0:T(8,128)(2,1)}, u32[]{:S(2)}, u32[]{:S(2)}) collective-permute-start(bf16[8,48,1120]{2,1,0:T(8,128)(2,1)} %dynamic-slice_bitcast_fusion.3), channel_id=1, source_target_pairs={{0,16},{16,0},{1,17},{17,1},{2,18},{18,2},{3,19},{19,3},{4,20},{20... | collective-permute-start | bytes 2580488 | tf_op jit(solution)/shard_map/ppermute | solution.py:881
  602.3 7.7 %copy-start.13 = (bf16[128,1536]{1,0:T(8,128)(2,1)S(1)}, bf16[128,1536]{1,0:T(8,128)(2,1)}, u32[]{:S(2)}) copy-start(bf16[128,1536]{1,0:T(8,128)(2,1)} %get-tuple-element.103) | copy-start | bytes 1179652
  602.3 7.7 %copy-start.14 = (bf16[128,1536]{1,0:T(8,128)(2,1)S(1)}, bf16[128,1536]{1,0:T(8,128)(2,1)}, u32[]{:S(2)}) copy-start(bf16[128,1536]{1,0:T(8,128)(2,1)} %get-tuple-element.102) | copy-start | bytes 1179652
  602.3 10.9 %copy-start.4 = (bf16[1,2,128,1536]{3,2,1,0:T(8,128)(2,1)S(1)}, bf16[1,2,128,1536]{3,2,1,0:T(8,128)(2,1)}, u32[]{:S(2)}) copy-start(bf16[1,2,128,1536]{3,2,1,0:T(8,128)(2,1)} %param.15) | copy-start | bytes 2359300
  603.3 104.4 %collective-permute-start.5 = (bf16[280,1536]{1,0:T(8,128)(2,1)}, bf16[280,1536]{1,0:T(8,128)(2,1)}, u32[]{:S(2)}, u32[]{:S(2)}) collective-permute-start(bf16[280,1536]{1,0:T(8,128)(2,1)} %dynamic-slice_bitcast_fusion.5), channel_id=1, source_target_pairs={{0,16},{16,0},{1,17},{17,1},{2,18},{18,2},{3,19},{19,3},{4,20},{20... | collective-permute-start | bytes 2580488 | tf_op jit(solution)/shard_map/ppermute | solution.py:881
  613.2 11.3 %copy-start.12 = (bf16[256,512]{1,0:T(8,128)(2,1)S(1)}, bf16[256,512]{1,0:T(8,128)(2,1)}, u32[]{:S(2)}) copy-start(bf16[256,512]{1,0:T(8,128)(2,1)} %rotate.3) | copy-start | bytes 786436
  630.0 67.4 %copy-start.23 = (f32[256]{0:T(256)S(1)}, f32[256]{0:T(256)}, u32[]{:S(2)}) copy-start(f32[256]{0:T(256)} %get-tuple-element.121) | copy-start | bytes 3076
  694.6 9.6 %copy-start.19 = (f32[1536]{0:T(1024)S(1)}, f32[1536]{0:T(1024)}, u32[]{:S(2)}) copy-start(f32[1536]{0:T(1024)} %copy-done.18) | copy-start | bytes 18436
  694.6 9.6 %copy-start.21 = (f32[256]{0:T(256)S(1)}, f32[256]{0:T(256)}, u32[]{:S(2)}) copy-start(f32[256]{0:T(256)} %get-tuple-element.143) | copy-start | bytes 3076
  694.6 9.6 %copy-start.22 = (f32[256]{0:T(256)S(1)}, f32[256]{0:T(256)}, u32[]{:S(2)}) copy-start(f32[256]{0:T(256)} %multiply_multiply_fusion) | copy-start | bytes 3076
  (13 other events, 47.8 us)

commit v9 on v8

--- a/solution.py
+++ b/solution.py
@@ -339,7 +339,7 @@
 
 
 MESH = pl.DeviceIdType.MESH
-PARTS, AHEAD = {"pair": 4, "pair8": 8}, 2
+PARTS, AHEAD = {"pair": 4, "pair8": 2}, {"pair": 2, "pair8": 1}
 COST = 1024
 ANY = pl.BlockSpec(memory_space=pl.ANY)
 
@@ -499,7 +499,7 @@
     local.wait()
 
 
-def pair_steps(far, copies, parts, place, local, delay):
+def pair_steps(far, copies, parts, place, local, delay, ahead):
     ih, ix = lax.axis_index("h"), lax.axis_index("x")
     local.start()
     for _ in range(delay):
@@ -512,11 +512,11 @@
             arrived.append([copies.start(parts[i], target, other_h(far, k)) for k in range(1, far)])
             sent.append(copies.start(parts[i], target, flip("x")))
 
-    for i in range(AHEAD):
+    for i in range(ahead):
         send(i)
     for i in range(len(parts)):
         yield
-        send(i + AHEAD)
+        send(i + ahead)
         for k in range(1, far):
             arrived[i][k - 1].wait_recv()
             ref = place(lax.rem(ih - k + far, far), ix, i)
@@ -594,8 +594,8 @@
             def place(h, x, part, out=outs[i], cuts=cuts, wide=kind == "pair8"):
                 return out.at[h, cuts[part], x] if wide else out.at[h, x, :, cuts[part]]
 
-            wait = (PARTS[kind] - AHEAD + 1) * kinds[:i].count("pair8")
-            running.append(pair_steps(far, copies, parts, place, local, wait))
+            wait = (PARTS[kind] - AHEAD[kind] + 1) * kinds[:i].count("pair8")
+            running.append(pair_steps(far, copies, parts, place, local, wait, AHEAD[kind]))
         else:
             place = (ih, ip, iy, ic) if kind == "seq" else (ih, ip, iy, ic, ix)
             local = local_copy(i, sources[i], outs[i].at[place])

time: 720 us -> 709 us (0.985)
    pallas_call x3, Pallas kernels: 244 us -> 235 us  [move(): pl.pallas_call(functools.partial(move_kernel, kinds, far), out_shape=tupl...]
  transfers between devices with their start and end apart: 6 -> 6, of which waited for: 2 -> 2; matrix products, arithmetic and copies ran while one was open for 12% -> 13% of each run, Pallas kernels for 29% -> 29%
where the time goes in v9:
time: 709 us; the launch traced here: 705 us
  Pallas kernels  490 us (69%)
  matrix products  103 us (15%)
  other arithmetic  35.1 us (5%)
  local copies, waits for them, and re-layouts  33.9 us (5%)
  waiting for transfers between devices  26.5 us (4%)
  starting transfers between devices  13.8 us (2%)
    pallas_call x3, Pallas kernels, move(): pl.pallas_call(functools.partial(move_kernel, kinds, far), out_shape=tupl...  235 us
    pallas_call x3, Pallas kernels, reduce(): pl.pallas_call(functools.partial(reduce_kernel, kinds, far, fsdp, tuple(c...  188 us
    dot_general x12, matrix products, dot(): lax.dot_general(left, right, ((dims[0], dims[1]), ((), ())), preferred_el...  103 us
    pallas_call x1, Pallas kernels, hidden_units(): pl.pallas_call(hidden_kernel, grid=(total // rows,), in_specs=[tile(width...  33.3 us
    ppermute x3, waiting for transfers between devices, hop(): lax.ppermute(array, 'h', [(i, (i + shift) % far) for i in range(far)])  14.8 us
  transfers between devices with their start and end apart: 6, of which 2 were waited for; matrix products, arithmetic and copies ran while one was open for 13% of the time, Pallas kernels for 29%

profile of v9, /device:TPU:0, one launch (start us, length us, event | category | flops | bytes accessed | tf_op | source)
XLA Modules:
  0.0 704.9 jit_solution(3574368299176878630)
XLA Ops:
  9.6 75.6 %gather_first.1 = (bf16[2,2,2,2,2,48,2048]{6,5,4,3,2,1,0:T(8,128)(2,1)}, f32[2,2,2,2,2,8,128]{6,5,4,3,2,1,0:T(8,128)}, bf16[8,48,1120]{2,1,0:T(8,128)(2,1)}, bf1...) custom-call(bf16[48,2048]{1,0:T(8,128)(2,1)} %pad_maximum_fusion.2.refs_0_, f32[8,128]{1,0:T(8,128)} %bitcast_convert_fusion.refs_1_, ...), custom_call_target="tpu_custom_call" | custom-call | bytes 1024 | tf_op jit(solution)/shard_map/gather_first/pallas_call | solution.py:630
  91.2 5.9 fusion.45.pre_ref
  102.2 120.4 %gather_second.1 = (bf16[2,2,2,2,128,512]{5,4,3,2,1,0:T(8,128)(2,1)}, bf16[2,2,2,2,128,512]{5,4,3,2,1,0:T(8,128)(2,1)}, bf16[2,2,2,2,2,48,1536]{6,5,4,3,2,1,0:T(...) custom-call(bf16[128,512]{1,0:T(8,128)(2,1)} %get-tuple-element.71.r, ...), custom_call_target="tpu_custom_call" | custom-call | bytes 1024 | tf_op jit(solution)/shard_map/gather_second/pallas_call | solution.py:630
  222.6 4.7 attend_forward.2
  238.9 39.3 %gather_tokens.1 = bf16[2,2,2,256,1536]{4,3,2,1,0:T(8,128)(2,1)} custom-call(bf16[256,1536]{1,0:T(8,128)(2,1)} %multiply_convert_fusion.refs_0_), custom_call_target="tpu_custom_call" | custom-call | bytes 1024 | tf_op jit(solution)/shard_map/gather_tokens/pallas_call | solution.py:630
  278.2 33.3 %hidden_units.1 = (bf16[1536,2048]{1,0:T(8,128)(2,1)}, bf16[2048,1120]{1,0:T(8,128)(2,1)}, bf16[1120,2048]{1,0:T(8,128)(2,1)}, bf16[2048,1120]{1,0:T(8,128)(2,1)}, bf16[2048,1120]{1,0:T(8,128)(2,1)}) custom-call(bf16[2048,1536]{1,0:T(8,128)(2,1)} %bitcast.175, bf16[2048,1536]{1,0:T(8,128)(2,1)} %bitcast.207, bf16[1536,1120]{1,0:T(8,128)(2,1)} %bitcast.213, ...), custom_call_target="tpu_custom_call" | custom-call | flops 21139292160 | bytes 25165824 | tf_op jit(solution)/shard_map/hidden_units/pallas_call | solution.py:263
  311.4 13.0 %fusion.6 = bf16[2,8,2,48,1120]{4,3,1,0,2:T(8,128)(2,1)} fusion(bf16[2048,1120]{1,0:T(8,128)(2,1)} %get-tuple-element.84, bf16[2,8,2,48,2048]{4,3,2,1,0:T(8,128)(2,1)} %bitcast.217), kind=kOutput, calls=%fused_computation.10 | convolution fusion | flops 7048151040 | bytes 14319616 | tf_op jit(solution)/shard_map/dot_general | solution.py:53
  327.4 12.0 %fusion.11 = bf16[2,8,2,48,1120]{4,3,1,0,2:T(8,128)(2,1)S(1)} fusion(bf16[2048,1120]{1,0:T(8,128)(2,1)} %get-tuple-element.88, bf16[2,8,2,48,2048]{4,3,2,1,0:T(8,128)(2,1)} %bitcast.218), kind=kOutput, calls=%fused_computation.11 | convolution fusion | flops 7048151040 | bytes 14319616 | tf_op jit(solution)/shard_map/dot_general | solution.py:53
  344.6 11.0 %fusion.46 = f32[2048,1536]{1,0:T(8,128)} fusion(bf16[2048,1120]{1,0:T(8,128)(2,1)S(1)} %bitcast.223, bf16[1536,1120]{1,0:T(8,128)(2,1)S(1)} %bitcast.214), kind=kOutput, calls=%fused_computation.115 | convolution fusion | flops 7046430720 | bytes 20611072 | tf_op jit(solution)/shard_map/dot_general | solution.py:53
  355.6 13.8 %add_convert_fusion = bf16[2048,1536]{1,0:T(8,128)(2,1)} fusion(f32[2048,1536]{1,0:T(8,128)} %fusion.46, bf16[2048,1120]{1,0:T(8,128)(2,1)} %get-tuple-element.88, bf16[1536,1120]{1,0:T(8,128)(2,1)S(1)} %bitcast.212), kind=kOutput, calls=%fused_computation | convolution fusion | flops 7052722176 | bytes 26902528 | tf_op jit(solution)/shard_map/dot_general | solution.py:53
  369.4 33.4 %reduce_tokens.1 = f32[256,1536]{1,0:T(8,128)} custom-call(bf16[2,2,2,256,1536]{4,3,2,1,0:T(8,128)(2,1)} %bitcast.176), custom_call_target="tpu_custom_call" | custom-call | bytes 1024 | tf_op jit(solution)/shard_map/reduce_tokens/pallas_call | solution.py:831
  409.7 11.7 %collective-permute-done = bf16[2,8,48,1120]{3,2,1,0:T(8,128)(2,1)} collective-permute-done((bf16[2,8,48,1120]{3,2,1,0:T(8,128)(2,1)}, bf16[2,8,48,1120]{3,2,1,0:T(8,128)(2,1)}, u32[]{:S(2)}, u32[]{:S(2)}) %collective-permute-start) | collective-permute-done | bytes 1720352 | tf_op jit(solution)/shard_map/ppermute | solution.py:882
  425.5 7.6 %collective-permute-start.2 = (bf16[8,48,1120]{2,1,0:T(8,128)(2,1)}, bf16[8,48,1120]{2,1,0:T(8,128)(2,1)}, u32[]{:S(2)}, u32[]{:S(2)}) collective-permute-start(bf16[8,48,1120]{2,1,0:T(8,128)(2,1)} %dynamic-slice_bitcast_fusion.4), channel_id=1, source_target_pairs={{0,16},{16,0},{1,17},{17,1},{2,18},{18,2},{3,19},{19,3},{4,20},{20... | collective-permute-start | bytes 2580488 | tf_op jit(solution)/shard_map/ppermute | solution.py:881
  434.3 4.9 convolution_convert_fusion.4.do_ref
  439.2 6.3 attend_backward.3
  445.5 6.2 attend_backward.2
  451.7 5.1 convolution_convert_fusion.2
  456.8 14.8 %collective-permute-done.2 = bf16[8,48,1120]{2,1,0:T(8,128)(2,1)} collective-permute-done((bf16[8,48,1120]{2,1,0:T(8,128)(2,1)}, bf16[8,48,1120]{2,1,0:T(8,128)(2,1)}, u32[]{:S(2)}, u32[]{:S(2)}) %collective-permute-start.2) | collective-permute-done | bytes 860192 | tf_op jit(solution)/shard_map/ppermute | solution.py:881
  473.9 10.9 %convolution_convert_fusion.3 = bf16[2,2,280,1536]{3,2,1,0:T(8,128)(2,1)S(1)} fusion(bf16[2,2,280,2048]{3,2,1,0:T(8,128)(2,1)} %bitcast.219, bf16[2048,1536,1,1]{1,0,3,2:T(8,128)(2,1)} %bitcast.208), kind=kOutput, calls=%fused_computation.12 | convolution fusion | flops 7048151040 | bytes 14319616 | tf_op jit(solution)/shard_map/dot_general | solution.py:53
  488.7 10.3 %convolution_convert_fusion.1 = bf16[2048,1536]{1,0:T(8,128)(2,1)} fusion(bf16[2048,1120]{1,0:T(8,128)(2,1)S(1)} %bitcast.221, bf16[1120,1536]{1,0:T(8,128)(2,1)S(1)} %bitcast.216), kind=kOutput, calls=%fused_computation.2 | convolution fusion | flops 7049576448 | bytes 14319616 | tf_op jit(solution)/shard_map/dot_general | solution.py:53
  499.0 87.9 %reduce_second.1 = (f32[128,512]{1,0:T(8,128)}, f32[128,512]{1,0:T(8,128)}, f32[48,1536]{1,0:T(8,128)}, f32[256,1536]{1,0:T(8,128)}) custom-call(bf16[2,2,2,2,128,512]{5,4,3,2,1,0:T(8,128)(2,1)} %bitcast.180, bf16[2,2,2,2,128,512]{5,4,3,2,1,0:T(8,128)(2,1)} %bitcast.179, bf16[2,2,2,2,2,48,1536]{6,5,4,3,2,1,0:T(8,128)(2,1)} %bitcast.167, ...), custom_call_target="tpu_custom_call" | custom-call | bytes 1024 | tf_op jit(solution)/shard_map/reduce_second/pallas_call | solution.py:831
  604.0 7.0 fusion.31
  615.3 5.6 convolution_convert_fusion
  620.9 67.2 %reduce_last.1 = (f32[48,2048]{1,0:T(8,128)}, f32[8,128]{1,0:T(8,128)}, bf16[8,48,1120]{2,1,0:T(8,128)(2,1)}, bf16[8,48,1120]{2,1,0:T(8,128)(2,1)}) custom-call(bf16[2,2,2,2,2,48,2048]{6,5,4,3,2,1,0:T(8,128)(2,1)} %bitcast.166, f32[2,2,2,2,2,8,128]{6,5,4,3,2,1,0:T(8,128)} %bitcast.184, bf16[8,48,1120]{2,1,0:T(8,128)(2,1)} %fusion.20.refs_2_, ...), custom_call_target="tpu_custom_call" | custom-call | bytes 1024 | tf_op jit(solution)/shard_map/reduce_last/pallas_call | solution.py:831
  (158 shorter events, 95.4 us)
Async XLA Ops:
  7.8 78.5 %copy-start.20 = (s32[1,2,4]{2,1,0:T(2,128)S(1)}, s32[1,2,4]{2,1,0:T(2,128)}, u32[]{:S(2)}) copy-start(s32[1,2,4]{2,1,0:T(2,128)} %param.16) | copy-start | bytes 100
  7.8 79.7 %copy-start.3 = (bf16[1,2,128,1536]{3,2,1,0:T(8,128)(2,1)S(1)}, bf16[1,2,128,1536]{3,2,1,0:T(8,128)(2,1)}, u32[]{:S(2)}) copy-start(bf16[1,2,128,1536]{3,2,1,0:T(8,128)(2,1)} %param.15) | copy-start | bytes 2359300
  87.5 9.5 %copy-start.18 = (f32[1536]{0:T(1024)}, f32[1536]{0:T(1024)S(1)}, u32[]{:S(2)}) copy-start(f32[1536]{0:T(1024)S(1)} %mul.213) | copy-start | bytes 18436
  324.4 20.1 %slice-start.2 = ((s8[4718592]{0:T(1024)(128)(4,1)}), s8[4194304]{0:T(1024)(128)(4,1)S(1)}, s32[]{:S(2)}) async-start(s8[4718592]{0:T(1024)(128)(4,1)} %bitcast.222), calls=%async_computation.2 | async-start | bytes 8388608
  327.4 17.1 %slice-start.3 = ((s8[4718592]{0:T(1024)(128)(4,1)}), s8[524288]{0:T(1024)(128)(4,1)S(1)}, s32[]{:S(2)}) async-start(s8[4718592]{0:T(1024)(128)(4,1)} %bitcast.222), calls=%async_computation.3 | async-start | bytes 1048576
  342.5 13.1 %copy-start.24 = (bf16[2,8,2,48,1120]{4,3,2,1,0:T(8,128)(2,1)S(1)}, bf16[2,8,2,48,1120]{4,3,2,1,0:T(8,128)(2,1)}, u32[]{:S(2)}) copy-start(bf16[2,8,2,48,1120]{4,3,2,1,0:T(8,128)(2,1)} %get-tuple-element.82) | copy-start | bytes 10321924
  342.5 64.3 %collective-permute-start.1 = (bf16[2,8,48,1120]{3,2,1,0:T(8,128)(2,1)}, bf16[2,8,48,1120]{3,2,1,0:T(8,128)(2,1)}, u32[]{:S(2)}, u32[]{:S(2)}) collective-permute-start(bf16[2,8,48,1120]{3,2,1,0:T(8,128)(2,1)} %dynamic-slice_bitcast_fusion), channel_id=1, source_target_pairs={{0,1},{1,0},{2,3},{3,2},{4,5},{5,4},{6,7},{7,6},{8,9},{9,8},{10,11... | collective-permute-start | bytes 5160968 | tf_op jit(solution)/shard_map/ppermute | solution.py:882
  342.5 78.9 %collective-permute-start = (bf16[2,8,48,1120]{3,2,1,0:T(8,128)(2,1)}, bf16[2,8,48,1120]{3,2,1,0:T(8,128)(2,1)}, u32[]{:S(2)}, u32[]{:S(2)}) collective-permute-start(bf16[2,8,48,1120]{3,2,1,0:T(8,128)(2,1)} %dynamic-slice_bitcast_fusion.1), channel_id=1, source_target_pairs={{0,1},{1,0},{2,3},{3,2},{4,5},{5,4},{6,7},{7,6},{8,9},{9,8},{10,11... | collective-permute-start | bytes 5160968 | tf_op jit(solution)/shard_map/ppermute | solution.py:882
  406.8 14.6 %copy-start.5 = (bf16[2,8,2,48,1120]{4,3,1,0,2:T(8,128)(2,1)S(1)}, bf16[2,8,2,48,1120]{4,3,1,0,2:T(8,128)(2,1)}, u32[]{:S(2)}) copy-start(bf16[2,8,2,48,1120]{4,3,1,0,2:T(8,128)(2,1)} %fusion.6) | copy-start | bytes 10321924
  425.5 46.1 %collective-permute-start.2 = (bf16[8,48,1120]{2,1,0:T(8,128)(2,1)}, bf16[8,48,1120]{2,1,0:T(8,128)(2,1)}, u32[]{:S(2)}, u32[]{:S(2)}) collective-permute-start(bf16[8,48,1120]{2,1,0:T(8,128)(2,1)} %dynamic-slice_bitcast_fusion.4), channel_id=1, source_target_pairs={{0,16},{16,0},{1,17},{17,1},{2,18},{18,2},{3,19},{19,3},{4,20},{20... | collective-permute-start | bytes 2580488 | tf_op jit(solution)/shard_map/ppermute | solution.py:881
  451.7 19.9 %copy-start.2 = (bf16[2,8,48,1120]{3,2,1,0:T(8,128)(2,1)S(1)}, bf16[2,8,48,1120]{3,2,1,0:T(8,128)(2,1)}, u32[]{:S(2)}) copy-start(bf16[2,8,48,1120]{3,2,1,0:T(8,128)(2,1)} %copy-done.1) | copy-start | bytes 5160964
  451.7 37.0 %slice-start = ((s8[4718592]{0:T(1024)(128)(4,1)}), s8[4194304]{0:T(1024)(128)(4,1)S(1)}, s32[]{:S(2)}) async-start(s8[4718592]{0:T(1024)(128)(4,1)} %bitcast.220), calls=%async_computation | async-start | bytes 8388608
  473.9 14.8 %slice-start.1 = ((s8[4718592]{0:T(1024)(128)(4,1)}), s8[524288]{0:T(1024)(128)(4,1)S(1)}, s32[]{:S(2)}) async-start(s8[4718592]{0:T(1024)(128)(4,1)} %bitcast.220), calls=%async_computation.1 | async-start | bytes 1048576
  486.1 105.7 %collective-permute-start.3 = (bf16[2,280,1536]{2,1,0:T(8,128)(2,1)}, bf16[2,280,1536]{2,1,0:T(8,128)(2,1)}, u32[]{:S(2)}, u32[]{:S(2)}) collective-permute-start(bf16[2,280,1536]{2,1,0:T(8,128)(2,1)} %dynamic-slice_bitcast_fusion.2), channel_id=1, source_target_pairs={{0,1},{1,0},{2,3},{3,2},{4,5},{5,4},{6,7},{7,6},{8,9},{9,8},{10,11... | collective-permute-start | bytes 5160968 | tf_op jit(solution)/shard_map/ppermute | solution.py:882
  488.7 100.8 %collective-permute-start.4 = (bf16[8,48,1120]{2,1,0:T(8,128)(2,1)}, bf16[8,48,1120]{2,1,0:T(8,128)(2,1)}, u32[]{:S(2)}, u32[]{:S(2)}) collective-permute-start(bf16[8,48,1120]{2,1,0:T(8,128)(2,1)} %dynamic-slice_bitcast_fusion.3), channel_id=1, source_target_pairs={{0,16},{16,0},{1,17},{17,1},{2,18},{18,2},{3,19},{19,3},{4,20},{20... | collective-permute-start | bytes 2580488 | tf_op jit(solution)/shard_map/ppermute | solution.py:881
  593.8 7.0 copy-start.13
  593.8 7.0 copy-start.14
  593.8 10.2 %copy-start.4 = (bf16[1,2,128,1536]{3,2,1,0:T(8,128)(2,1)S(1)}, bf16[1,2,128,1536]{3,2,1,0:T(8,128)(2,1)}, u32[]{:S(2)}) copy-start(bf16[1,2,128,1536]{3,2,1,0:T(8,128)(2,1)} %param.15) | copy-start | bytes 2359300
  594.8 106.3 %collective-permute-start.5 = (bf16[280,1536]{1,0:T(8,128)(2,1)}, bf16[280,1536]{1,0:T(8,128)(2,1)}, u32[]{:S(2)}, u32[]{:S(2)}) collective-permute-start(bf16[280,1536]{1,0:T(8,128)(2,1)} %dynamic-slice_bitcast_fusion.5), channel_id=1, source_target_pairs={{0,16},{16,0},{1,17},{17,1},{2,18},{18,2},{3,19},{19,3},{4,20},{20... | collective-permute-start | bytes 2580488 | tf_op jit(solution)/shard_map/ppermute | solution.py:881
  604.0 11.3 %copy-start.12 = (bf16[256,512]{1,0:T(8,128)(2,1)S(1)}, bf16[256,512]{1,0:T(8,128)(2,1)}, u32[]{:S(2)}) copy-start(bf16[256,512]{1,0:T(8,128)(2,1)} %rotate.3) | copy-start | bytes 786436
  620.8 70.1 %copy-start.23 = (f32[256]{0:T(256)S(1)}, f32[256]{0:T(256)}, u32[]{:S(2)}) copy-start(f32[256]{0:T(256)} %get-tuple-element.121) | copy-start | bytes 3076
  688.1 9.6 %copy-start.19 = (f32[1536]{0:T(1024)S(1)}, f32[1536]{0:T(1024)}, u32[]{:S(2)}) copy-start(f32[1536]{0:T(1024)} %copy-done.18) | copy-start | bytes 18436
  688.1 9.6 %copy-start.21 = (f32[256]{0:T(256)S(1)}, f32[256]{0:T(256)}, u32[]{:S(2)}) copy-start(f32[256]{0:T(256)} %get-tuple-element.143) | copy-start | bytes 3076
  688.1 9.6 %copy-start.22 = (f32[256]{0:T(256)S(1)}, f32[256]{0:T(256)}, u32[]{:S(2)}) copy-start(f32[256]{0:T(256)} %multiply_multiply_fusion) | copy-start | bytes 3076
  (13 other events, 44.0 us)
